TPU v7x, 32 devices: a whole 2x2x4 slice. The times are simulated.
32 devices in a mesh: dp: 8 (over z, y), var: 4 (over x, core).
Axes of the slice: x: 2, y: 2, z: 4, core: 2. Of those that a mesh axis runs over, the one named last changes fastest.
Arguments:
- img_lo: bfloat16 [320, 128, 320], P('dp', None, 'var'), may hold values from -6 to 6
- img_hi: bfloat16 [160, 512, 320], P('dp', None, 'var'), may hold values from -6 to 6
- keep_lo: int32 [320, 32], P('dp'), may hold values from 0 to 127, as said below
- keep_hi: int32 [160, 128], P('dp'), may hold values from 0 to 511, as said below
- mask_lo: int32 [320, 32], P('dp'), may hold values 0 or 1
- mask_hi: int32 [160, 128], P('dp'), may hold values 0 or 1
- w_embed: bfloat16 [320, 768], P('var'), may hold values from -0.3125 to 0.3125
- pos_lo: bfloat16 [128, 768], replicated, may hold values from -3 to 3
- pos_hi: bfloat16 [512, 768], replicated, may hold values from -3 to 3
- ln1_gain: float32 [768], replicated, may hold values from 0.25 to 1.75
- w_qkv: bfloat16 [768, 2304], replicated, may hold values from -0.21875 to 0.21875
- w_out: bfloat16 [768, 768], replicated, may hold values from -0.625 to 0.625
- ln2_gain: float32 [768], replicated, may hold values from 0.25 to 1.75
- w_fc1: bfloat16 [768, 3072], replicated, may hold values from -0.21875 to 0.21875
- b_fc1: float32 [3072], replicated, may hold values from -3 to 3
- w_fc2: bfloat16 [3072, 768], replicated, may hold values from -0.109375 to 0.109375
- b_fc2: float32 [768], replicated, may hold values from -3 to 3
- w_head: bfloat16 [768, 320], P(None, 'var'), may hold values from -0.21875 to 0.21875
- cot_lo: bfloat16 [320, 32, 320], P('dp', None, 'var'), may hold values from -6 to 6
- cot_hi: bfloat16 [160, 128, 320], P('dp', None, 'var'), may hold values from -6 to 6
Outputs:
- pred_lo: bfloat16 [320, 32, 320], P('dp', None, 'var')
- pred_hi: bfloat16 [160, 128, 320], P('dp', None, 'var')
- grad_img_lo: bfloat16 [320, 128, 320], P('dp', None, 'var')
- grad_img_hi: bfloat16 [160, 512, 320], P('dp', None, 'var')
- grad_embed: float32 [320, 768], P('var')
- grad_pos_lo: float32 [128, 768], P(('dp', 'var'))
- grad_pos_hi: float32 [512, 768], P(('dp', 'var'))
- grad_ln1: float32 [768], P(('dp', 'var'))
- grad_qkv: float32 [768, 2304], P(('dp', 'var'))
- grad_out: float32 [768, 768], P(('dp', 'var'))
- grad_ln2: float32 [768], P(('dp', 'var'))
- grad_fc1: float32 [768, 3072], P(('dp', 'var'))
- grad_b1: float32 [3072], P(('dp', 'var'))
- grad_fc2: float32 [3072, 768], P(('dp', 'var'))
- grad_b2: float32 [768], P(('dp', 'var'))
- grad_head: float32 [768, 320], P(None, 'var')
Inputs may be any that keep to these rules, and one draw needn't show every extreme that they name: `keep_lo`: each row names 32 different patches of its sample. `keep_hi`: each row names 128 different patches of its sample. `mask_lo`: slot 0 counts as visible whatever its entry. `mask_hi`: slot 0 counts as visible whatever its entry.
All inputs are finite; a program needn't handle non-finite values. No bound on the sum of `mask_lo` or of `mask_hi` on one device may be relied on, other than what follows from the above.
Results may differ from a plain program's by a relative error of at most 0.02.
Values may be sent and summed in bfloat16 or wider, within the bound.
No kernel may reach another device: no remote copies, remote signals or barrier semaphores. Data moves between devices by JAX's collectives and lax.ppermute only.
A program may use at most 256 MiB of HBM per device.

v0:
```python
import math

import jax
import jax.numpy as jnp
from jax import lax
from jax.sharding import PartitionSpec as P

HEADS = 12


epsilon = 1e-06


def product(left, right):
    return jnp.dot(left, right, preferred_element_type=jnp.float32)


def inner_rows(left, right):
    return lax.dot_general(
        left, right, (((0,), (0,)), ((), ())), preferred_element_type=jnp.float32
    )


def inner_cols(left, right):
    return lax.dot_general(
        left, right, (((1,), (1,)), ((), ())), preferred_element_type=jnp.float32
    )


def normalize(values, gains):
    center = values - jnp.mean(values, axis=-1, keepdims=True)
    inverse = lax.rsqrt(jnp.mean(center * center, axis=-1, keepdims=True) + epsilon)
    normed = center * inverse
    return (normed * gains, normed, inverse)


def normalize_back(upstream, normed, inverse, gains):
    scaled = upstream * gains
    mean_plain = jnp.mean(scaled, axis=-1, keepdims=True)
    mean_mixed = jnp.mean(scaled * normed, axis=-1, keepdims=True)
    return (
        inverse * (scaled - mean_plain - normed * mean_mixed),
        jnp.sum(upstream * normed, axis=0),
    )


def score_table(queries, keys_in, visible, scale):
    scores = (
        jnp.einsum("bqhd,bkhd->bhqk", queries, keys_in, preferred_element_type=jnp.float32) * scale
    )
    return jnp.where(visible[:, None, None, :] > 0, scores, -1000000000.0)


def attention(queries, keys_in, values_in, visible, scale):
    scores = score_table(queries, keys_in, visible, scale)
    topmost = jnp.max(scores, axis=-1, keepdims=True)
    raised = jnp.exp(scores - topmost)
    summed = jnp.sum(raised, axis=-1, keepdims=True)
    chances = (raised / summed).astype(jnp.bfloat16)
    mixed = jnp.einsum("bhqk,bkhd->bqhd", chances, values_in, preferred_element_type=jnp.float32)
    return (mixed, topmost + jnp.log(summed))


def attention_back(queries, keys_in, values_in, visible, scale, logsum, upstream):
    chances = jnp.exp(score_table(queries, keys_in, visible, scale) - logsum)
    grad_values = jnp.einsum(
        "bhqk,bqhd->bkhd",
        chances.astype(jnp.bfloat16),
        upstream,
        preferred_element_type=jnp.float32,
    )
    grad_chances = jnp.einsum(
        "bqhd,bkhd->bhqk", upstream, values_in, preferred_element_type=jnp.float32
    )
    centred = grad_chances - jnp.sum(chances * grad_chances, axis=-1, keepdims=True)
    grad_scores = (chances * centred).astype(jnp.bfloat16)
    grad_queries = (
        jnp.einsum("bhqk,bkhd->bqhd", grad_scores, keys_in, preferred_element_type=jnp.float32)
        * scale
    )
    grad_keys = (
        jnp.einsum("bhqk,bqhd->bkhd", grad_scores, queries, preferred_element_type=jnp.float32)
        * scale
    )
    return jnp.stack([grad_queries, grad_keys, grad_values], axis=2)


def visible_of(mask):
    first = (lax.broadcasted_iota(jnp.int32, mask.shape, 1) == 0).astype(jnp.int32)
    return jnp.maximum(mask, first)


def body(
    img_lo,
    img_hi,
    keep_lo,
    keep_hi,
    mask_lo,
    mask_hi,
    w_embed,
    pos_lo,
    pos_hi,
    ln1_gain,
    w_qkv,
    w_out,
    ln2_gain,
    w_fc1,
    b_fc1,
    w_fc2,
    b_fc2,
    w_head,
    cot_lo,
    cot_hi,
):
    groups = lax.axis_size("var")
    member = lax.axis_index("var")
    lo_group, lo_length = keep_lo.shape
    hi_group, hi_length = keep_hi.shape
    lo_each = lo_group // groups
    hi_each = hi_group // groups
    lo_rows = lo_each * lo_length
    hi_rows = hi_each * hi_length
    own_rows = lo_rows + hi_rows
    model_width = w_qkv.shape[0]
    head_dim = model_width // HEADS
    scale = 1.0 / math.sqrt(head_dim)
    visible_lo = visible_of(mask_lo)
    visible_hi = visible_of(mask_hi)

    def group_order(lower, upper):
        trailing = lower.shape[2:]
        joined = jnp.concatenate(
            [
                lower.reshape((groups, lo_rows) + trailing),
                upper.reshape((groups, hi_rows) + trailing),
            ],
            axis=1,
        )
        return joined.reshape((groups * own_rows,) + trailing)

    def split_order(joined):
        trailing = joined.shape[1:]
        blocks = joined.reshape((groups, own_rows) + trailing)
        lower = blocks[:, :lo_rows].reshape((lo_group, lo_length) + trailing)
        upper = blocks[:, lo_rows:].reshape((hi_group, hi_length) + trailing)
        return (lower, upper)

    patches = group_order(
        jnp.take_along_axis(img_lo, keep_lo[:, :, None], axis=1),
        jnp.take_along_axis(img_hi, keep_hi[:, :, None], axis=1),
    )
    visible_all = group_order(visible_lo[:, :, None], visible_hi[:, :, None]).astype(jnp.bfloat16)
    grad_pred = group_order(cot_lo, cot_hi) * visible_all
    own_keep_lo = lax.dynamic_slice_in_dim(keep_lo, member * lo_each, lo_each, 0).reshape(-1)
    own_keep_hi = lax.dynamic_slice_in_dim(keep_hi, member * hi_each, hi_each, 0).reshape(-1)
    own_visible_lo = lax.dynamic_slice_in_dim(visible_lo, member * lo_each, lo_each, 0)
    own_visible_hi = lax.dynamic_slice_in_dim(visible_hi, member * hi_each, hi_each, 0)
    embedded = lax.psum_scatter(product(patches, w_embed), "var", scatter_dimension=0, tiled=True)
    onehot_lo = (
        own_keep_lo[:, None] == lax.broadcasted_iota(jnp.int32, (1, pos_lo.shape[0]), 1)
    ).astype(jnp.bfloat16)
    onehot_hi = (
        own_keep_hi[:, None] == lax.broadcasted_iota(jnp.int32, (1, pos_hi.shape[0]), 1)
    ).astype(jnp.bfloat16)
    places = jnp.concatenate([product(onehot_lo, pos_lo), product(onehot_hi, pos_hi)], axis=0)
    start_rows = embedded + places
    normed_one, plain_one, inverse_one = normalize(start_rows, ln1_gain)
    normed_one = normed_one.astype(jnp.bfloat16)
    triple = product(normed_one, w_qkv).astype(jnp.bfloat16)
    triple_lo = triple[:lo_rows].reshape(lo_each, lo_length, 3, HEADS, head_dim)
    triple_hi = triple[lo_rows:].reshape(hi_each, hi_length, 3, HEADS, head_dim)
    mixed_lo, logsum_lo = attention(
        triple_lo[:, :, 0], triple_lo[:, :, 1], triple_lo[:, :, 2], own_visible_lo, scale
    )
    mixed_hi, logsum_hi = attention(
        triple_hi[:, :, 0], triple_hi[:, :, 1], triple_hi[:, :, 2], own_visible_hi, scale
    )
    mixed = jnp.concatenate(
        [mixed_lo.reshape(lo_rows, model_width), mixed_hi.reshape(hi_rows, model_width)], axis=0
    ).astype(jnp.bfloat16)
    middle = start_rows + product(mixed, w_out)
    normed_two, plain_two, inverse_two = normalize(middle, ln2_gain)
    normed_two = normed_two.astype(jnp.bfloat16)
    hidden = product(normed_two, w_fc1) + b_fc1
    activated, gelu_pull = jax.vjp(lambda values: jax.nn.gelu(values, approximate=False), hidden)
    activated = activated.astype(jnp.bfloat16)
    final_rows = (middle + (product(activated, w_fc2) + b_fc2)).astype(jnp.bfloat16)
    outputs = product(lax.all_gather(final_rows, "var", axis=0, tiled=True), w_head)
    grad_head = inner_rows(lax.all_gather(final_rows, "var", axis=0, tiled=True), grad_pred)
    pred_lo, pred_hi = split_order((outputs * visible_all.astype(jnp.float32)).astype(jnp.bfloat16))
    grad_final = lax.psum_scatter(
        inner_cols(grad_pred, w_head).astype(jnp.bfloat16), "var", scatter_dimension=0, tiled=True
    ).astype(jnp.float32)
    grad_branch = grad_final.astype(jnp.bfloat16)
    grad_b2 = jnp.sum(grad_branch.astype(jnp.float32), axis=0)
    grad_fc2 = inner_rows(activated, grad_branch)
    grad_hidden = gelu_pull(inner_cols(grad_branch, w_fc2))[0].astype(jnp.bfloat16)
    grad_b1 = jnp.sum(grad_hidden.astype(jnp.float32), axis=0)
    grad_fc1 = inner_rows(normed_two, grad_hidden)
    grad_norm_two, grad_ln2 = normalize_back(
        inner_cols(grad_hidden, w_fc1), plain_two, inverse_two, ln2_gain
    )
    grad_middle = grad_final + grad_norm_two
    grad_attn = grad_middle.astype(jnp.bfloat16)
    grad_out = inner_rows(mixed, grad_attn)
    grad_mixed = inner_cols(grad_attn, w_out).astype(jnp.bfloat16)
    grad_triple_lo = attention_back(
        triple_lo[:, :, 0],
        triple_lo[:, :, 1],
        triple_lo[:, :, 2],
        own_visible_lo,
        scale,
        logsum_lo,
        grad_mixed[:lo_rows].reshape(lo_each, lo_length, HEADS, head_dim),
    )
    grad_triple_hi = attention_back(
        triple_hi[:, :, 0],
        triple_hi[:, :, 1],
        triple_hi[:, :, 2],
        own_visible_hi,
        scale,
        logsum_hi,
        grad_mixed[lo_rows:].reshape(hi_each, hi_length, HEADS, head_dim),
    )
    grad_triple = jnp.concatenate(
        [
            grad_triple_lo.reshape(lo_rows, 3 * model_width),
            grad_triple_hi.reshape(hi_rows, 3 * model_width),
        ],
        axis=0,
    ).astype(jnp.bfloat16)
    grad_qkv = inner_rows(normed_one, grad_triple)
    grad_norm_one, grad_ln1 = normalize_back(
        inner_cols(grad_triple, w_qkv), plain_one, inverse_one, ln1_gain
    )
    grad_start = (grad_middle + grad_norm_one).astype(jnp.bfloat16)
    grad_pos_lo = inner_rows(onehot_lo, grad_start[:lo_rows])
    grad_pos_hi = inner_rows(onehot_hi, grad_start[lo_rows:])
    pieces = lax.all_gather(grad_start, "var", axis=0, tiled=True)
    summed = inner_rows(patches, pieces)
    rows_grad = inner_cols(pieces, w_embed)
    grad_embed = summed
    grad_lo, grad_hi = split_order(rows_grad)
    sample_lo = lax.broadcasted_iota(jnp.int32, keep_lo.shape, 0)
    sample_hi = lax.broadcasted_iota(jnp.int32, keep_hi.shape, 0)
    grad_img_lo = (
        jnp.zeros(img_lo.shape, jnp.float32)
        .at[sample_lo, keep_lo]
        .set(grad_lo)
        .astype(jnp.bfloat16)
    )
    grad_img_hi = (
        jnp.zeros(img_hi.shape, jnp.float32)
        .at[sample_hi, keep_hi]
        .set(grad_hi)
        .astype(jnp.bfloat16)
    )
    grad_embed, grad_head = (
        lax.psum(grad_embed.astype(jnp.bfloat16), "dp").astype(jnp.float32),
        lax.psum(grad_head.astype(jnp.bfloat16), "dp").astype(jnp.float32),
    )
    (
        grad_pos_lo,
        grad_pos_hi,
        grad_ln1,
        grad_qkv,
        grad_out,
        grad_ln2,
        grad_fc1,
        grad_b1,
        grad_fc2,
        grad_b2,
    ) = (
        lax.psum_scatter(grad_pos_lo, ("dp", "var"), scatter_dimension=0, tiled=True),
        lax.psum_scatter(grad_pos_hi, ("dp", "var"), scatter_dimension=0, tiled=True),
        lax.psum_scatter(grad_ln1, ("dp", "var"), scatter_dimension=0, tiled=True),
        lax.psum_scatter(grad_qkv, ("dp", "var"), scatter_dimension=0, tiled=True),
        lax.psum_scatter(grad_out, ("dp", "var"), scatter_dimension=0, tiled=True),
        lax.psum_scatter(grad_ln2, ("dp", "var"), scatter_dimension=0, tiled=True),
        lax.psum_scatter(grad_fc1, ("dp", "var"), scatter_dimension=0, tiled=True),
        lax.psum_scatter(grad_b1, ("dp", "var"), scatter_dimension=0, tiled=True),
        lax.psum_scatter(grad_fc2, ("dp", "var"), scatter_dimension=0, tiled=True),
        lax.psum_scatter(grad_b2, ("dp", "var"), scatter_dimension=0, tiled=True),
    )
    return (
        pred_lo,
        pred_hi,
        grad_img_lo,
        grad_img_hi,
        grad_embed,
        grad_pos_lo,
        grad_pos_hi,
        grad_ln1,
        grad_qkv,
        grad_out,
        grad_ln2,
        grad_fc1,
        grad_b1,
        grad_fc2,
        grad_b2,
        grad_head,
    )


def solution(mesh):
    placed = (
        P("dp", None, "var"),
        P("dp", None, "var"),
        P("dp", None),
        P("dp", None),
        P("dp", None),
        P("dp", None),
        P("var", None),
        P(),
        P(),
        P(),
        P(),
        P(),
        P(),
        P(),
        P(),
        P(),
        P(),
        P(None, "var"),
        P("dp", None, "var"),
        P("dp", None, "var"),
    )
    return jax.shard_map(
        body,
        mesh=mesh,
        in_specs=placed,
        out_specs=(
            P("dp", None, "var"),
            P("dp", None, "var"),
            P("dp", None, "var"),
            P("dp", None, "var"),
            P("var", None),
            P(("dp", "var"), None),
            P(("dp", "var"), None),
            P(("dp", "var")),
            P(("dp", "var"), None),
            P(("dp", "var"), None),
            P(("dp", "var")),
            P(("dp", "var"), None),
            P(("dp", "var")),
            P(("dp", "var"), None),
            P(("dp", "var")),
            P(None, "var"),
        ),
        check_vma=False,
    )
```

profile of v0, /device:TPU:0, one launch (start us, length us, event | category | flops | bytes accessed | tf_op | source)
XLA Modules:
  0.0 1299.1 jit_solution(8479959728861448618)
XLA Ops:
  23.3 15.5 %gather_fusion = bf16[1280,80]{1,0:T(8,128)(2,1)} fusion(bf16[40,128,80]{2,1,0:T(8,128)(2,1)} %copy.182, s32[1280]{0:T(1024)} %reshape.252), kind=kCustom, calls=%fused_computation | custom fusion | bytes 419840 | tf_op jit(solution)/shard_map/jit(take_along_axis)/gather | solution.py:149
  40.7 42.0 %gather_fusion.1 = bf16[2560,80]{1,0:T(8,128)(2,1)} fusion(bf16[20,512,80]{2,1,0:T(8,128)(2,1)} %copy.183, s32[2560]{0:T(1024)S(1)} %or_bitcast_fusion), kind=kCustom, calls=%fused_computation.1 | custom fusion | bytes 839680 | tf_op jit(solution)/shard_map/jit(take_along_axis)/gather | solution.py:150
  125.7 63.5 %reduce-scatter.8.cloned.1.call-done = f32[960,768]{1,0:T(8,128)} async-done(((f32[3840,768]{1,0:T(8,128)}), f32[960,768]{1,0:T(8,128)}) %reduce-scatter.8.cloned.1.call-update) | async-done | bytes 2949136 | tf_op jit(solution)/shard_map/reduce_scatter | solution.py:158
  218.2 9.9 reshape.280
  228.1 6.2 fusion.77
  259.8 7.9 fusion.72
  267.8 37.2 %convert_reduce_fusion = (f32[3072]{0:T(1024)}, bf16[960,3072]{1,0:T(8,128)(2,1)S(1)}, f32[960,3072]{1,0:T(8,128)}) fusion(f32[960,3072]{1,0:T(8,128)} %fusion.72, f32[3072]{0:T(1024)} %param.34, bf16[960,768]{1,0:T(8,128)(2,1)} %reduce-scatter.10.cloned.1.call-done, bf16[3072,768]{1,0:T(8,128)(2,1)} %param.35), kind=kOutput, calls=%fused_computation.6 | convolution fusion | flops 4751029248 | bytes 35708928 | tf_op jit(solution)/shard_map/dot_general | solution.py:25
  378.5 11.1 multiply_convert_fusion
  392.1 8.2 add_convert_fusion.2
  402.6 20.3 %all-gather.5.cloned.1.call-done = bf16[3840,768]{1,0:T(8,128)(2,1)} async-done(((bf16[960,768]{1,0:T(8,128)(2,1)}), bf16[3840,768]{1,0:T(8,128)(2,1)}) %all-gather.5.cloned.1.call-update) | async-done | bytes 5898256 | tf_op jit(solution)/shard_map/all_gather | solution.py:239
  427.5 41.7 %all-gather.3.cloned.1.call-done = bf16[3840,768]{1,0:T(8,128)(2,1)} async-done(((bf16[960,768]{1,0:T(8,128)(2,1)}), bf16[3840,768]{1,0:T(8,128)(2,1)}) %all-gather.3.cloned.1.call-update) | async-done | bytes 5898256 | tf_op jit(solution)/shard_map/all_gather | solution.py:188
  482.8 11.6 fusion.8
  495.0 10.9 fusion.71
  506.0 9.8 fusion.84
  522.9 40.4 %all-reduce.5 = (f32[768]{0:T(1024)}, f32[768]{0:T(1024)}, f32[3072]{0:T(1024)}, f32[768]{0:T(1024)S(1)}) all-reduce(f32[768]{0:T(1024)} %get-tuple-element.82, f32[768]{0:T(1024)} %get-tuple-element.80, f32[3072]{0:T(1024)} %get-tuple-element.92, f32[768]{0:T(1024)} %get-tuple-element.107), channel_id=6, replica_groups=mesh['dp'=8,'var'=4] {'dp','var'}, use_global_device_ids=true, to_apply=%region_22.23.clone | all-reduce | flops 5376 | bytes 43008
  567.8 35.5 %all-reduce.10.cloned.1.call-done = f32[128,768]{1,0:T(8,128)} async-done(((f32[128,768]{1,0:T(8,128)}), f32[128,768]{1,0:T(8,128)}) %all-reduce.10.cloned.1.call-update) | async-done | bytes 393232
  640.8 8.0 scatter_custom_fusion
  651.5 9.8 scatter_custom_fusion.1
  670.0 6.8 all-reduce.12.cloned.1.call-done
  680.0 99.6 %reduce-scatter.12.cloned.1.call-done = f32[16,768]{1,0:T(8,128)} async-done(((f32[512,768]{1,0:T(8,128)}), f32[16,768]{1,0:T(8,128)}) %reduce-scatter.12.cloned.1.call-update) | async-done | bytes 49168 | tf_op jit(solution)/shard_map/reduce_scatter | solution.py:275
  779.6 104.7 %reduce-scatter.16.cloned.1.call-done = f32[24,768]{1,0:T(8,128)} async-done(((f32[768,768]{1,0:T(8,128)}), f32[24,768]{1,0:T(8,128)}) %reduce-scatter.16.cloned.1.call-update) | async-done | bytes 73744 | tf_op jit(solution)/shard_map/reduce_scatter | solution.py:278
  884.3 124.6 %reduce-scatter.14.cloned.1.call-done = f32[24,2304]{1,0:T(8,128)} async-done(((f32[768,2304]{1,0:T(8,128)}), f32[24,2304]{1,0:T(8,128)}) %reduce-scatter.14.cloned.1.call-update) | async-done | bytes 221200 | tf_op jit(solution)/shard_map/reduce_scatter | solution.py:277
  1008.9 142.2 %reduce-scatter.18.cloned.1.call-done = f32[24,3072]{1,0:T(8,128)} async-done(((f32[768,3072]{1,0:T(8,128)}), f32[24,3072]{1,0:T(8,128)}) %reduce-scatter.18.cloned.1.call-update) | async-done | bytes 294928 | tf_op jit(solution)/shard_map/reduce_scatter | solution.py:280
  1151.1 141.1 %reduce-scatter.20.cloned.1.call-done = f32[96,768]{1,0:T(8,128)} async-done(((f32[3072,768]{1,0:T(8,128)}), f32[96,768]{1,0:T(8,128)}) %reduce-scatter.20.cloned.1.call-update) | async-done | bytes 294928 | tf_op jit(solution)/shard_map/reduce_scatter | solution.py:282
  (307 shorter events, 275.5 us)
Async XLA Ops:
  7.2 185.7 %copy-start = (bf16[768,2304]{1,0:T(8,128)(2,1)S(1)}, bf16[768,2304]{1,0:T(8,128)(2,1)}, u32[]{:S(2)}) copy-start(bf16[768,2304]{1,0:T(8,128)(2,1)} %param.30) | copy-start | bytes 10616836
  7.2 182.0 %reduce-scatter.8.cloned.1.call-start = ((), (), s32[]{:S(2)}) async-start(), calls=%async_computation.7 | async-start | bytes 14745600 | tf_op jit(solution)/shard_map/reduce_scatter | solution.py:158
  40.7 42.0 %copy-start.62 = (pred[4,640]{1,0:T(4,128)(4,1)S(1)}, pred[4,640]{1,0:T(4,128)(4,1)}, u32[]{:S(2)}) copy-start(pred[4,640]{1,0:T(4,128)(4,1)} %broadcast_in_dim.91) | copy-start | bytes 7684
  92.6 175.2 %reduce-scatter.10.cloned.1.call-start = ((), (), s32[]{:S(2)}) async-start(), calls=%async_computation.9 | async-start | bytes 7372800 | tf_op jit(solution)/shard_map/reduce_scatter | solution.py:191
  98.8 16.9 %copy-start.49 = (bf16[3840]{0:T(1024)(128)(2,1)}, bf16[3840]{0:T(1024)(128)(2,1)S(1)}, u32[]{:S(2)}) copy-start(bf16[3840]{0:T(1024)(128)(2,1)S(1)} %convert_element_type.118) | copy-start | bytes 23044
  115.7 307.2 %all-gather.5.cloned.1.call-start = ((), (), s32[]{:S(2)}) async-start(), calls=%async_computation.10 | async-start | bytes 7372800 | tf_op jit(solution)/shard_map/all_gather | solution.py:239
  118.0 74.3 %copy-start.57 = (s32[320]{0:T(512)}, s32[320]{0:T(512)S(1)}, u32[]{:S(2)}) copy-start(s32[320]{0:T(512)S(1)} %eq.38) | copy-start | bytes 3844
  120.1 72.2 %copy-start.65 = (s32[640]{0:T(1024)}, s32[640]{0:T(1024)S(1)}, u32[]{:S(2)}) copy-start(s32[640]{0:T(1024)S(1)} %dynamic-slice_bitcast_fusion) | copy-start | bytes 7684
  267.8 37.3 %copy-start.6 = (f32[960,768]{1,0:T(8,128)S(1)}, f32[960,768]{1,0:T(8,128)}, u32[]{:S(2)}) copy-start(f32[960,768]{1,0:T(8,128)} %copy-done.5) | copy-start | bytes 8847364
  267.8 37.3 %copy-start.40 = (f32[960]{0:T(1024)S(1)}, f32[960]{0:T(1024)}, u32[]{:S(2)}) copy-start(f32[960]{0:T(1024)} %copy-done.39) | copy-start | bytes 11524
  267.8 37.3 %copy-start.46 = (f32[960]{0:T(1024)S(1)}, f32[960]{0:T(1024)}, u32[]{:S(2)}) copy-start(f32[960]{0:T(1024)} %copy-done.45) | copy-start | bytes 11524
  267.8 37.3 %copy-start.52 = (f32[768]{0:T(1024)S(1)}, f32[768]{0:T(1024)}, u32[]{:S(2)}) copy-start(f32[768]{0:T(1024)} %param.32) | copy-start | bytes 9220
  267.8 37.3 %copy-start.66 = (bf16[768,3072]{1,0:T(8,128)(2,1)S(1)}, bf16[768,3072]{1,0:T(8,128)(2,1)}, u32[]{:S(2)}) copy-start(bf16[768,3072]{1,0:T(8,128)(2,1)} %param.33) | copy-start | bytes 14155780
  378.4 90.7 %all-gather.3.cloned.1.call-start = ((), (), s32[]{:S(2)}) async-start(), calls=%async_computation.8 | async-start | bytes 7372800 | tf_op jit(solution)/shard_map/all_gather | solution.py:188
  378.5 13.6 %copy-start.7 = (f32[960,768]{1,0:T(8,128)S(1)}, f32[960,768]{1,0:T(8,128)}, u32[]{:S(2)}) copy-start(f32[960,768]{1,0:T(8,128)} %copy-done.5) | copy-start | bytes 8847364
  378.5 13.6 %copy-start.69 = (f32[768]{0:T(1024)S(1)}, f32[768]{0:T(1024)}, u32[]{:S(2)}) copy-start(f32[768]{0:T(1024)} %param.36) | copy-start | bytes 9220
  400.3 203.0 %all-reduce.10.cloned.1.call-start = ((), (), s32[]{:S(2)}) async-start(), calls=%async_computation.16 | async-start | bytes 786432
  402.5 66.6 %copy-start.50 = (bf16[3840]{0:T(1024)(128)(2,1)S(1)}, bf16[3840]{0:T(1024)(128)(2,1)}, u32[]{:S(2)}) copy-start(bf16[3840]{0:T(1024)(128)(2,1)} %copy-done.49) | copy-start | bytes 23044
  402.5 274.3 %all-reduce.12.cloned.1.call-start = ((), (), s32[]{:S(2)}) async-start(), calls=%async_computation.17 | async-start | bytes 491520 | tf_op jit(solution)/shard_map/psum | solution.py:259
  473.8 305.8 %reduce-scatter.12.cloned.1.call-start = ((), (), s32[]{:S(2)}) async-start(), calls=%async_computation.11 | async-start | bytes 1622016 | tf_op jit(solution)/shard_map/reduce_scatter | solution.py:275
  477.3 407.1 %reduce-scatter.16.cloned.1.call-start = ((), (), s32[]{:S(2)}) async-start(), calls=%async_computation.13 | async-start | bytes 2433024 | tf_op jit(solution)/shard_map/reduce_scatter | solution.py:278
  482.5 526.4 %reduce-scatter.14.cloned.1.call-start = ((), (), s32[]{:S(2)}) async-start(), calls=%async_computation.12 | async-start | bytes 7299072 | tf_op jit(solution)/shard_map/reduce_scatter | solution.py:277
  494.4 656.7 %reduce-scatter.18.cloned.1.call-start = ((), (), s32[]{:S(2)}) async-start(), calls=%async_computation.14 | async-start | bytes 9732096 | tf_op jit(solution)/shard_map/reduce_scatter | solution.py:280
  505.9 786.2 %reduce-scatter.20.cloned.1.call-start = ((), (), s32[]{:S(2)}) async-start(), calls=%async_computation.15 | async-start | bytes 9732096 | tf_op jit(solution)/shard_map/reduce_scatter | solution.py:282
  (59 other events, 188.0 us)
Sparse Core Ops, SparseCore 0:
  92.7 96.4 reduce-scatter.7
  191.8 55.7 reduce-scatter.9
  378.5 44.3 all-gather.4
  425.0 44.1 all-gather.2
  475.7 127.4 all-reduce.9
  607.0 69.7 all-reduce.11
  683.5 96.1 reduce-scatter.11
  786.3 97.9 reduce-scatter.15
  890.6 118.2 reduce-scatter.13
  1016.2 134.7 reduce-scatter.17
  1157.6 134.5 reduce-scatter.19
where the time goes:
time: 1310 us; the launch traced here: 1300 us
  waiting for transfers between devices  780 us (60%)
  local copies, waits for them, and re-layouts  235 us (18%)
  matrix products  176 us (13%)
  other arithmetic  51.5 us (4%)
  blocking collectives  40.4 us (3%)
  between operations  15.2 us (1%)
    reduce_scatter x1, waiting for transfers between devices, body(): lax.psum_scatter(grad_fc1, ('dp', 'var'), scatter_dimension=0, tiled=True)  142 us
    reduce_scatter x1, waiting for transfers between devices, body(): lax.psum_scatter(grad_fc2, ('dp', 'var'), scatter_dimension=0, tiled=True)  141 us
    reduce_scatter x1, waiting for transfers between devices, body(): lax.psum_scatter(grad_qkv, ('dp', 'var'), scatter_dimension=0, tiled=True)  125 us
    reduce_scatter x1, waiting for transfers between devices, body(): lax.psum_scatter(grad_out, ('dp', 'var'), scatter_dimension=0, tiled=True)  105 us
    reduce_scatter x1, waiting for transfers between devices, body(): lax.psum_scatter(grad_pos_hi, ('dp', 'var'), scatter_dimension=0, tiled=T...  99.6 us
    unnamed x166, local copies, waits for them, and re-layouts  71.4 us
    reduce_scatter x1, waiting for transfers between devices, body(): lax.psum_scatter(product(patches, w_embed), 'var', scatter_dimension=0, t...  63.5 us
    dot_general x6, matrix products, inner_cols(): lax.dot_general(left, right, (((1,), (1,)), ((), ())), preferred_element_...  61.8 us
  transfers between devices with their start and end apart: 11, of which 10 were waited for; matrix products, arithmetic and copies ran while one was open for 20% of the time, Pallas kernels for 0%

commit v1 on v0

v1 whole, which is shorter than its diff:
```python
import math

import jax
import jax.numpy as jnp
from jax import lax
from jax.sharding import PartitionSpec as P

HEADS = 12
EPSILON = 1e-06
AXES = ("dp", "var")
BF16 = jnp.bfloat16
F32 = jnp.float32


def dot(left, right, dims):
    return lax.dot_general(left, right, (dims, ((), ())), preferred_element_type=F32)


def nn(left, right):
    return dot(left, right, ((1,), (0,)))


def nt(left, right):
    return dot(left, right, ((1,), (1,)))


def tn(left, right):
    return dot(left, right, ((0,), (0,)))


def swap(value, data_bit, var_bit):
    dp, var = lax.axis_size("dp"), lax.axis_size("var")
    pairs = [
        (d * var + v, (d ^ data_bit) * var + (v ^ var_bit)) for d in range(dp) for v in range(var)
    ]
    return lax.ppermute(value, AXES, pairs)


def add_rounded(left, right):
    return (left.astype(F32) + right.astype(F32)).astype(BF16)


def stages(order):
    dp, var = lax.axis_size("dp"), lax.axis_size("var")
    data = [("d", 1 << i) for i in range(dp.bit_length() - 1)]
    core = [("v", 1 << i) for i in range(var.bit_length() - 1)]
    if order == 0:
        return core + data
    return core[:1] + data[:1] + core[1:] + data[1:]


def reduce_scatter(full, order):
    dp, var = lax.axis_size("dp"), lax.axis_size("var")
    places = [("d", 1 << i) for i in reversed(range(dp.bit_length() - 1))]
    places += [("v", 1 << i) for i in reversed(range(var.bit_length() - 1))]
    rows = full.shape[0] // (dp * var)
    value = full.astype(BF16).reshape((2,) * len(places) + (rows,) + full.shape[1:])
    d, v = lax.axis_index("dp"), lax.axis_index("var")
    for stage in stages(order):
        axis = places.index(stage)
        kind, bit = stage
        mine = ((d if kind == "d" else v) // bit) % 2
        keep = lax.dynamic_index_in_dim(value, mine, axis, keepdims=False)
        send = lax.dynamic_index_in_dim(value, 1 - mine, axis, keepdims=False)
        got = swap(send, bit if kind == "d" else 0, bit if kind == "v" else 0)
        value = add_rounded(keep, got)
        places.remove(stage)
    return value.astype(F32)


def reduce_relative(blocks):
    var, dp = lax.axis_size("var"), lax.axis_size("dp")
    value = blocks
    bit = 1
    while bit < var:
        value = value.reshape((value.shape[0] // 2, 2) + value.shape[1:])
        value = add_rounded(value[:, 0], swap(value[:, 1], 0, bit))
        bit *= 2
    value = value[0]
    bit = 1
    while bit < dp:
        value = add_rounded(value, swap(value, bit, 0))
        bit *= 2
    return value.astype(F32)


def gather_relative(value):
    value = value[None]
    bit = 1
    while bit < lax.axis_size("var"):
        value = jnp.concatenate([value, swap(value, 0, bit)], axis=0)
        bit *= 2
    return value


def exchange_relative(blocks):
    return [blocks[0]] + [swap(blocks[k], 0, k) for k in range(1, len(blocks))]


def normalize(values, gains):
    center = values - jnp.mean(values, axis=-1, keepdims=True)
    inverse = lax.rsqrt(jnp.mean(center * center, axis=-1, keepdims=True) + EPSILON)
    normed = center * inverse
    return (normed * gains, normed, inverse)


def normalize_back(upstream, normed, inverse, gains):
    scaled = upstream * gains
    mean_plain = jnp.mean(scaled, axis=-1, keepdims=True)
    mean_mixed = jnp.mean(scaled * normed, axis=-1, keepdims=True)
    return (
        inverse * (scaled - mean_plain - normed * mean_mixed),
        jnp.sum(upstream * normed, axis=0),
    )


def score_table(queries, keys_in, visible, scale):
    scores = (
        jnp.einsum("bqhd,bkhd->bhqk", queries, keys_in, preferred_element_type=F32) * scale
    )
    return jnp.where(visible[:, None, None, :] > 0, scores, -1000000000.0)


def attention(queries, keys_in, values_in, visible, scale):
    scores = score_table(queries, keys_in, visible, scale)
    topmost = jnp.max(scores, axis=-1, keepdims=True)
    raised = jnp.exp(scores - topmost)
    summed = jnp.sum(raised, axis=-1, keepdims=True)
    chances = (raised / summed).astype(BF16)
    mixed = jnp.einsum("bhqk,bkhd->bqhd", chances, values_in, preferred_element_type=F32)
    return (mixed, topmost + jnp.log(summed))


def attention_back(queries, keys_in, values_in, visible, scale, logsum, upstream):
    chances = jnp.exp(score_table(queries, keys_in, visible, scale) - logsum)
    grad_values = jnp.einsum(
        "bhqk,bqhd->bkhd", chances.astype(BF16), upstream, preferred_element_type=F32
    )
    grad_chances = jnp.einsum("bqhd,bkhd->bhqk", upstream, values_in, preferred_element_type=F32)
    centred = grad_chances - jnp.sum(chances * grad_chances, axis=-1, keepdims=True)
    grad_scores = (chances * centred).astype(BF16)
    grad_queries = (
        jnp.einsum("bhqk,bkhd->bqhd", grad_scores, keys_in, preferred_element_type=F32) * scale
    )
    grad_keys = (
        jnp.einsum("bhqk,bqhd->bkhd", grad_scores, queries, preferred_element_type=F32) * scale
    )
    return jnp.stack([grad_queries, grad_keys, grad_values], axis=2)


def visible_of(mask):
    first = (lax.broadcasted_iota(jnp.int32, mask.shape, 1) == 0).astype(jnp.int32)
    return jnp.maximum(mask, first)


def one_hot(indices, size):
    places = lax.broadcasted_iota(jnp.int32, indices.shape + (size,), indices.ndim)
    return (indices[..., None] == places).astype(BF16)


def body(
    img_lo,
    img_hi,
    keep_lo,
    keep_hi,
    mask_lo,
    mask_hi,
    w_embed,
    pos_lo,
    pos_hi,
    ln1_gain,
    w_qkv,
    w_out,
    ln2_gain,
    w_fc1,
    b_fc1,
    w_fc2,
    b_fc2,
    w_head,
    cot_lo,
    cot_hi,
):
    groups = lax.axis_size("var")
    member = lax.axis_index("var")
    lo_group, lo_length = keep_lo.shape
    hi_group, hi_length = keep_hi.shape
    lo_each = lo_group // groups
    hi_each = hi_group // groups
    lo_rows = lo_each * lo_length
    hi_rows = hi_each * hi_length
    features = w_embed.shape[0]
    model_width = w_qkv.shape[0]
    head_dim = model_width // HEADS
    scale = 1.0 / math.sqrt(head_dim)
    visible_lo = visible_of(mask_lo)
    visible_hi = visible_of(mask_hi)
    kept_lo = one_hot(keep_lo, img_lo.shape[1])
    kept_hi = one_hot(keep_hi, img_hi.shape[1])

    def to_rows(lower, upper):
        return jnp.concatenate(
            [
                lower.transpose(1, 0, 2).reshape(features, -1),
                upper.transpose(1, 0, 2).reshape(features, -1),
            ],
            axis=1,
        )

    def for_member(lower, upper, k):
        other = member ^ k
        return to_rows(
            lax.dynamic_slice_in_dim(lower, other * lo_each, lo_each, 0),
            lax.dynamic_slice_in_dim(upper, other * hi_each, hi_each, 0),
        )

    def from_members(pieces):
        stacked = jnp.stack(pieces)
        ordered = jnp.concatenate(
            [lax.dynamic_index_in_dim(stacked, member ^ v, 0) for v in range(groups)], axis=0
        )
        lower = ordered[:, :, :lo_rows].reshape(groups, features, lo_each, lo_length)
        upper = ordered[:, :, lo_rows:].reshape(groups, features, hi_each, hi_length)
        return (
            lower.transpose(0, 2, 1, 3).reshape(lo_group, features, lo_length),
            upper.transpose(0, 2, 1, 3).reshape(hi_group, features, hi_length),
        )

    picked_lo = jnp.einsum(
        "scp,sjp->scj", img_lo.transpose(0, 2, 1), kept_lo, preferred_element_type=F32
    ).astype(BF16)
    picked_hi = jnp.einsum(
        "scp,sjp->scj", img_hi.transpose(0, 2, 1), kept_hi, preferred_element_type=F32
    ).astype(BF16)
    patches = jnp.concatenate(
        exchange_relative([for_member(picked_lo, picked_hi, k) for k in range(groups)]), axis=0
    )
    embed_all = gather_relative(w_embed).reshape(groups * features, model_width)
    head_all = gather_relative(w_head.T).reshape(groups * features, model_width)
    cots = exchange_relative(
        [
            for_member(
                cot_lo.transpose(0, 2, 1) * visible_lo[:, None, :].astype(BF16),
                cot_hi.transpose(0, 2, 1) * visible_hi[:, None, :].astype(BF16),
                k,
            )
            for k in range(groups)
        ]
    )
    grad_pred = jnp.concatenate(cots, axis=0)

    own_keep_lo = lax.dynamic_slice_in_dim(kept_lo, member * lo_each, lo_each, 0)
    own_keep_hi = lax.dynamic_slice_in_dim(kept_hi, member * hi_each, hi_each, 0)
    onehot_lo = own_keep_lo.reshape(lo_rows, -1)
    onehot_hi = own_keep_hi.reshape(hi_rows, -1)
    own_visible_lo = lax.dynamic_slice_in_dim(visible_lo, member * lo_each, lo_each, 0)
    own_visible_hi = lax.dynamic_slice_in_dim(visible_hi, member * hi_each, hi_each, 0)
    own_visible = jnp.concatenate([own_visible_lo.reshape(-1), own_visible_hi.reshape(-1)])

    places = jnp.concatenate([nn(onehot_lo, pos_lo), nn(onehot_hi, pos_hi)], axis=0)
    start_rows = tn(patches, embed_all) + places
    normed_one, plain_one, inverse_one = normalize(start_rows, ln1_gain)
    normed_one = normed_one.astype(BF16)
    triple = nn(normed_one, w_qkv).astype(BF16)
    triple_lo = triple[:lo_rows].reshape(lo_each, lo_length, 3, HEADS, head_dim)
    triple_hi = triple[lo_rows:].reshape(hi_each, hi_length, 3, HEADS, head_dim)
    mixed_lo, logsum_lo = attention(
        triple_lo[:, :, 0], triple_lo[:, :, 1], triple_lo[:, :, 2], own_visible_lo, scale
    )
    mixed_hi, logsum_hi = attention(
        triple_hi[:, :, 0], triple_hi[:, :, 1], triple_hi[:, :, 2], own_visible_hi, scale
    )
    mixed = jnp.concatenate(
        [mixed_lo.reshape(lo_rows, model_width), mixed_hi.reshape(hi_rows, model_width)], axis=0
    ).astype(BF16)
    middle = start_rows + nn(mixed, w_out)
    normed_two, plain_two, inverse_two = normalize(middle, ln2_gain)
    normed_two = normed_two.astype(BF16)
    hidden = nn(normed_two, w_fc1) + b_fc1
    activated, gelu_pull = jax.vjp(lambda values: jax.nn.gelu(values, approximate=False), hidden)
    activated = activated.astype(BF16)

    grad_final = tn(grad_pred, head_all)
    grad_branch = grad_final.astype(BF16)
    grad_b2 = jnp.sum(grad_branch.astype(F32), axis=0)
    grad_fc2 = reduce_scatter(tn(activated, grad_branch), 0)
    grad_hidden = gelu_pull(nt(grad_branch, w_fc2))[0].astype(BF16)
    grad_b1 = jnp.sum(grad_hidden.astype(F32), axis=0)
    grad_fc1 = reduce_scatter(tn(normed_two, grad_hidden), 1)

    final_rows = (middle + (nn(activated, w_fc2) + b_fc2)).astype(BF16)
    outputs = (nt(head_all, final_rows) * own_visible.astype(F32)).astype(BF16)
    pred_lo, pred_hi = from_members(
        exchange_relative([outputs[k * features : (k + 1) * features] for k in range(groups)])
    )
    grad_head = nn(grad_pred, final_rows)

    grad_norm_two, grad_ln2 = normalize_back(
        nt(grad_hidden, w_fc1), plain_two, inverse_two, ln2_gain
    )
    grad_middle = grad_final + grad_norm_two
    grad_attn = grad_middle.astype(BF16)
    grad_out = tn(mixed, grad_attn)
    grad_mixed = nt(grad_attn, w_out).astype(BF16)
    grad_triple_lo = attention_back(
        triple_lo[:, :, 0],
        triple_lo[:, :, 1],
        triple_lo[:, :, 2],
        own_visible_lo,
        scale,
        logsum_lo,
        grad_mixed[:lo_rows].reshape(lo_each, lo_length, HEADS, head_dim),
    )
    grad_triple_hi = attention_back(
        triple_hi[:, :, 0],
        triple_hi[:, :, 1],
        triple_hi[:, :, 2],
        own_visible_hi,
        scale,
        logsum_hi,
        grad_mixed[lo_rows:].reshape(hi_each, hi_length, HEADS, head_dim),
    )
    grad_triple = jnp.concatenate(
        [
            grad_triple_lo.reshape(lo_rows, 3 * model_width),
            grad_triple_hi.reshape(hi_rows, 3 * model_width),
        ],
        axis=0,
    ).astype(BF16)
    grad_qkv = reduce_scatter(tn(normed_one, grad_triple), 0)
    grad_norm_one, grad_ln1 = normalize_back(
        nt(grad_triple, w_qkv), plain_one, inverse_one, ln1_gain
    )
    grad_start = (grad_middle + grad_norm_one).astype(BF16)
    grad_pos_lo = tn(onehot_lo, grad_start[:lo_rows])
    grad_pos_hi = tn(onehot_hi, grad_start[lo_rows:])

    devices = lax.axis_size("dp") * groups
    pieces = [
        value.reshape((devices, -1, model_width)) for value in (grad_out, grad_pos_lo, grad_pos_hi)
    ]
    sides = [value.reshape(devices, -1) for value in (grad_ln1, grad_ln2, grad_b1, grad_b2)]
    width = sum(side.shape[1] for side in sides)
    side_rows = -(-width // model_width)
    sides = jnp.pad(jnp.concatenate(sides, axis=1), ((0, 0), (0, side_rows * model_width - width)))
    pieces.append(sides.reshape(devices, side_rows, model_width))
    counts = [piece.shape[1] for piece in pieces]
    total = sum(counts)
    rest = reduce_scatter(
        jnp.concatenate([p.astype(BF16) for p in pieces], axis=1).reshape(-1, model_width), 1
    )
    grad_out = rest[: counts[0]]
    grad_pos_lo = rest[counts[0] : counts[0] + counts[1]]
    grad_pos_hi = rest[counts[0] + counts[1] : counts[0] + counts[1] + counts[2]]
    sides = rest[total - side_rows :].reshape(-1)
    n1 = model_width // devices
    nf = w_fc1.shape[1] // devices
    grad_ln1 = sides[:n1]
    grad_ln2 = sides[n1 : 2 * n1]
    grad_b1 = sides[2 * n1 : 2 * n1 + nf]
    grad_b2 = sides[2 * n1 + nf : 3 * n1 + nf]

    grad_embed = nn(patches, grad_start)
    both = reduce_relative(
        jnp.concatenate(
            [
                grad_embed.astype(BF16).reshape(groups, features, model_width),
                grad_head.astype(BF16).reshape(groups, features, model_width),
            ],
            axis=1,
        )
    )
    grad_embed = both[:features]
    grad_head = both[features:].T

    rows_grad = nt(embed_all, grad_start).astype(BF16)
    back_lo, back_hi = from_members(
        exchange_relative([rows_grad[k * features : (k + 1) * features] for k in range(groups)])
    )
    grad_img_lo = jnp.einsum("scj,sjp->scp", back_lo, kept_lo, preferred_element_type=F32)
    grad_img_hi = jnp.einsum("scj,sjp->scp", back_hi, kept_hi, preferred_element_type=F32)
    return (
        pred_lo.transpose(0, 2, 1),
        pred_hi.transpose(0, 2, 1),
        grad_img_lo.astype(BF16).transpose(0, 2, 1),
        grad_img_hi.astype(BF16).transpose(0, 2, 1),
        grad_embed,
        grad_pos_lo,
        grad_pos_hi,
        grad_ln1,
        grad_qkv,
        grad_out,
        grad_ln2,
        grad_fc1,
        grad_b1,
        grad_fc2,
        grad_b2,
        grad_head,
    )


def solution(mesh):
    placed = (
        P("dp", None, "var"),
        P("dp", None, "var"),
        P("dp", None),
        P("dp", None),
        P("dp", None),
        P("dp", None),
        P("var", None),
        P(),
        P(),
        P(),
        P(),
        P(),
        P(),
        P(),
        P(),
        P(),
        P(),
        P(None, "var"),
        P("dp", None, "var"),
        P("dp", None, "var"),
    )
    return jax.shard_map(
        body,
        mesh=mesh,
        in_specs=placed,
        out_specs=(
            P("dp", None, "var"),
            P("dp", None, "var"),
            P("dp", None, "var"),
            P("dp", None, "var"),
            P("var", None),
            P(("dp", "var"), None),
            P(("dp", "var"), None),
            P(("dp", "var")),
            P(("dp", "var"), None),
            P(("dp", "var"), None),
            P(("dp", "var")),
            P(("dp", "var"), None),
            P(("dp", "var")),
            P(("dp", "var"), None),
            P(("dp", "var")),
            P(None, "var"),
        ),
        check_vma=False,
    )
```

time: 1310 us -> 531 us (0.41)
  waiting for transfers between devices: 780 us -> 85.2 us
  local copies, waits for them, and re-layouts: 235 us -> 163 us
  blocking collectives: 40.4 us -> 0 us
  starting transfers between devices: 0.88 us -> 40.3 us
  other arithmetic: 51.5 us -> 68.9 us
    reduce_scatter x7 -> x0, waiting for transfers between devices: 676 us -> none  [the longest x1 142 us: body(): lax.psum_scatter(grad_fc1, ('dp', 'var'), scatter_dimension=0, tiled=True)]
    ppermute x0 -> x41, waiting for transfers between devices: none -> 85.2 us  [swap(): return lax.ppermute(value, AXES, pairs)]
    all_gather x2 -> x0, waiting for transfers between devices: 62 us -> none  [the longest x1 41.7 us: body(): lax.all_gather(final_rows, 'var', axis=0, tiled=True)]
    gather x6 -> x0, local copies, waits for them, and re-layouts: 60.2 us -> none  [the longest x2 42 us: body(): jnp.take_along_axis(img_hi, keep_hi[:, :, None], axis=1)]
    unnamed x1 -> x0, blocking collectives: 40.4 us -> none
    ppermute x0 -> x41, starting transfers between devices: none -> 40.3 us  [swap(): return lax.ppermute(value, AXES, pairs)]
    unnamed x166 -> x204, local copies, waits for them, and re-layouts: 71.4 us -> 32.9 us
    unnamed x12 -> x0, waiting for transfers between devices: 35.7 us -> none
  transfers between devices with their start and end apart: 11 -> 41, of which waited for: 10 -> 21; matrix products, arithmetic and copies ran while one was open for 20% -> 48% of each run, Pallas kernels for 0% -> 0%
where the time goes in v1:
time: 531 us; the launch traced here: 525 us
  matrix products  165 us (31%)
  local copies, waits for them, and re-layouts  163 us (31%)
  waiting for transfers between devices  85.2 us (16%)
  other arithmetic  68.9 us (13%)
  starting transfers between devices  40.3 us (8%)
    dot_general x22, matrix products, dot(): lax.dot_general(left, right, (dims, ((), ())), preferred_element_type=F32)  133 us
    ppermute x41, waiting for transfers between devices, swap(): return lax.ppermute(value, AXES, pairs)  85.2 us
    ppermute x41, starting transfers between devices, swap(): return lax.ppermute(value, AXES, pairs)  40.3 us
    unnamed x204, local copies, waits for them, and re-layouts  32.9 us
    reshape x8, local copies, waits for them, and re-layouts, to_rows(): lower.transpose(1, 0, 2).reshape(features, -1)  12.8 us
    convert_element_type x19, other arithmetic, add_rounded(): return (left.astype(F32) + right.astype(F32)).astype(BF16)  12.2 us
  transfers between devices with their start and end apart: 41, of which 21 were waited for; matrix products, arithmetic and copies ran while one was open for 48% of the time, Pallas kernels for 0%

profile of v1, /device:TPU:0, one launch (start us, length us, event | category | flops | bytes accessed | tf_op | source)
XLA Modules:
  0.0 524.8 jit_solution(8409418013768259197)
XLA Ops:
  81.1 4.1 convolution_convert_fusion
  88.3 5.6 %reshape.357 = bf16[10,32,3,12,64]{4,3,2,1,0:T(8,128)(2,1)} reshape(bf16[320,2304]{1,0:T(8,128)(2,1)} %slice.219) | data formatting | bytes 2949120 | tf_op jit(solution)/shard_map/reshape | solution.py:264
  106.1 10.1 %reshape.411 = bf16[5,128,3,12,64]{4,3,2,1,0:T(8,128)(2,1)} reshape(bf16[640,2304]{1,0:T(8,128)(2,1)} %slice.223) | data formatting | bytes 5898240 | tf_op jit(solution)/shard_map/reshape | solution.py:265
  116.2 6.3 %fusion.109 = (bf16[5,128,1,12,64]{4,3,2,1,0:T(8,128)(2,1)}, bf16[5,128,1,12,64]{4,3,2,1,0:T(8,128)(2,1)}, bf16[5,128,1,12,64]{4,3,2,1,0:T(8,128)(2,1)}) fusion(bf16[5,128,3,12,64]{4,3,2,1,0:T(8,128)(2,1)} %reshape.411), kind=kLoop, calls=%fused_computation.330 | loop fusion | bytes 5898240 | tf_op jit(solution)/shard_map/slice | solution.py:270
  122.4 4.3 copy.594
  126.7 4.3 copy.595
  131.0 4.3 copy.596
  146.1 33.7 %multiply_convert_fusion = (bf16[960,3072]{1,0:T(8,128)(2,1)}, f32[960,3072]{1,0:T(8,128)}, f32[960,3072]{1,0:T(8,128)}) fusion(f32[3072]{0:T(1024)S(1)} %copy-done.87, bf16[768,3072]{1,0:T(8,128)(2,1)S(1)} %bitcast.451, f32[960,768]{1,0:T(8,128)S(1)} %get-tuple-element.90, f32[768]{0:T(1024)S(1)} %copy-done.78, f32[960]{0:T(1024)S(1)} %add_rsqrt_fusion, ...), kind=kOutput, calls=%fused_computation.3 | convolution fusion | flops 4727439360 | bytes 37181952 | tf_op jit(solution)/shard_map/dot_general | solution.py:16
  182.3 4.5 convert_reduce_fusion
  186.9 18.4 %fusion.115 = (bf16[3072]{0:T(1024)(128)(2,1)}, bf16[960,3072]{1,0:T(8,128)(2,1)}) fusion(f32[960,3072]{1,0:T(8,128)} %get-tuple-element.27, bf16[3072,768]{1,0:T(8,128)(2,1)} %param.35, f32[960,768]{1,0:T(8,128)} %get-tuple-element.99, f32[960,3072]{1,0:T(8,128)} %get-tuple-element.91, f32[3072]{0:T(1024)S(1)} %copy-done.87), kind=kOutput, calls=%fused_computation.336 | convolution fusion | flops 4577768448 | bytes 37177344 | tf_op jit(solution)/shard_map/dot_general | solution.py:16
  205.3 10.1 %multiply_reduce_fusion.1 = (bf16[768]{0:T(1024)(128)(2,1)}, f32[960]{0:T(1024)S(1)}, f32[960]{0:T(1024)S(1)}, f32[960,768]{1,0:T(8,128)S(1)}) fusion(f32[960,768]{1,0:T(8,128)S(1)} %get-tuple-element.90, f32[960]{0:T(1024)S(1)} %add_rsqrt_fusion, f32[960]{0:T(1024)S(1)} %broadcast_multiply_fusion.6, f32[768]{0:T(1024)S(1)} %copy-done.78, ...), kind=kOutput, calls=%fused_computation.42 | convolution fusion | flops 4535743488 | bytes 16535040 | tf_op jit(solution)/shard_map/dot_general | solution.py:16
  215.4 7.5 %convolution_convert_fusion.2 = bf16[768,3072]{1,0:T(8,128)(2,1)} fusion(bf16[960,3072]{1,0:T(8,128)(2,1)S(1)} %copy-done.91, f32[960,768]{1,0:T(8,128)S(1)} %get-tuple-element.90, f32[768]{0:T(1024)S(1)} %copy-done.78, f32[960]{0:T(1024)S(1)} %add_rsqrt_fusion, f32[960]{0:T(1024)S(1)} %broadcast_multiply_fusion.6), kind=kOutput, calls=%fused_computation.20 | convolution fusion | flops 4535156736 | bytes 13576704 | tf_op jit(solution)/shard_map/dot_general | solution.py:16
  241.9 4.1 reshape.412
  246.0 4.3 copy.548
  250.3 5.0 fusion.34
  266.1 5.9 %reshape.373 = bf16[320,2304]{1,0:T(8,128)(2,1)} reshape(bf16[10,32,3,12,64]{4,3,2,1,0:T(8,128)(2,1)} %copy.546) | data formatting | bytes 2949120 | tf_op jit(solution)/shard_map/reshape | solution.py:324
  283.4 7.9 %multiply_reduce_fusion.2 = (bf16[768]{0:T(1024)(128)(2,1)}, f32[960]{0:T(1024)}, f32[960]{0:T(1024)}, f32[960,768]{1,0:T(8,128)}) fusion(f32[960,768]{1,0:T(8,128)S(1)} %copy-done.7, f32[960]{0:T(1024)S(1)} %copy-done.74, f32[960]{0:T(1024)S(1)} %copy-done.72, f32[768]{0:T(1024)S(1)} %copy-done.80, bf16[768,2304]{1,0:T(8,128)(2,1)S(1)} %copy-done, ...), kind=kOutput, calls=%fused_computation.43 | convolution fusion | flops 3412129024 | bytes 13880832 | tf_op jit(solution)/shard_map/dot_general | solution.py:16
  291.3 8.6 %convolution_convert_fusion.3 = bf16[768,2304]{1,0:T(8,128)(2,1)} fusion(bf16[640,2304]{0,1:T(8,128)(2,1)S(1)} %bitcast.400, bf16[320,2304]{0,1:T(8,128)(2,1)S(1)} %copy-done.42, f32[960,768]{1,0:T(8,128)S(1)} %copy-done.7, f32[768]{0:T(1024)S(1)} %copy-done.80, f32[960]{0:T(1024)S(1)} %copy-done.74, f32[960]{0:T(1024)S(1)} %copy-done.72), kind=kOutput, calls=%fused_computation.21 | convolution fusion | flops 3410952192 | bytes 10922496 | tf_op jit(solution)/shard_map/dot_general | solution.py:16
  302.1 8.5 %convolution_convert_fusion.1 = bf16[3072,768]{1,0:T(8,128)(2,1)S(1)} fusion(bf16[960,3072]{1,0:T(8,128)(2,1)} %get-tuple-element.26, f32[960,768]{1,0:T(8,128)} %get-tuple-element.99), kind=kOutput, calls=%fused_computation.19 | convolution fusion | flops 4532944896 | bytes 13565952 | tf_op jit(solution)/shard_map/dot_general | solution.py:16
  310.6 8.9 %add_convert_fusion.2 = bf16[960,768]{1,0:T(8,128)(2,1)S(1)} fusion(f32[960,768]{1,0:T(8,128)S(1)} %copy-done.10, bf16[960,3072]{1,0:T(8,128)(2,1)} %get-tuple-element.26, bf16[3072,768]{1,0:T(8,128)(2,1)} %param.35, f32[768]{0:T(1024)S(1)} %copy-done.88), kind=kOutput, calls=%fused_computation.48 | convolution fusion | flops 4532060160 | bytes 15043584 | tf_op jit(solution)/shard_map/dot_general | solution.py:16
  344.9 4.5 add_convert_fusion.1
  446.6 13.3 %collective-permute-done.27 = bf16[2,2,2,24,2304]{4,3,0,1,2:T(8,128)(2,1)S(1)} collective-permute-done((bf16[2,2,2,24,2304]{4,3,0,1,2:T(8,128)(2,1)S(1)}, bf16[2,2,2,24,2304]{4,3,0,1,2:T(8,128)(2,1)S(1)}, u32[]{:S(2)}, u32[]{:S(2)}) %collective-permute-start.27) | collective-permute-done | bytes 884768 | tf_op jit(solution)/shard_map/ppermute | solution.py:36
  464.4 9.0 %collective-permute-done.28 = bf16[2,2,24,2304]{3,2,0,1:T(8,128)(2,1)S(1)} collective-permute-done((bf16[2,2,24,2304]{3,2,0,1:T(8,128)(2,1)S(1)}, bf16[2,2,24,2304]{3,2,0,1:T(8,128)(2,1)S(1)}, u32[]{:S(2)}, u32[]{:S(2)}) %collective-permute-start.28) | collective-permute-done | bytes 442400 | tf_op jit(solution)/shard_map/ppermute | solution.py:36
  481.6 17.0 %collective-permute-done.32 = bf16[2,2,2,24,3072]{4,3,0,1,2:T(8,128)(2,1)S(1)} collective-permute-done((bf16[2,2,2,24,3072]{4,3,0,1,2:T(8,128)(2,1)S(1)}, bf16[2,2,2,24,3072]{4,3,0,1,2:T(8,128)(2,1)S(1)}, u32[]{:S(2)}, u32[]{:S(2)}) %collective-permute-start.32) | collective-permute-done | bytes 1179680 | tf_op jit(solution)/shard_map/ppermute | solution.py:36
  (475 shorter events, 311.9 us)
Async XLA Ops:
  0.7 51.5 %collective-permute-start.5 = (bf16[1,80,768]{2,1,0:T(8,128)(2,1)}, bf16[1,80,768]{2,1,0:T(8,128)(2,1)}, u32[]{:S(2)}, u32[]{:S(2)}) collective-permute-start(bf16[1,80,768]{2,1,0:T(8,128)(2,1)} %bitcast.416), channel_id=1, source_target_pairs={{0,1},{1,0},{2,3},{3,2},{4,5},{5,4},{6,7},{7,6},{8,9},{9,8},{10,11... | collective-permute-start | bytes 368648 | tf_op jit(solution)/shard_map/ppermute | solution.py:36
  1.2 70.7 %collective-permute-start = (bf16[1,80,768]{2,1,0:T(8,128)(2,1)}, bf16[1,80,768]{2,1,0:T(8,128)(2,1)}, u32[]{:S(2)}, u32[]{:S(2)}) collective-permute-start(bf16[1,80,768]{2,1,0:T(8,128)(2,1)} %bitcast.419), channel_id=1, source_target_pairs={{0,1},{1,0},{2,3},{3,2},{4,5},{5,4},{6,7},{7,6},{8,9},{9,8},{10,11... | collective-permute-start | bytes 368648 | tf_op jit(solution)/shard_map/ppermute | solution.py:36
  17.3 57.9 %collective-permute-start.4 = (bf16[80,960]{1,0:T(8,128)(2,1)}, bf16[80,960]{1,0:T(8,128)(2,1)}, u32[]{:S(2)}, u32[]{:S(2)}) collective-permute-start(bf16[80,960]{1,0:T(8,128)(2,1)} %pad_maximum_fusion.21), channel_id=1, source_target_pairs={{0,3},{1,2},{2,1},{3,0},{4,7},{5,6},{6,5},{7,4},{8,11},{9,10},{10,... | collective-permute-start | bytes 460808 | tf_op jit(solution)/shard_map/ppermute | solution.py:36
  23.9 52.7 %collective-permute-start.3 = (bf16[80,960]{1,0:T(8,128)(2,1)}, bf16[80,960]{1,0:T(8,128)(2,1)}, u32[]{:S(2)}, u32[]{:S(2)}) collective-permute-start(bf16[80,960]{1,0:T(8,128)(2,1)} %pad_maximum_fusion.20), channel_id=1, source_target_pairs={{0,2},{1,3},{2,0},{3,1},{4,6},{5,7},{6,4},{7,5},{8,10},{9,11},{10,... | collective-permute-start | bytes 460808 | tf_op jit(solution)/shard_map/ppermute | solution.py:36
  28.5 48.5 %collective-permute-start.2 = (bf16[80,960]{1,0:T(8,128)(2,1)}, bf16[80,960]{1,0:T(8,128)(2,1)}, u32[]{:S(2)}, u32[]{:S(2)}) collective-permute-start(bf16[80,960]{1,0:T(8,128)(2,1)} %pad_maximum_fusion.19), channel_id=1, source_target_pairs={{0,1},{1,0},{2,3},{3,2},{4,5},{5,4},{6,7},{7,6},{8,9},{9,8},{10,11... | collective-permute-start | bytes 460808 | tf_op jit(solution)/shard_map/ppermute | solution.py:36
  53.9 19.7 %collective-permute-start.6 = (bf16[2,80,768]{2,1,0:T(8,128)(2,1)}, bf16[2,80,768]{2,1,0:T(8,128)(2,1)}, u32[]{:S(2)}, u32[]{:S(2)}) collective-permute-start(bf16[2,80,768]{2,1,0:T(8,128)(2,1)} %pad_maximum_fusion.18), channel_id=1, source_target_pairs={{0,2},{1,3},{2,0},{3,1},{4,6},{5,7},{6,4},{7,5},{8,10},{9,11},{10,... | collective-permute-start | bytes 737288 | tf_op jit(solution)/shard_map/ppermute | solution.py:36
  71.8 110.4 %collective-permute-start.10 = (bf16[80,960]{1,0:T(8,128)(2,1)}, bf16[80,960]{1,0:T(8,128)(2,1)}, u32[]{:S(2)}, u32[]{:S(2)}) collective-permute-start(bf16[80,960]{1,0:T(8,128)(2,1)} %pad_maximum_fusion.22), channel_id=1, source_target_pairs={{0,1},{1,0},{2,3},{3,2},{4,5},{5,4},{6,7},{7,6},{8,9},{9,8},{10,11... | collective-permute-start | bytes 460808 | tf_op jit(solution)/shard_map/ppermute | solution.py:36
  73.5 108.8 %collective-permute-start.11 = (bf16[80,960]{1,0:T(8,128)(2,1)}, bf16[80,960]{1,0:T(8,128)(2,1)}, u32[]{:S(2)}, u32[]{:S(2)}) collective-permute-start(bf16[80,960]{1,0:T(8,128)(2,1)} %pad_maximum_fusion.23), channel_id=1, source_target_pairs={{0,2},{1,3},{2,0},{3,1},{4,6},{5,7},{6,4},{7,5},{8,10},{9,11},{10,... | collective-permute-start | bytes 460808 | tf_op jit(solution)/shard_map/ppermute | solution.py:36
  75.2 107.1 %collective-permute-start.12 = (bf16[80,960]{1,0:T(8,128)(2,1)}, bf16[80,960]{1,0:T(8,128)(2,1)}, u32[]{:S(2)}, u32[]{:S(2)}) collective-permute-start(bf16[80,960]{1,0:T(8,128)(2,1)} %pad_maximum_fusion.24), channel_id=1, source_target_pairs={{0,3},{1,2},{2,1},{3,0},{4,7},{5,6},{6,5},{7,4},{8,11},{9,10},{10,... | collective-permute-start | bytes 460808 | tf_op jit(solution)/shard_map/ppermute | solution.py:36
  76.6 104.6 %collective-permute-start.1 = (bf16[2,80,768]{2,1,0:T(8,128)(2,1)}, bf16[2,80,768]{2,1,0:T(8,128)(2,1)}, u32[]{:S(2)}, u32[]{:S(2)}) collective-permute-start(bf16[2,80,768]{2,1,0:T(8,128)(2,1)} %pad_maximum_fusion.17), channel_id=1, source_target_pairs={{0,2},{1,3},{2,0},{3,1},{4,6},{5,7},{6,4},{7,5},{8,10},{9,11},{10,... | collective-permute-start | bytes 737288 | tf_op jit(solution)/shard_map/ppermute | solution.py:36
  321.1 43.9 %collective-permute-start.9 = (bf16[80,960]{1,0:T(8,128)(2,1)}, bf16[80,960]{1,0:T(8,128)(2,1)}, u32[]{:S(2)}, u32[]{:S(2)}) collective-permute-start(bf16[80,960]{1,0:T(8,128)(2,1)} %get-tuple-element.55), channel_id=1, source_target_pairs={{0,3},{1,2},{2,1},{3,0},{4,7},{5,6},{6,5},{7,4},{8,11},{9,10},{10,... | collective-permute-start | bytes 460808 | tf_op jit(solution)/shard_map/ppermute | solution.py:36
  322.4 44.1 %collective-permute-start.8 = (bf16[80,960]{1,0:T(8,128)(2,1)}, bf16[80,960]{1,0:T(8,128)(2,1)}, u32[]{:S(2)}, u32[]{:S(2)}) collective-permute-start(bf16[80,960]{1,0:T(8,128)(2,1)} %get-tuple-element.56), channel_id=1, source_target_pairs={{0,2},{1,3},{2,0},{3,1},{4,6},{5,7},{6,4},{7,5},{8,10},{9,11},{10,... | collective-permute-start | bytes 460808 | tf_op jit(solution)/shard_map/ppermute | solution.py:36
  322.9 44.1 %collective-permute-start.7 = (bf16[80,960]{1,0:T(8,128)(2,1)}, bf16[80,960]{1,0:T(8,128)(2,1)}, u32[]{:S(2)}, u32[]{:S(2)}) collective-permute-start(bf16[80,960]{1,0:T(8,128)(2,1)} %get-tuple-element.57), channel_id=1, source_target_pairs={{0,1},{1,0},{2,3},{3,2},{4,5},{5,4},{6,7},{7,6},{8,9},{9,8},{10,11... | collective-permute-start | bytes 460808 | tf_op jit(solution)/shard_map/ppermute | solution.py:36
  326.2 116.4 %collective-permute-start.36 = (bf16[2,2,2,2,96,768]{5,4,0,1,2,3:T(8,128)(2,1)}, bf16[2,2,2,2,96,768]{5,4,0,1,2,3:T(8,128)(2,1)}, u32[]{:S(2)}, u32[]{:S(2)}) collective-permute-start(bf16[2,2,2,2,96,768]{5,4,0,1,2,3:T(8,128)(2,1)} %bitcast.375), channel_id=1, source_target_pairs={{0,1},{1,0},{2,3},{3,2},{4,5},{5,4},{6,7},{7,6},{8,9},{9,8},{10,11... | collective-permute-start | bytes 7077896 | tf_op jit(solution)/shard_map/ppermute | solution.py:36
  336.2 125.6 %collective-permute-start.31 = (bf16[2,2,2,2,24,3072]{5,4,0,1,3,2:T(8,128)(2,1)}, bf16[2,2,2,2,24,3072]{5,4,0,1,3,2:T(8,128)(2,1)}, u32[]{:S(2)}, u32[]{:S(2)}) collective-permute-start(bf16[2,2,2,2,24,3072]{5,4,0,1,3,2:T(8,128)(2,1)} %bitcast.376), channel_id=1, source_target_pairs={{0,1},{1,0},{2,3},{3,2},{4,5},{5,4},{6,7},{7,6},{8,9},{9,8},{10,11... | collective-permute-start | bytes 7077896 | tf_op jit(solution)/shard_map/ppermute | solution.py:36
  371.0 20.1 %collective-permute-start.16 = (bf16[2,160,768]{2,1,0:T(8,128)(2,1)}, bf16[2,160,768]{2,1,0:T(8,128)(2,1)}, u32[]{:S(2)}, u32[]{:S(2)}) collective-permute-start(bf16[2,160,768]{2,1,0:T(8,128)(2,1)} %fusion.69), channel_id=1, source_target_pairs={{0,1},{1,0},{2,3},{3,2},{4,5},{5,4},{6,7},{7,6},{8,9},{9,8},{10,11... | collective-permute-start | bytes 1474568 | tf_op jit(solution)/shard_map/ppermute | solution.py:36
  375.0 27.3 %collective-permute-start.21 = (bf16[2,2,2,2,45,768]{5,3,4,2,1,0:T(2,128)(2,1)}, bf16[2,2,2,2,45,768]{5,3,4,2,1,0:T(2,128)(2,1)}, u32[]{:S(2)}, u32[]{:S(2)}) collective-permute-start(bf16[2,2,2,2,45,768]{5,3,4,2,1,0:T(2,128)(2,1)} %bitcast.378), channel_id=1, source_target_pairs={{0,1},{1,0},{2,3},{3,2},{4,5},{5,4},{6,7},{7,6},{8,9},{9,8},{10,11... | collective-permute-start | bytes 3317768 | tf_op jit(solution)/shard_map/ppermute | solution.py:36
  375.0 55.3 %collective-permute-start.26 = (bf16[2,2,2,2,24,2304]{5,4,0,1,2,3:T(8,128)(2,1)}, bf16[2,2,2,2,24,2304]{5,4,0,1,2,3:T(8,128)(2,1)}, u32[]{:S(2)}, u32[]{:S(2)}) collective-permute-start(bf16[2,2,2,2,24,2304]{5,4,0,1,2,3:T(8,128)(2,1)} %bitcast.377), channel_id=1, source_target_pairs={{0,1},{1,0},{2,3},{3,2},{4,5},{5,4},{6,7},{7,6},{8,9},{9,8},{10,11... | collective-permute-start | bytes 5308424 | tf_op jit(solution)/shard_map/ppermute | solution.py:36
  405.5 14.0 %collective-permute-start.22 = (bf16[2,2,2,45,768]{4,2,3,1,0:T(2,128)(2,1)S(1)}, bf16[2,2,2,45,768]{4,2,3,1,0:T(2,128)(2,1)S(1)}, u32[]{:S(2)}, u32[]{:S(2)}) collective-permute-start(bf16[2,2,2,45,768]{4,2,3,1,0:T(2,128)(2,1)S(1)} %bitcast.411), channel_id=1, source_target_pairs={{0,4},{1,5},{2,6},{3,7},{4,0},{5,1},{6,2},{7,3},{8,12},{9,13},{10,... | collective-permute-start | bytes 1658888 | tf_op jit(solution)/shard_map/ppermute | solution.py:36
  437.3 22.7 %collective-permute-start.27 = (bf16[2,2,2,24,2304]{4,3,0,1,2:T(8,128)(2,1)S(1)}, bf16[2,2,2,24,2304]{4,3,0,1,2:T(8,128)(2,1)S(1)}, u32[]{:S(2)}, u32[]{:S(2)}) collective-permute-start(bf16[2,2,2,24,2304]{4,3,0,1,2:T(8,128)(2,1)S(1)} %dynamic-slice_bitcast_fusion.2), channel_id=1, source_target_pairs={{0,2},{1,3},{2,0},{3,1},{4,6},{5,7},{6,4},{7,5},{8,10},{9,11},{10,... | collective-permute-start | bytes 2654216 | tf_op jit(solution)/shard_map/ppermute | solution.py:36
  445.1 35.0 %collective-permute-start.37 = (bf16[2,2,2,96,768]{4,3,0,1,2:T(8,128)(2,1)S(1)}, bf16[2,2,2,96,768]{4,3,0,1,2:T(8,128)(2,1)S(1)}, u32[]{:S(2)}, u32[]{:S(2)}) collective-permute-start(bf16[2,2,2,96,768]{4,3,0,1,2:T(8,128)(2,1)S(1)} %dynamic-slice_bitcast_fusion), channel_id=1, source_target_pairs={{0,2},{1,3},{2,0},{3,1},{4,6},{5,7},{6,4},{7,5},{8,10},{9,11},{10,... | collective-permute-start | bytes 3538952 | tf_op jit(solution)/shard_map/ppermute | solution.py:36
  474.8 23.8 %collective-permute-start.32 = (bf16[2,2,2,24,3072]{4,3,0,1,2:T(8,128)(2,1)S(1)}, bf16[2,2,2,24,3072]{4,3,0,1,2:T(8,128)(2,1)S(1)}, u32[]{:S(2)}, u32[]{:S(2)}) collective-permute-start(bf16[2,2,2,24,3072]{4,3,0,1,2:T(8,128)(2,1)S(1)} %dynamic-slice_bitcast_fusion.1), channel_id=1, source_target_pairs={{0,4},{1,5},{2,6},{3,7},{4,0},{5,1},{6,2},{7,3},{8,12},{9,13},{10,... | collective-permute-start | bytes 3538952 | tf_op jit(solution)/shard_map/ppermute | solution.py:36
  479.6 21.1 %collective-permute-start.30 = (bf16[24,2304]{1,0:T(8,128)(2,1)S(1)}, bf16[24,2304]{1,0:T(8,128)(2,1)S(1)}, u32[]{:S(2)}, u32[]{:S(2)}) collective-permute-start(bf16[24,2304]{1,0:T(8,128)(2,1)S(1)} %dynamic-slice_bitcast_fusion.13), channel_id=1, source_target_pairs={{0,16},{1,17},{2,18},{3,19},{4,20},{5,21},{6,22},{7,23},{8,24},{9,... | collective-permute-start | bytes 331784 | tf_op jit(solution)/shard_map/ppermute | solution.py:36
  480.5 24.5 %collective-permute-start.38 = (bf16[2,2,96,768]{3,2,0,1:T(8,128)(2,1)S(1)}, bf16[2,2,96,768]{3,2,0,1:T(8,128)(2,1)S(1)}, u32[]{:S(2)}, u32[]{:S(2)}) collective-permute-start(bf16[2,2,96,768]{3,2,0,1:T(8,128)(2,1)S(1)} %dynamic-slice_bitcast_fusion.3), channel_id=1, source_target_pairs={{0,4},{1,5},{2,6},{3,7},{4,0},{5,1},{6,2},{7,3},{8,12},{9,13},{10,... | collective-permute-start | bytes 1769480 | tf_op jit(solution)/shard_map/ppermute | solution.py:36
  (113 other events, 827.4 us)

commit v2 on v1

v2 whole, which is shorter than its diff:
```python
import functools
import math

import jax
import jax.numpy as jnp
from jax import lax
from jax.experimental import pallas as pl
from jax.experimental.pallas import tpu as pltpu
from jax.sharding import PartitionSpec as P

HEADS = 12
EPSILON = 1e-06
AXES = ("dp", "var")
BF16 = jnp.bfloat16
F32 = jnp.float32
LANES = 128
ROWS = 256
MASKED = -1000000000.0


def dot(left, right, dims):
    return lax.dot_general(left, right, (dims, ((), ())), preferred_element_type=F32)


def nn(left, right):
    return dot(left, right, ((1,), (0,)))


def nt(left, right):
    return dot(left, right, ((1,), (1,)))


def tn(left, right):
    return dot(left, right, ((0,), (0,)))


def shape(dims, dtype):
    return jax.ShapeDtypeStruct(dims, dtype)


def whole(array):
    zeros = (0,) * array.ndim
    return pl.BlockSpec(array.shape, lambda *_: zeros, pipeline_mode=pl.Buffered(1))


def across(rows, width):
    return pl.BlockSpec((rows, width), lambda i, *_: (i, 0))


def along(height, columns):
    return pl.BlockSpec((height, columns), lambda i, *_: (0, i))


def fixed(*dims):
    zeros = (0,) * len(dims)
    return pl.BlockSpec(dims, lambda *_: zeros)


def params(mebibytes):
    return pltpu.CompilerParams(vmem_limit_bytes=mebibytes << 20)


def cost(flops, nbytes):
    return pl.CostEstimate(flops=int(flops), bytes_accessed=int(nbytes), transcendentals=0)


def iota(dims, axis):
    return lax.broadcasted_iota(jnp.int32, dims, axis)


def accumulate(ref, first, value):
    @pl.when(first)
    def _():
        ref[...] = value

    @pl.when(jnp.logical_not(first))
    def _():
        ref[...] += value


def normalize(values):
    center = values - jnp.mean(values, axis=-1, keepdims=True)
    inverse = lax.rsqrt(jnp.mean(center * center, axis=-1, keepdims=True) + EPSILON)
    return center * inverse, inverse


def normalize_back(upstream, normed, inverse, gains):
    scaled = upstream * gains
    mean_plain = jnp.mean(scaled, axis=-1, keepdims=True)
    mean_mixed = jnp.mean(scaled * normed, axis=-1, keepdims=True)
    return inverse * (scaled - mean_plain - normed * mean_mixed)


def gelu_parts(u):
    ratio = 1.0 / (1.0 + (0.3275911 * math.sqrt(0.5)) * jnp.abs(u))
    bell = jnp.exp(-0.5 * u * u)
    series = 0.5 * 1.061405429
    for factor in (-1.453152027, 1.421413741, -0.284496736, 0.254829592):
        series = series * ratio + 0.5 * factor
    tail = series * ratio * bell
    below = jnp.where(u < 0, tail, 1.0 - tail)
    return u * below, below + u * (bell * (1.0 / math.sqrt(2.0 * math.pi)))


class Sizes:
    def __init__(self, keep_lo, keep_hi, w_embed, img_lo, img_hi, groups):
        self.lo_each, self.hi_each = keep_lo[0] // groups, keep_hi[0] // groups
        self.lo_length, self.hi_length = keep_lo[1], keep_hi[1]
        self.features, self.width = w_embed
        self.lo_patches, self.hi_patches = img_lo[1], img_hi[1]
        self.groups = groups
        self.pack = LANES // self.lo_length
        self.lo_tiles = -(-self.lo_each // self.pack)
        self.hi_rows = self.hi_each * self.hi_length
        tiles = self.hi_each + self.lo_tiles
        self.tiles = tiles + tiles % 2
        self.rows = self.tiles * LANES


def sample_tiles(s):
    out = []
    for t in range(s.tiles - s.hi_each):
        first = t * s.pack
        out.append((s.hi_each + t, first, max(0, min(s.pack, s.lo_each - first))))
    return out


def slots(rows, fill, s):
    missing = s.pack - len(rows)
    if missing:
        rows = rows + [jnp.full((1, missing * s.lo_length), fill, rows[0].dtype if rows else jnp.int32)]
    return rows[0] if len(rows) == 1 else jnp.concatenate(rows, axis=1)


def pick_kernel(s, members, member_ref, keep_lo_ref, keep_hi_ref, img_lo_ref, img_hi_ref, *out_refs):
    for k, out_ref in zip(members, out_refs):
        other = member_ref[0] ^ k
        for i in range(s.hi_each):
            at = other * s.hi_each + i
            chosen = iota((s.hi_patches, LANES), 0) == keep_hi_ref[pl.ds(at, 1), :]
            got = nn(img_hi_ref[at], jnp.where(chosen, 1.0, 0.0).astype(BF16))
            out_ref[:, i * LANES : (i + 1) * LANES] = got.astype(BF16)
        for tile, first, count in sample_tiles(s):
            parts = []
            for j in range(count):
                at = other * s.lo_each + first + j
                chosen = iota((s.lo_patches, s.lo_length), 0) == keep_lo_ref[pl.ds(at, 1), :]
                parts.append(nn(img_lo_ref[at], jnp.where(chosen, 1.0, 0.0).astype(BF16)))
            if count < s.pack:
                parts.append(jnp.zeros((s.features, (s.pack - count) * s.lo_length), F32))
            joined = jnp.concatenate(parts, axis=1) if len(parts) > 1 else parts[0]
            out_ref[:, tile * LANES : (tile + 1) * LANES] = joined.astype(BF16)


def pick(s, members, member, keep_lo, keep_hi, img_lo, img_hi):
    args = (keep_lo, keep_hi, img_lo, img_hi)
    return pl.pallas_call(
        functools.partial(pick_kernel, s, members),
        grid_spec=pltpu.PrefetchScalarGridSpec(
            num_scalar_prefetch=1,
            grid=(1,),
            in_specs=[whole(a) for a in args],
            out_specs=[fixed(s.features, s.rows)] * len(members),
        ),
        out_shape=[shape((s.features, s.rows), BF16)] * len(members),
        compiler_params=params(24),
        cost_estimate=cost(2e9, 4e6),
    )(member, *args)


def stage_kernel(s, member_ref, keep_lo_ref, keep_hi_ref, mask_lo_ref, mask_hi_ref, cot_lo_ref, cot_hi_ref, keep_ref, seen_ref, *out_refs):
    eye = jnp.where(iota((s.features, s.features), 0) == iota((s.features, s.features), 1), 1.0, 0.0).astype(BF16)
    first_hi = (iota((1, s.hi_length), 1) == 0).astype(jnp.int32)
    first_lo = (iota((1, s.lo_length), 1) == 0).astype(jnp.int32)
    for k, out_ref in enumerate(out_refs):
        other = member_ref[0] ^ k
        for i in range(s.hi_each):
            at = other * s.hi_each + i
            keep_ref[k, i : i + 1, :] = keep_hi_ref[pl.ds(at, 1), :]
            out_ref[:, i * LANES : (i + 1) * LANES] = cot_hi_ref[at]
            if k == 0:
                seen_ref[i : i + 1, :] = jnp.maximum(mask_hi_ref[pl.ds(at, 1), :], first_hi).astype(F32)
        for tile, first, count in sample_tiles(s):
            begin = other * s.lo_each + first
            keep_ref[k, tile : tile + 1, :] = slots([keep_lo_ref[pl.ds(begin + j, 1), :] for j in range(count)], -1, s)
            if k == 0:
                seen = [jnp.maximum(mask_lo_ref[pl.ds(begin + j, 1), :], first_lo) for j in range(count)]
                seen_ref[tile : tile + 1, :] = slots(seen, 0, s).astype(F32)
            where = slice(tile * LANES, (tile + 1) * LANES)
            if count < s.pack:
                out_ref[:, where] = jnp.zeros((s.features, LANES), BF16)
            if count:
                size = count * s.lo_length
                start = pl.multiple_of(begin * s.lo_length, s.lo_length)
                out_ref[:, tile * LANES : tile * LANES + size] = nt(eye, cot_lo_ref[pl.ds(start, size), :]).astype(BF16)


def stage(s, member, keep_lo, keep_hi, mask_lo, mask_hi, cot_lo, cot_hi):
    args = (keep_lo, keep_hi, mask_lo, mask_hi, cot_lo, cot_hi)
    return pl.pallas_call(
        functools.partial(stage_kernel, s),
        grid_spec=pltpu.PrefetchScalarGridSpec(
            num_scalar_prefetch=1,
            grid=(1,),
            in_specs=[whole(a) for a in args],
            out_specs=[fixed(s.groups, s.tiles, LANES), fixed(s.tiles, LANES)]
            + [fixed(s.features, s.rows)] * s.groups,
        ),
        out_shape=[shape((s.groups, s.tiles, LANES), jnp.int32), shape((s.tiles, LANES), F32)]
        + [shape((s.features, s.rows), BF16)] * s.groups,
        compiler_params=params(24),
        cost_estimate=cost(1e8, 4e6),
    )(member, *args)


def chosen_rows(s, keep_ref, tile, patches, wanted_hi):
    row = keep_ref[pl.ds(tile, 1), :]
    is_hi = tile < s.hi_each
    row = jnp.where(is_hi if wanted_hi else jnp.logical_not(is_hi), row, -1)
    return jnp.where(iota((patches, LANES), 0) == row, 1.0, 0.0).astype(BF16)


def pair_masks():
    lane = iota((1, LANES), 1)
    low = jnp.where(lane < LANES // 2, 1.0, 0.0).astype(BF16)
    high = jnp.where(lane < LANES // 2, 0.0, 1.0).astype(BF16)
    return low, high


def doubled(block, masks):
    return jnp.concatenate([block * masks[0], block * masks[1]], axis=0)


def allowed(s, seen_ref, tile):
    bits = jnp.where(tile < s.hi_each, s.hi_length.bit_length() - 1, s.lo_length.bit_length() - 1)
    same = (iota((LANES, LANES), 0) >> bits) == (iota((LANES, LANES), 1) >> bits)
    open_to = jnp.logical_and(same, seen_ref[pl.ds(tile, 1), :] > 0)
    return jnp.concatenate([open_to, open_to], axis=0)


def forward_kernel(s, heads, keep_ref, seen_ref, p0, p1, p2, p3, w0, w1, w2, w3, pos_lo_ref, pos_hi_ref, gain1_ref, wqkv_ref, gain2_ref, wout_ref, x0_ref, a_ref, qkv_ref, probs_ref, mixed_ref, x1_ref, b_ref):
    step = pl.program_id(0)
    per = ROWS // LANES
    width = s.width
    picked = jnp.concatenate([p[...] for p in (p0, p1, p2, p3)], axis=0)
    embed = jnp.concatenate([w[: s.features, :] for w in (w0, w1, w2, w3)], axis=0)
    hot_hi = jnp.concatenate([chosen_rows(s, keep_ref, step * per + j, s.hi_patches, True) for j in range(per)], axis=1)
    hot_lo = jnp.concatenate([chosen_rows(s, keep_ref, step * per + j, s.lo_patches, False) for j in range(per)], axis=1)
    start = tn(picked, embed) + (tn(hot_hi, pos_hi_ref[...]) + tn(hot_lo, pos_lo_ref[...]))
    x0_ref[...] = start
    normed, _ = normalize(start)
    normed = (normed * gain1_ref[...]).astype(BF16)
    a_ref[...] = normed
    for c in range(3):
        part = slice(c * width, (c + 1) * width)
        qkv_ref[:, part] = nn(normed, wqkv_ref[:, part]).astype(BF16)
    masks = pair_masks()
    scale = 1.0 / math.sqrt(width // heads)
    for j in range(per):
        rows = slice(j * LANES, (j + 1) * LANES)
        ok = allowed(s, seen_ref, step * per + j)
        for h in range(width // LANES):
            at = h * LANES
            q = qkv_ref[rows, at : at + LANES]
            k = qkv_ref[rows, width + at : width + at + LANES]
            v = qkv_ref[rows, 2 * width + at : 2 * width + at + LANES]
            scores = nt(doubled(q, masks), k) * scale
            scores = jnp.where(ok, scores, MASKED)
            raised = jnp.exp(scores - jnp.max(scores, axis=-1, keepdims=True))
            probs = raised / jnp.sum(raised, axis=-1, keepdims=True)
            probs_ref[j, h] = probs
            rounded = probs.astype(BF16)
            wide = jnp.concatenate([rounded[:LANES], rounded[LANES:]], axis=1)
            mixed_ref[rows, at : at + LANES] = nn(wide, doubled(v, masks)).astype(BF16)
    middle = start + nn(mixed_ref[...], wout_ref[...])
    x1_ref[...] = middle
    normed, _ = normalize(middle)
    b_ref[...] = (normed * gain2_ref[...]).astype(BF16)


def forward(s, heads, keep, seen, picked, weights, pos_lo, pos_hi, gain1, wqkv, gain2, wout):
    width, rows = s.width, s.rows
    per, pairs = ROWS // LANES, width // LANES
    return pl.pallas_call(
        functools.partial(forward_kernel, s, heads),
        grid=(rows // ROWS,),
        in_specs=[whole(keep), whole(seen)]
        + [along(s.features, ROWS)] * 4
        + [whole(w) for w in weights]
        + [whole(a) for a in (pos_lo, pos_hi, gain1, wqkv, gain2, wout)],
        out_specs=[
            across(ROWS, width),
            across(ROWS, width),
            across(ROWS, 3 * width),
            pl.BlockSpec((per, pairs, 2 * LANES, LANES), lambda i: (i, 0, 0, 0)),
            across(ROWS, width),
            across(ROWS, width),
            across(ROWS, width),
        ],
        out_shape=[
            shape((rows, width), F32),
            shape((rows, width), BF16),
            shape((rows, 3 * width), BF16),
            shape((s.tiles, pairs, 2 * LANES, LANES), F32),
            shape((rows, width), BF16),
            shape((rows, width), F32),
            shape((rows, width), BF16),
        ],
        compiler_params=params(40),
        cost_estimate=cost(1.5e10, 3e7),
    )(keep, seen, *picked, *weights, pos_lo, pos_hi, gain1, wqkv, gain2, wout)


def upstream_kernel(s, seen_ref, c0, c1, c2, c3, w0, w1, w2, w3, gpred_ref, gm_ref, gb2_ref):
    step = pl.program_id(0)
    per = ROWS // LANES
    seen = jnp.concatenate([seen_ref[pl.ds(step * per + j, 1), :] for j in range(per)], axis=1).astype(BF16)
    grads = jnp.concatenate([c[...] for c in (c0, c1, c2, c3)], axis=0) * seen
    gpred_ref[...] = grads
    head = jnp.concatenate([w[s.features :, :] for w in (w0, w1, w2, w3)], axis=0)
    rounded = tn(grads, head).astype(BF16)
    gm_ref[...] = rounded
    accumulate(gb2_ref, step == 0, jnp.sum(rounded.astype(F32), axis=0, keepdims=True))


def upstream(s, seen, cots, weights):
    rows, width = s.rows, s.width
    high = s.groups * s.features
    return pl.pallas_call(
        functools.partial(upstream_kernel, s),
        grid=(rows // ROWS,),
        in_specs=[whole(seen)] + [along(s.features, ROWS)] * 4 + [whole(w) for w in weights],
        out_specs=[along(high, ROWS), across(ROWS, width), fixed(1, width)],
        out_shape=[shape((high, rows), BF16), shape((rows, width), BF16), shape((1, width), F32)],
        compiler_params=params(16),
        cost_estimate=cost(1e9, 4e6),
    )(seen, *cots, *weights)


def hidden_kernel(sub, b_ref, gm_ref, w1_ref, b1_ref, w2_ref, z_ref, gu_ref, gb1_ref):
    w1, w2, bias = w1_ref[...], w2_ref[...], b1_ref[...]
    total = None
    for i in range(b_ref.shape[0] // sub):
        rows = slice(i * sub, (i + 1) * sub)
        u = nn(b_ref[rows, :], w1) + bias
        upward = nt(gm_ref[rows, :], w2)
        z, slope = gelu_parts(u)
        z_ref[rows, :] = z.astype(BF16)
        gu = (upward * slope).astype(BF16)
        gu_ref[rows, :] = gu
        part = jnp.sum(gu.astype(F32), axis=0, keepdims=True)
        total = part if total is None else total + part
    gb1_ref[...] = total


def hidden(b, gm, w1, b1, w2, columns=768, sub=256):
    rows, width = b.shape
    inner = w1.shape[1]
    return pl.pallas_call(
        functools.partial(hidden_kernel, sub),
        grid=(inner // columns,),
        in_specs=[
            whole(b),
            whole(gm),
            along(width, columns),
            along(1, columns),
            across(columns, width),
        ],
        out_specs=[along(rows, columns), along(rows, columns), along(1, columns)],
        out_shape=[shape((rows, inner), BF16), shape((rows, inner), BF16), shape((1, inner), F32)],
        compiler_params=params(40),
        cost_estimate=cost(2e10, 2.5e7),
    )(b, gm, w1, b1, w2)


def weight_kernel(left_ref, right_ref, out_ref):
    out_ref[...] = tn(left_ref[...], right_ref[...]).astype(BF16)


def weight_grad(left, right, tall, broad):
    rows = left.shape[0]
    m, n = left.shape[1], right.shape[1]
    return pl.pallas_call(
        weight_kernel,
        grid=(m // tall, n // broad),
        in_specs=[
            pl.BlockSpec((rows, tall), lambda i, j: (0, i)),
            pl.BlockSpec((rows, broad), lambda i, j: (0, j)),
        ],
        out_specs=pl.BlockSpec((tall, broad), lambda i, j: (i, j)),
        out_shape=shape((m, n), BF16),
        compiler_params=params(32),
        cost_estimate=cost(2 * rows * m * n, 2 * (rows * (m + n) + m * n)),
    )(left, right)


def middle_kernel(s, seen_ref, x1_ref, z_ref, gu_ref, gm_ref, gpred_ref, mixed_ref, w1_ref, w2_ref, b2_ref, gain2_ref, wout_ref, h0, h1, h2, h3, o0, o1, o2, o3, g1_ref, go_ref, ghead_ref, gln2_ref, gout_ref):
    step = pl.program_id(0)
    per = ROWS // LANES
    first = step == 0
    middle = x1_ref[...]
    final = (middle + (nn(z_ref[...], w2_ref[...]) + b2_ref[...])).astype(BF16)
    seen = jnp.concatenate([seen_ref[pl.ds(step * per + j, 1), :] for j in range(per)], axis=1)
    for head, out in zip((h0, h1, h2, h3), (o0, o1, o2, o3)):
        out[...] = (nt(head[s.features :, :], final) * seen).astype(BF16)
    accumulate(ghead_ref, first, nn(gpred_ref[...], final))
    upward = nt(gu_ref[...], w1_ref[...])
    normed, inverse = normalize(middle)
    accumulate(gln2_ref, first, jnp.sum(upward * normed, axis=0, keepdims=True))
    grad = gm_ref[...].astype(F32) + normalize_back(upward, normed, inverse, gain2_ref[...])
    g1_ref[...] = grad
    rounded = grad.astype(BF16)
    go_ref[...] = nt(rounded, wout_ref[...]).astype(BF16)
    accumulate(gout_ref, first, tn(mixed_ref[...], rounded))


def middle(s, seen, x1, z, gu, gm, gpred, mixed, w1, w2, b2, gain2, wout, weights):
    rows, width = s.rows, s.width
    inner = w1.shape[1]
    high = s.groups * s.features
    return pl.pallas_call(
        functools.partial(middle_kernel, s),
        grid=(rows // ROWS,),
        in_specs=[
            whole(seen),
            across(ROWS, width),
            across(ROWS, inner),
            across(ROWS, inner),
            across(ROWS, width),
            along(high, ROWS),
            across(ROWS, width),
        ]
        + [whole(a) for a in (w1, w2, b2, gain2, wout, *weights)],
        out_specs=[along(s.features, ROWS)] * 4
        + [
            across(ROWS, width),
            across(ROWS, width),
            fixed(high, width),
            fixed(1, width),
            fixed(width, width),
        ],
        out_shape=[shape((s.features, rows), BF16)] * 4
        + [
            shape((rows, width), F32),
            shape((rows, width), BF16),
            shape((high, width), F32),
            shape((1, width), F32),
            shape((width, width), F32),
        ],
        compiler_params=params(44),
        cost_estimate=cost(1.5e10, 3e7),
    )(seen, x1, z, gu, gm, gpred, mixed, w1, w2, b2, gain2, wout, *weights)


def backward_kernel(s, heads, keep_ref, qkv_ref, probs_ref, go_ref, x0_ref, g1_ref, p0, p1, p2, p3, wqkv_ref, gain1_ref, w0, w1, w2, w3, gqkv_ref, o0, o1, o2, o3, gln1_ref, glo_ref, ghi_ref, gembed_ref):
    step = pl.program_id(0)
    per = ROWS // LANES
    width = s.width
    first = step == 0
    masks = pair_masks()
    scale = 1.0 / math.sqrt(width // heads)
    for j in range(per):
        rows = slice(j * LANES, (j + 1) * LANES)
        for h in range(width // LANES):
            at = h * LANES
            q = doubled(qkv_ref[rows, at : at + LANES], masks)
            k = doubled(qkv_ref[rows, width + at : width + at + LANES], masks)
            v = qkv_ref[rows, 2 * width + at : 2 * width + at + LANES]
            out = doubled(go_ref[rows, at : at + LANES], masks)
            probs = probs_ref[j, h]
            upward = nt(out, v)
            centred = upward - jnp.sum(probs * upward, axis=-1, keepdims=True)
            grads = (probs * centred).astype(BF16)
            wide = jnp.concatenate([grads[:LANES], grads[LANES:]], axis=1)
            gqkv_ref[rows, at : at + LANES] = (nn(wide, k) * scale).astype(BF16)
            gqkv_ref[rows, width + at : width + at + LANES] = (tn(grads, q) * scale).astype(BF16)
            gqkv_ref[rows, 2 * width + at : 2 * width + at + LANES] = tn(probs.astype(BF16), out).astype(BF16)
    upward = nt(gqkv_ref[...], wqkv_ref[...])
    normed, inverse = normalize(x0_ref[...])
    accumulate(gln1_ref, first, jnp.sum(upward * normed, axis=0, keepdims=True))
    grad = (g1_ref[...] + normalize_back(upward, normed, inverse, gain1_ref[...])).astype(BF16)
    for weight, out in zip((w0, w1, w2, w3), (o0, o1, o2, o3)):
        out[...] = nt(weight[: s.features, :], grad).astype(BF16)
    hot_hi = jnp.concatenate([chosen_rows(s, keep_ref, step * per + j, s.hi_patches, True) for j in range(per)], axis=1)
    hot_lo = jnp.concatenate([chosen_rows(s, keep_ref, step * per + j, s.lo_patches, False) for j in range(per)], axis=1)
    accumulate(ghi_ref, first, nn(hot_hi, grad))
    accumulate(glo_ref, first, nn(hot_lo, grad))
    picked = jnp.concatenate([p[...] for p in (p0, p1, p2, p3)], axis=0)
    accumulate(gembed_ref, first, nn(picked, grad))


def backward(s, heads, keep, qkv, probs, go, x0, g1, picked, wqkv, gain1, weights):
    rows, width = s.rows, s.width
    per, pairs = ROWS // LANES, width // LANES
    high = s.groups * s.features
    return pl.pallas_call(
        functools.partial(backward_kernel, s, heads),
        grid=(rows // ROWS,),
        in_specs=[
            whole(keep),
            across(ROWS, 3 * width),
            pl.BlockSpec((per, pairs, 2 * LANES, LANES), lambda i: (i, 0, 0, 0)),
            across(ROWS, width),
            across(ROWS, width),
            across(ROWS, width),
        ]
        + [along(s.features, ROWS)] * 4
        + [whole(a) for a in (wqkv, gain1, *weights)],
        out_specs=[across(ROWS, 3 * width)]
        + [along(s.features, ROWS)] * 4
        + [
            fixed(1, width),
            fixed(s.lo_patches, width),
            fixed(s.hi_patches, width),
            fixed(high, width),
        ],
        out_shape=[shape((rows, 3 * width), BF16)]
        + [shape((s.features, rows), BF16)] * 4
        + [
            shape((1, width), F32),
            shape((s.lo_patches, width), F32),
            shape((s.hi_patches, width), F32),
            shape((high, width), F32),
        ],
        compiler_params=params(44),
        cost_estimate=cost(1.5e10, 3e7),
    )(keep, qkv, probs, go, x0, g1, *picked, wqkv, gain1, *weights)


def place_kernel(s, member_ref, keep_ref, r0, r1, r2, r3, lo_ref, hi_ref):
    lane_sample = iota((1, LANES), 1) // s.lo_length
    for k, got_ref in enumerate((r0, r1, r2, r3)):
        other = member_ref[0] ^ k
        for i in range(s.hi_each):
            chosen = iota((s.hi_patches, LANES), 0) == keep_ref[k, i : i + 1, :]
            hot = jnp.where(chosen, 1.0, 0.0).astype(BF16)
            hi_ref[other * s.hi_each + i] = nt(got_ref[:, i * LANES : (i + 1) * LANES], hot).astype(BF16)
        for tile, first, count in sample_tiles(s):
            got = got_ref[:, tile * LANES : (tile + 1) * LANES]
            for j in range(count):
                row = jnp.where(lane_sample == j, keep_ref[k, tile : tile + 1, :], -1)
                hot = jnp.where(iota((s.lo_patches, LANES), 0) == row, 1.0, 0.0).astype(BF16)
                lo_ref[other * s.lo_each + first + j] = nt(got, hot).astype(BF16)


def place(s, member, keep, blocks):
    lo = s.groups * s.lo_each
    hi = s.groups * s.hi_each
    return pl.pallas_call(
        functools.partial(place_kernel, s),
        grid_spec=pltpu.PrefetchScalarGridSpec(
            num_scalar_prefetch=1,
            grid=(1,),
            in_specs=[whole(keep)] + [whole(b) for b in blocks],
            out_specs=[fixed(lo, s.features, s.lo_patches), fixed(hi, s.features, s.hi_patches)],
        ),
        out_shape=[
            shape((lo, s.features, s.lo_patches), BF16),
            shape((hi, s.features, s.hi_patches), BF16),
        ],
        compiler_params=params(24),
        cost_estimate=cost(2e9, 4e6),
    )(member, keep, *blocks)


def predict_kernel(s, member_ref, r0, r1, r2, r3, lo_ref, hi_ref):
    eye = jnp.where(iota((s.features, s.features), 0) == iota((s.features, s.features), 1), 1.0, 0.0).astype(BF16)
    for k, got_ref in enumerate((r0, r1, r2, r3)):
        other = member_ref[0] ^ k
        for i in range(s.hi_each):
            hi_ref[other * s.hi_each + i] = got_ref[:, i * LANES : (i + 1) * LANES]
        for tile, first, count in sample_tiles(s):
            if count:
                size = count * s.lo_length
                turned = tn(got_ref[:, tile * LANES : (tile + 1) * LANES], eye).astype(BF16)
                start = pl.multiple_of((other * s.lo_each + first) * s.lo_length, s.lo_length)
                lo_ref[pl.ds(start, size), :] = turned[:size]


def predict(s, member, blocks):
    lo = s.groups * s.lo_each * s.lo_length
    hi = s.groups * s.hi_each
    return pl.pallas_call(
        functools.partial(predict_kernel, s),
        grid_spec=pltpu.PrefetchScalarGridSpec(
            num_scalar_prefetch=1,
            grid=(1,),
            in_specs=[whole(b) for b in blocks],
            out_specs=[fixed(lo, s.features), fixed(hi, s.features, s.hi_length)],
        ),
        out_shape=[shape((lo, s.features), BF16), shape((hi, s.features, s.hi_length), BF16)],
        compiler_params=params(16),
        cost_estimate=cost(1e8, 3e6),
    )(member, *blocks)


def swap(value, data_bit, var_bit):
    dp, var = lax.axis_size("dp"), lax.axis_size("var")
    pairs = [
        (d * var + v, (d ^ data_bit) * var + (v ^ var_bit)) for d in range(dp) for v in range(var)
    ]
    return lax.ppermute(value, AXES, pairs)


def add_rounded(left, right):
    return (left.astype(F32) + right.astype(F32)).astype(BF16)


def stages(order):
    dp, var = lax.axis_size("dp"), lax.axis_size("var")
    data = [("d", 1 << i) for i in range(dp.bit_length() - 1)]
    core = [("v", 1 << i) for i in range(var.bit_length() - 1)]
    if order == 0:
        return core + data
    return core[:1] + data[:1] + core[1:] + data[1:]


def reduce_scatter(full, order):
    dp, var = lax.axis_size("dp"), lax.axis_size("var")
    places = [("d", 1 << i) for i in reversed(range(dp.bit_length() - 1))]
    places += [("v", 1 << i) for i in reversed(range(var.bit_length() - 1))]
    rows = full.shape[0] // (dp * var)
    value = full.astype(BF16).reshape((2,) * len(places) + (rows,) + full.shape[1:])
    d, v = lax.axis_index("dp"), lax.axis_index("var")
    for stage_of in stages(order):
        axis = places.index(stage_of)
        kind, bit = stage_of
        mine = ((d if kind == "d" else v) // bit) % 2
        keep = lax.dynamic_index_in_dim(value, mine, axis, keepdims=False)
        send = lax.dynamic_index_in_dim(value, 1 - mine, axis, keepdims=False)
        got = swap(send, bit if kind == "d" else 0, bit if kind == "v" else 0)
        value = add_rounded(keep, got)
        places.remove(stage_of)
    return value.astype(F32)


def reduce_relative(blocks):
    var, dp = lax.axis_size("var"), lax.axis_size("dp")
    value = blocks
    bit = 1
    while bit < var:
        value = value.reshape((value.shape[0] // 2, 2) + value.shape[1:])
        value = add_rounded(value[:, 0], swap(value[:, 1], 0, bit))
        bit *= 2
    value = value[0]
    bit = 1
    while bit < dp:
        value = add_rounded(value, swap(value, bit, 0))
        bit *= 2
    return value.astype(F32)


def exchange_relative(blocks):
    return [blocks[0]] + [swap(blocks[k], 0, k) for k in range(1, len(blocks))]


def body(
    img_lo,
    img_hi,
    keep_lo,
    keep_hi,
    mask_lo,
    mask_hi,
    w_embed,
    pos_lo,
    pos_hi,
    ln1_gain,
    w_qkv,
    w_out,
    ln2_gain,
    w_fc1,
    b_fc1,
    w_fc2,
    b_fc2,
    w_head,
    cot_lo,
    cot_hi,
):
    groups = lax.axis_size("var")
    devices = lax.axis_size("dp") * groups
    member = lax.axis_index("var").astype(jnp.int32).reshape(1)
    s = Sizes(keep_lo.shape, keep_hi.shape, w_embed.shape, img_lo.shape, img_hi.shape, groups)
    features, width = s.features, s.width
    gain1, gain2 = ln1_gain.reshape(1, -1), ln2_gain.reshape(1, -1)
    img_lo_t, img_hi_t = img_lo.transpose(0, 2, 1), img_hi.transpose(0, 2, 1)

    own = jnp.concatenate([w_embed, w_head.T], axis=0)
    crossed = swap(own, 0, 2)
    weights = [own, swap(own, 0, 1), crossed, swap(crossed, 0, 1)]
    sent = pick(s, (1, 2, 3), member, keep_lo, keep_hi, img_lo_t, img_hi_t)
    picked = [swap(value, 0, k + 1) for k, value in enumerate(sent)]
    picked = [*pick(s, (0,), member, keep_lo, keep_hi, img_lo_t, img_hi_t), *picked]
    keep, seen, *cots = stage(
        s,
        member,
        keep_lo,
        keep_hi,
        mask_lo,
        mask_hi,
        cot_lo.reshape(-1, features),
        cot_hi.transpose(0, 2, 1),
    )
    cots = exchange_relative(cots)
    own_keep = keep[0]
    x0, a, qkv, probs, mixed, x1, b = forward(
        s, HEADS, own_keep, seen, picked, weights, pos_lo, pos_hi, gain1, w_qkv, gain2, w_out
    )
    gpred, gm, grad_b2 = upstream(s, seen, cots, weights)
    z, gu, grad_b1 = hidden(b, gm, w_fc1, b_fc1.reshape(1, -1), w_fc2)
    grad_fc2 = reduce_scatter(weight_grad(z, gm, 768, width), 0)
    grad_fc1 = reduce_scatter(weight_grad(b, gu, width, 1024), 1)
    *preds, g1, go, grad_head, grad_ln2, grad_out = middle(
        s,
        seen,
        x1,
        z,
        gu,
        gm,
        gpred,
        mixed,
        w_fc1,
        w_fc2,
        b_fc2.reshape(1, -1),
        gain2,
        w_out,
        weights,
    )
    pred_lo, pred_hi = predict(s, member, exchange_relative(preds))
    gqkv, *blocks, grad_ln1, grad_pos_lo, grad_pos_hi, grad_embed = backward(
        s, HEADS, own_keep, qkv, probs, go, x0, g1, picked, w_qkv, gain1, weights
    )
    grad_qkv = reduce_scatter(weight_grad(a, gqkv, width, 768), 0)
    grad_img_lo, grad_img_hi = place(s, member, keep, exchange_relative(blocks))

    pieces = [
        value.reshape((devices, -1, width)) for value in (grad_out, grad_pos_lo, grad_pos_hi)
    ]
    sides = [value.reshape(devices, -1) for value in (grad_ln1, grad_ln2, grad_b1, grad_b2)]
    length = sum(side.shape[1] for side in sides)
    side_rows = -(-length // width)
    sides = jnp.pad(jnp.concatenate(sides, axis=1), ((0, 0), (0, side_rows * width - length)))
    pieces.append(sides.reshape(devices, side_rows, width))
    counts = [piece.shape[1] for piece in pieces]
    total = sum(counts)
    rest = reduce_scatter(
        jnp.concatenate([p.astype(BF16) for p in pieces], axis=1).reshape(-1, width), 1
    )
    grad_out = rest[: counts[0]]
    grad_pos_lo = rest[counts[0] : counts[0] + counts[1]]
    grad_pos_hi = rest[counts[0] + counts[1] : counts[0] + counts[1] + counts[2]]
    sides = rest[total - side_rows :].reshape(-1)
    n1 = width // devices
    nf = w_fc1.shape[1] // devices
    grad_ln1 = sides[:n1]
    grad_ln2 = sides[n1 : 2 * n1]
    grad_b1 = sides[2 * n1 : 2 * n1 + nf]
    grad_b2 = sides[2 * n1 + nf : 3 * n1 + nf]

    both = reduce_relative(
        jnp.concatenate(
            [
                grad_embed.astype(BF16).reshape(groups, features, width),
                grad_head.astype(BF16).reshape(groups, features, width),
            ],
            axis=1,
        )
    )
    grad_embed = both[:features]
    grad_head = both[features:].T
    return (
        pred_lo.reshape(cot_lo.shape),
        pred_hi.transpose(0, 2, 1),
        grad_img_lo.transpose(0, 2, 1),
        grad_img_hi.transpose(0, 2, 1),
        grad_embed,
        grad_pos_lo,
        grad_pos_hi,
        grad_ln1,
        grad_qkv,
        grad_out,
        grad_ln2,
        grad_fc1,
        grad_b1,
        grad_fc2,
        grad_b2,
        grad_head,
    )


def solution(mesh):
    placed = (
        P("dp", None, "var"),
        P("dp", None, "var"),
        P("dp", None),
        P("dp", None),
        P("dp", None),
        P("dp", None),
        P("var", None),
        P(),
        P(),
        P(),
        P(),
        P(),
        P(),
        P(),
        P(),
        P(),
        P(),
        P(None, "var"),
        P("dp", None, "var"),
        P("dp", None, "var"),
    )
    return jax.shard_map(
        body,
        mesh=mesh,
        in_specs=placed,
        out_specs=(
            P("dp", None, "var"),
            P("dp", None, "var"),
            P("dp", None, "var"),
            P("dp", None, "var"),
            P("var", None),
            P(("dp", "var"), None),
            P(("dp", "var"), None),
            P(("dp", "var")),
            P(("dp", "var"), None),
            P(("dp", "var"), None),
            P(("dp", "var")),
            P(("dp", "var"), None),
            P(("dp", "var")),
            P(("dp", "var"), None),
            P(("dp", "var")),
            P(None, "var"),
        ),
        check_vma=False,
    )
```

time: 531 us -> 339 us (0.64)
  matrix products: 165 us -> 0 us
  Pallas kernels: 0 us -> 130 us
  local copies, waits for them, and re-layouts: 163 us -> 57.2 us
  other arithmetic: 68.9 us -> 17.7 us
  waiting for transfers between devices: 85.2 us -> 90.7 us
    dot_general x38 -> x0, matrix products: 165 us -> none  [the longest x22 133 us: dot(): lax.dot_general(left, right, (dims, ((), ())), preferred_element_type=F32)]
    pallas_call x0 -> x13, Pallas kernels: none -> 130 us  [the longest x1 33.3 us: backward(): pl.pallas_call(functools.partial(backward_kernel, s, heads), grid=(rows /...]
    reshape x25 -> x3, local copies, waits for them, and re-layouts: 62.8 us -> 0.01 us  [the longest x2 0.01 us: body(): gain1, gain2 = (ln1_gain.reshape(1, -1), ln2_gain.reshape(1, -1))]
    slice x10 -> x0, local copies, waits for them, and re-layouts: 20.4 us -> none  [the longest x1 6.25 us: body(): triple_hi[:, :, 2]]
    concatenate x12 -> x1, other arithmetic: 15.5 us -> 0.98 us  [body(): own = jnp.concatenate([w_embed, w_head.T], axis=0)]
    unnamed x204 -> x178, local copies, waits for them, and re-layouts: 32.9 us -> 42.4 us
    another operation x5 -> x0, local copies, waits for them, and re-layouts: 7.75 us -> none  [the longest x2 5.98 us: attention_back(): return jnp.stack([grad_queries, grad_keys, grad_values], axis=2)]
    dynamic_slice x7, local copies, waits for them, and re-layouts: 9.44 us -> 2.91 us  [reduce_scatter(): send = lax.dynamic_index_in_dim(value, 1 - mine, axis, keepdims=False)]
  transfers between devices with their start and end apart: 41 -> 40, of which waited for: 21 -> 18; matrix products, arithmetic and copies ran while one was open for 48% -> 5% of each run, Pallas kernels for 0% -> 6%
where the time goes in v2:
time: 339 us; the launch traced here: 335 us
  Pallas kernels  130 us (38%)
  waiting for transfers between devices  90.7 us (27%)
  local copies, waits for them, and re-layouts  57.2 us (17%)
  starting transfers between devices  37.4 us (11%)
  other arithmetic  17.7 us (5%)
    ppermute x40, waiting for transfers between devices, swap(): return lax.ppermute(value, AXES, pairs)  90.7 us
    unnamed x178, local copies, waits for them, and re-layouts  42.4 us
    ppermute x40, starting transfers between devices, swap(): return lax.ppermute(value, AXES, pairs)  37.4 us
    pallas_call x1, Pallas kernels, backward(): pl.pallas_call(functools.partial(backward_kernel, s, heads), grid=(rows /...  33.3 us
    pallas_call x1, Pallas kernels, middle(): pl.pallas_call(functools.partial(middle_kernel, s), grid=(rows // ROWS,),...  32.2 us
    pallas_call x1, Pallas kernels, forward(): pl.pallas_call(functools.partial(forward_kernel, s, heads), grid=(rows //...  18.9 us
    pallas_call x1, Pallas kernels, hidden(): pl.pallas_call(functools.partial(hidden_kernel, sub), grid=(inner // colu...  18.7 us
    pallas_call x3, Pallas kernels, weight_grad(): pl.pallas_call(weight_kernel, grid=(m // tall, n // broad), in_specs=[pl....  17.5 us
  transfers between devices with their start and end apart: 40, of which 18 were waited for; matrix products, arithmetic and copies ran while one was open for 5% of the time, Pallas kernels for 6%

profile of v2, /device:TPU:0, one launch (start us, length us, event | category | flops | bytes accessed | tf_op | source)
XLA Modules:
  0.0 335.1 jit_solution(11128792516058409097)
XLA Ops:
  1.6 3.0 collective-permute-start.4
  32.7 18.9 %shard_map.318 = (f32[1024,768]{1,0:T(8,128)S(1)}, bf16[1024,768]{1,0:T(8,128)(2,1)S(1)}, bf16[1024,2304]{1,0:T(8,128)(2,1)}, f32[8,6,256,128]{3,2,1,0:T(8,128)}...) custom-call(s32[8,128]{1,0:T(8,128)S(1)} %slice_bitcast_fusion.3.keep_ref, ...), custom_call_target="tpu_custom_call" | custom-call | flops 15000000512 | bytes 30000000 | tf_op jit(solution)/shard_map/pallas_call | solution.py:284
  51.8 5.1 %copy-done.17 = bf16[3072,768]{1,0:T(8,128)(2,1)S(1)} copy-done((bf16[3072,768]{1,0:T(8,128)(2,1)S(1)}, bf16[3072,768]{1,0:T(8,128)(2,1)}, u32[]{:S(2)}) %copy-start.17) | copy-done | bytes 4718616
  56.8 18.7 %shard_map.320 = (bf16[1024,3072]{1,0:T(8,128)(2,1)}, bf16[1024,3072]{1,0:T(8,128)(2,1)}, f32[1,3072]{1,0:T(1,128)S(1)}) custom-call(bf16[1024,768]{1,0:T(8,128)(2,1)S(1)} %get-tuple-element.66.b_ref.left_ref, bf16[1024,768]{1,0:T(8,128)(2,1)S(1)} %get-tuple-element.71.gm_ref.right_ref, bf16[768,3072]{1,0:T(8,128)(2,1)S(1)} %bitcast.175, ...), custom_call_target="tpu_custom_call" | custom-call | flops 20000000000 | bytes 25000000 | tf_op jit(solution)/shard_map/pallas_call | solution.py:359
  79.8 6.2 %shard_map.326 = bf16[768,3072]{1,0:T(8,128)(2,1)S(1)} custom-call(bf16[1024,768]{1,0:T(8,128)(2,1)S(1)} %copy-done.63, bf16[1024,3072]{1,0:T(8,128)(2,1)S(1)} %copy-done.57), custom_call_target="tpu_custom_call" | custom-call | flops 4831838208 | bytes 12582912 | tf_op jit(solution)/shard_map/pallas_call | solution.py:383
  88.3 32.2 %shard_map.321 = (bf16[80,1024]{1,0:T(8,128)(2,1)S(1)}, bf16[80,1024]{1,0:T(8,128)(2,1)S(1)}, bf16[80,1024]{1,0:T(8,128)(2,1)S(1)}, bf16[80,1024]{1,0:T(8,128)(2...) custom-call(f32[8,128]{1,0:T(8,128)S(1)} %get-tuple-element.60.seen_, ...), custom_call_target="tpu_custom_call" | custom-call | flops 15000000512 | bytes 30000000 | tf_op jit(solution)/shard_map/pallas_call | solution.py:421
  124.5 33.3 %shard_map.323 = (bf16[1024,2304]{1,0:T(8,128)(2,1)}, bf16[80,1024]{1,0:T(8,128)(2,1)S(1)}, bf16[80,1024]{1,0:T(8,128)(2,1)S(1)}, bf16[80,1024]{1,0:T(8,128)(2,1...) custom-call(s32[8,128]{1,0:T(8,128)S(1)} %slice_bitcast_fusion.3.kee, ...), custom_call_target="tpu_custom_call" | custom-call | flops 15000000512 | bytes 30000000 | tf_op jit(solution)/shard_map/pallas_call | solution.py:496
  180.9 4.8 %shard_map.325 = bf16[768,2304]{1,0:T(8,128)(2,1)S(1)} custom-call(bf16[1024,768]{1,0:T(8,128)(2,1)S(1)} %copy-done.61, bf16[1024,2304]{1,0:T(8,128)(2,1)S(1)} %bitcast.182), custom_call_target="tpu_custom_call" | custom-call | flops 3623878656 | bytes 9830400 | tf_op jit(solution)/shard_map/pallas_call | solution.py:383
  189.9 5.4 %collective-permute-done.16 = bf16[1,160,768]{2,1,0:T(8,128)(2,1)S(1)} collective-permute-done((bf16[1,160,768]{2,1,0:T(8,128)(2,1)S(1)}, bf16[1,160,768]{2,1,0:T(8,128)(2,1)S(1)}, u32[]{:S(2)}, u32[]{:S(2)}) %collective-permute-start.16) | collective-permute-done | bytes 245792 | tf_op jit(solution)/shard_map/ppermute | solution.py:602
  197.0 6.5 %shard_map.327 = bf16[3072,768]{1,0:T(8,128)(2,1)S(1)} custom-call(bf16[1024,3072]{1,0:T(8,128)(2,1)S(1)} %bitcast.184, bf16[1024,768]{1,0:T(8,128)(2,1)S(1)} %copy-done.56), custom_call_target="tpu_custom_call" | custom-call | flops 4831838208 | bytes 12582912 | tf_op jit(solution)/shard_map/pallas_call | solution.py:383
  216.2 3.2 shard_map.324
  227.6 6.0 %collective-permute-done.19 = bf16[160,768]{1,0:T(8,128)(2,1)S(1)} collective-permute-done((bf16[160,768]{1,0:T(8,128)(2,1)S(1)}, bf16[160,768]{1,0:T(8,128)(2,1)S(1)}, u32[]{:S(2)}, u32[]{:S(2)}) %collective-permute-start.19) | collective-permute-done | bytes 245792 | tf_op jit(solution)/shard_map/ppermute | solution.py:602
  236.1 4.0 %collective-permute-done.23 = bf16[2,45,768]{2,0,1:T(2,128)(2,1)S(1)} collective-permute-done((bf16[2,45,768]{2,0,1:T(2,128)(2,1)S(1)}, bf16[2,45,768]{2,0,1:T(2,128)(2,1)S(1)}, u32[]{:S(2)}, u32[]{:S(2)}) %collective-permute-start.23) | collective-permute-done | bytes 138272 | tf_op jit(solution)/shard_map/ppermute | solution.py:602
  240.5 2.9 collective-permute-start.24
  251.6 14.6 %collective-permute-done.26 = bf16[2,2,2,24,2304]{4,3,0,1,2:T(8,128)(2,1)S(1)} collective-permute-done((bf16[2,2,2,24,2304]{4,3,0,1,2:T(8,128)(2,1)S(1)}, bf16[2,2,2,24,2304]{4,3,0,1,2:T(8,128)(2,1)S(1)}, u32[]{:S(2)}, u32[]{:S(2)}) %collective-permute-start.26) | collective-permute-done | bytes 884768 | tf_op jit(solution)/shard_map/ppermute | solution.py:602
  268.0 7.9 %collective-permute-done.27 = bf16[2,2,24,2304]{3,2,0,1:T(8,128)(2,1)S(1)} collective-permute-done((bf16[2,2,24,2304]{3,2,0,1:T(8,128)(2,1)S(1)}, bf16[2,2,24,2304]{3,2,0,1:T(8,128)(2,1)S(1)}, u32[]{:S(2)}, u32[]{:S(2)}) %collective-permute-start.27) | collective-permute-done | bytes 442400 | tf_op jit(solution)/shard_map/ppermute | solution.py:602
  278.6 4.4 %collective-permute-done.28 = bf16[2,24,2304]{2,1,0:T(8,128)(2,1)S(1)} collective-permute-done((bf16[2,24,2304]{2,1,0:T(8,128)(2,1)S(1)}, bf16[2,24,2304]{2,1,0:T(8,128)(2,1)S(1)}, u32[]{:S(2)}, u32[]{:S(2)}) %collective-permute-start.28) | collective-permute-done | bytes 221216 | tf_op jit(solution)/shard_map/ppermute | solution.py:602
  283.7 6.0 %collective-permute-done.36 = bf16[2,2,2,96,768]{4,3,0,1,2:T(8,128)(2,1)S(1)} collective-permute-done((bf16[2,2,2,96,768]{4,3,0,1,2:T(8,128)(2,1)S(1)}, bf16[2,2,2,96,768]{4,3,0,1,2:T(8,128)(2,1)S(1)}, u32[]{:S(2)}, u32[]{:S(2)}) %collective-permute-start.36) | collective-permute-done | bytes 1179680 | tf_op jit(solution)/shard_map/ppermute | solution.py:602
  290.6 16.0 %collective-permute-done.31 = bf16[2,2,2,24,3072]{4,3,0,1,2:T(8,128)(2,1)S(1)} collective-permute-done((bf16[2,2,2,24,3072]{4,3,0,1,2:T(8,128)(2,1)S(1)}, bf16[2,2,2,24,3072]{4,3,0,1,2:T(8,128)(2,1)S(1)}, u32[]{:S(2)}, u32[]{:S(2)}) %collective-permute-start.31) | collective-permute-done | bytes 1179680 | tf_op jit(solution)/shard_map/ppermute | solution.py:602
  309.3 3.6 %collective-permute-done.37 = bf16[2,2,96,768]{3,2,0,1:T(8,128)(2,1)S(1)} collective-permute-done((bf16[2,2,96,768]{3,2,0,1:T(8,128)(2,1)S(1)}, bf16[2,2,96,768]{3,2,0,1:T(8,128)(2,1)S(1)}, u32[]{:S(2)}, u32[]{:S(2)}) %collective-permute-start.37) | collective-permute-done | bytes 589856 | tf_op jit(solution)/shard_map/ppermute | solution.py:602
  317.8 4.9 %collective-permute-done.38 = bf16[2,96,768]{2,1,0:T(8,128)(2,1)S(1)} collective-permute-done((bf16[2,96,768]{2,1,0:T(8,128)(2,1)S(1)}, bf16[2,96,768]{2,1,0:T(8,128)(2,1)S(1)}, u32[]{:S(2)}, u32[]{:S(2)}) %collective-permute-start.38) | collective-permute-done | bytes 294944 | tf_op jit(solution)/shard_map/ppermute | solution.py:602
  322.8 3.4 %collective-permute-done.33 = bf16[2,24,3072]{2,1,0:T(8,128)(2,1)S(1)} collective-permute-done((bf16[2,24,3072]{2,1,0:T(8,128)(2,1)S(1)}, bf16[2,24,3072]{2,1,0:T(8,128)(2,1)S(1)}, u32[]{:S(2)}, u32[]{:S(2)}) %collective-permute-start.33) | collective-permute-done | bytes 294944 | tf_op jit(solution)/shard_map/ppermute | solution.py:602
  327.0 3.5 %collective-permute-done.39 = bf16[96,768]{1,0:T(8,128)(2,1)S(1)} collective-permute-done((bf16[96,768]{1,0:T(8,128)(2,1)S(1)}, bf16[96,768]{1,0:T(8,128)(2,1)S(1)}, u32[]{:S(2)}, u32[]{:S(2)}) %collective-permute-start.39) | collective-permute-done | bytes 147488 | tf_op jit(solution)/shard_map/ppermute | solution.py:602
  331.2 2.9 collective-permute-done.34
  (332 shorter events, 115.5 us)
Async XLA Ops:
  1.6 10.9 %collective-permute-start.4 = (bf16[160,768]{1,0:T(8,128)(2,1)S(1)}, bf16[160,768]{1,0:T(8,128)(2,1)S(1)}, u32[]{:S(2)}, u32[]{:S(2)}) collective-permute-start(bf16[160,768]{1,0:T(8,128)(2,1)S(1)} %pad_maximum_fusion.1.w0.h0), channel_id=1, source_target_pairs={{0,2},{1,3},{2,0},{3,1},{4,6},{5,7},{6,4},{7,5},{8,10},{9,11},{10,... | collective-permute-start | bytes 737288 | tf_op jit(solution)/shard_map/ppermute | solution.py:602
  4.6 18.7 %collective-permute-start.3 = (bf16[160,768]{1,0:T(8,128)(2,1)S(1)}, bf16[160,768]{1,0:T(8,128)(2,1)S(1)}, u32[]{:S(2)}, u32[]{:S(2)}) collective-permute-start(bf16[160,768]{1,0:T(8,128)(2,1)S(1)} %pad_maximum_fusion.1.w0.h0), channel_id=1, source_target_pairs={{0,1},{1,0},{2,3},{3,2},{4,5},{5,4},{6,7},{7,6},{8,9},{9,8},{10,11... | collective-permute-start | bytes 737288 | tf_op jit(solution)/shard_map/ppermute | solution.py:602
  12.5 10.8 %collective-permute-start.5 = (bf16[160,768]{1,0:T(8,128)(2,1)S(1)}, bf16[160,768]{1,0:T(8,128)(2,1)S(1)}, u32[]{:S(2)}, u32[]{:S(2)}) collective-permute-start(bf16[160,768]{1,0:T(8,128)(2,1)S(1)} %collective-permute-done.4.w2.h2), channel_id=1, source_target_pairs={{0,1},{1,0},{2,3},{3,2},{4,5},{5,4},{6,7},{7,6},{8,9},{9,8},{10,11... | collective-permute-start | bytes 737288 | tf_op jit(solution)/shard_map/ppermute | solution.py:602
  18.8 12.4 %collective-permute-start = (bf16[80,1024]{1,0:T(8,128)(2,1)}, bf16[80,1024]{1,0:T(8,128)(2,1)S(1)}, u32[]{:S(2)}, u32[]{:S(2)}) collective-permute-start(bf16[80,1024]{1,0:T(8,128)(2,1)} %get-tuple-element.62), channel_id=1, source_target_pairs={{0,1},{1,0},{2,3},{3,2},{4,5},{5,4},{6,7},{7,6},{8,9},{9,8},{10,11... | collective-permute-start | bytes 491528 | tf_op jit(solution)/shard_map/ppermute | solution.py:602
  19.6 11.7 %collective-permute-start.1 = (bf16[80,1024]{1,0:T(8,128)(2,1)}, bf16[80,1024]{1,0:T(8,128)(2,1)S(1)}, u32[]{:S(2)}, u32[]{:S(2)}) collective-permute-start(bf16[80,1024]{1,0:T(8,128)(2,1)} %get-tuple-element.63), channel_id=1, source_target_pairs={{0,2},{1,3},{2,0},{3,1},{4,6},{5,7},{6,4},{7,5},{8,10},{9,11},{10,... | collective-permute-start | bytes 491528 | tf_op jit(solution)/shard_map/ppermute | solution.py:602
  20.6 10.6 %collective-permute-start.2 = (bf16[80,1024]{1,0:T(8,128)(2,1)}, bf16[80,1024]{1,0:T(8,128)(2,1)}, u32[]{:S(2)}, u32[]{:S(2)}) collective-permute-start(bf16[80,1024]{1,0:T(8,128)(2,1)} %get-tuple-element.64), channel_id=1, source_target_pairs={{0,3},{1,2},{2,1},{3,0},{4,7},{5,6},{6,5},{7,4},{8,11},{9,10},{10,... | collective-permute-start | bytes 491528 | tf_op jit(solution)/shard_map/ppermute | solution.py:602
  179.1 24.5 %collective-permute-start.20 = (bf16[2,2,2,2,45,768]{5,3,4,2,1,0:T(2,128)(2,1)S(1)}, bf16[2,2,2,2,45,768]{5,3,4,2,1,0:T(2,128)(2,1)S(1)}, u32[]{:S(2)}, u32[]{:S(2)}) collective-permute-start(bf16[2,2,2,2,45,768]{5,3,4,2,1,0:T(2,128)(2,1)S(1)} %bitcast.194), channel_id=1, source_target_pairs={{0,1},{1,0},{2,3},{3,2},{4,5},{5,4},{6,7},{7,6},{8,9},{9,8},{10,11... | collective-permute-start | bytes 3317768 | tf_op jit(solution)/shard_map/ppermute | solution.py:602
  187.4 48.3 %collective-permute-start.25 = (bf16[2,2,2,2,24,2304]{5,4,0,1,2,3:T(8,128)(2,1)S(1)}, bf16[2,2,2,2,24,2304]{5,4,0,1,2,3:T(8,128)(2,1)S(1)}, u32[]{:S(2)}, u32[]{:S(2)}) collective-permute-start(bf16[2,2,2,2,24,2304]{5,4,0,1,2,3:T(8,128)(2,1)S(1)} %bitcast.193), channel_id=1, source_target_pairs={{0,1},{1,0},{2,3},{3,2},{4,5},{5,4},{6,7},{7,6},{8,9},{9,8},{10,11... | collective-permute-start | bytes 5308424 | tf_op jit(solution)/shard_map/ppermute | solution.py:602
  188.7 17.6 %collective-permute-start.12 = (bf16[80,1024]{1,0:T(8,128)(2,1)S(1)}, bf16[80,1024]{1,0:T(8,128)(2,1)S(1)}, u32[]{:S(2)}, u32[]{:S(2)}) collective-permute-start(bf16[80,1024]{1,0:T(8,128)(2,1)S(1)} %copy-done.52), channel_id=1, source_target_pairs={{0,1},{1,0},{2,3},{3,2},{4,5},{5,4},{6,7},{7,6},{8,9},{9,8},{10,11... | collective-permute-start | bytes 491528 | tf_op jit(solution)/shard_map/ppermute | solution.py:602
  188.9 19.0 %collective-permute-start.10 = (bf16[80,1024]{1,0:T(8,128)(2,1)S(1)}, bf16[80,1024]{1,0:T(8,128)(2,1)S(1)}, u32[]{:S(2)}, u32[]{:S(2)}) collective-permute-start(bf16[80,1024]{1,0:T(8,128)(2,1)S(1)} %copy-done.50), channel_id=1, source_target_pairs={{0,2},{1,3},{2,0},{3,1},{4,6},{5,7},{6,4},{7,5},{8,10},{9,11},{10,... | collective-permute-start | bytes 491528 | tf_op jit(solution)/shard_map/ppermute | solution.py:602
  209.1 10.4 %collective-permute-start.18 = (bf16[160,768]{1,0:T(8,128)(2,1)S(1)}, bf16[160,768]{1,0:T(8,128)(2,1)S(1)}, u32[]{:S(2)}, u32[]{:S(2)}) collective-permute-start(bf16[160,768]{1,0:T(8,128)(2,1)S(1)} %add_convert_fusion.2), channel_id=1, source_target_pairs={{0,8},{1,9},{2,10},{3,11},{4,12},{5,13},{6,14},{7,15},{8,0},{9,1},... | collective-permute-start | bytes 737288 | tf_op jit(solution)/shard_map/ppermute | solution.py:602
  210.7 13.6 %collective-permute-start.21 = (bf16[2,2,2,45,768]{4,2,3,1,0:T(2,128)(2,1)S(1)}, bf16[2,2,2,45,768]{4,2,3,1,0:T(2,128)(2,1)S(1)}, u32[]{:S(2)}, u32[]{:S(2)}) collective-permute-start(bf16[2,2,2,45,768]{4,2,3,1,0:T(2,128)(2,1)S(1)} %bitcast.195), channel_id=1, source_target_pairs={{0,4},{1,5},{2,6},{3,7},{4,0},{5,1},{6,2},{7,3},{8,12},{9,13},{10,... | collective-permute-start | bytes 1658888 | tf_op jit(solution)/shard_map/ppermute | solution.py:602
  213.9 35.4 %collective-permute-start.35 = (bf16[2,2,2,2,96,768]{5,4,0,1,2,3:T(8,128)(2,1)S(1)}, bf16[2,2,2,2,96,768]{5,4,0,1,2,3:T(8,128)(2,1)S(1)}, u32[]{:S(2)}, u32[]{:S(2)}) collective-permute-start(bf16[2,2,2,2,96,768]{5,4,0,1,2,3:T(8,128)(2,1)S(1)} %bitcast.192), channel_id=1, source_target_pairs={{0,1},{1,0},{2,3},{3,2},{4,5},{5,4},{6,7},{7,6},{8,9},{9,8},{10,11... | collective-permute-start | bytes 7077896 | tf_op jit(solution)/shard_map/ppermute | solution.py:602
  215.2 51.9 %collective-permute-start.30 = (bf16[2,2,2,2,24,3072]{5,4,0,1,3,2:T(8,128)(2,1)S(1)}, bf16[2,2,2,2,24,3072]{5,4,0,1,3,2:T(8,128)(2,1)S(1)}, u32[]{:S(2)}, u32[]{:S(2)}) collective-permute-start(bf16[2,2,2,2,24,3072]{5,4,0,1,3,2:T(8,128)(2,1)S(1)} %bitcast.191), channel_id=1, source_target_pairs={{0,1},{1,0},{2,3},{3,2},{4,5},{5,4},{6,7},{7,6},{8,9},{9,8},{10,11... | collective-permute-start | bytes 7077896 | tf_op jit(solution)/shard_map/ppermute | solution.py:602
  219.5 14.1 %collective-permute-start.19 = (bf16[160,768]{1,0:T(8,128)(2,1)S(1)}, bf16[160,768]{1,0:T(8,128)(2,1)S(1)}, u32[]{:S(2)}, u32[]{:S(2)}) collective-permute-start(bf16[160,768]{1,0:T(8,128)(2,1)S(1)} %add_convert_fusion.1), channel_id=1, source_target_pairs={{0,16},{1,17},{2,18},{3,19},{4,20},{5,21},{6,22},{7,23},{8,24},{9,... | collective-permute-start | bytes 737288 | tf_op jit(solution)/shard_map/ppermute | solution.py:602
  243.5 22.6 %collective-permute-start.26 = (bf16[2,2,2,24,2304]{4,3,0,1,2:T(8,128)(2,1)S(1)}, bf16[2,2,2,24,2304]{4,3,0,1,2:T(8,128)(2,1)S(1)}, u32[]{:S(2)}, u32[]{:S(2)}) collective-permute-start(bf16[2,2,2,24,2304]{4,3,0,1,2:T(8,128)(2,1)S(1)} %dynamic-slice_bitcast_fusion.2), channel_id=1, source_target_pairs={{0,2},{1,3},{2,0},{3,1},{4,6},{5,7},{6,4},{7,5},{8,10},{9,11},{10,... | collective-permute-start | bytes 2654216 | tf_op jit(solution)/shard_map/ppermute | solution.py:602
  250.1 39.5 %collective-permute-start.36 = (bf16[2,2,2,96,768]{4,3,0,1,2:T(8,128)(2,1)S(1)}, bf16[2,2,2,96,768]{4,3,0,1,2:T(8,128)(2,1)S(1)}, u32[]{:S(2)}, u32[]{:S(2)}) collective-permute-start(bf16[2,2,2,96,768]{4,3,0,1,2:T(8,128)(2,1)S(1)} %dynamic-slice_bitcast_fusion), channel_id=1, source_target_pairs={{0,2},{1,3},{2,0},{3,1},{4,6},{5,7},{6,4},{7,5},{8,10},{9,11},{10,... | collective-permute-start | bytes 3538952 | tf_op jit(solution)/shard_map/ppermute | solution.py:602
  266.4 9.4 %collective-permute-start.27 = (bf16[2,2,24,2304]{3,2,0,1:T(8,128)(2,1)S(1)}, bf16[2,2,24,2304]{3,2,0,1:T(8,128)(2,1)S(1)}, u32[]{:S(2)}, u32[]{:S(2)}) collective-permute-start(bf16[2,2,24,2304]{3,2,0,1:T(8,128)(2,1)S(1)} %dynamic-slice_bitcast_fusion.5), channel_id=1, source_target_pairs={{0,4},{1,5},{2,6},{3,7},{4,0},{5,1},{6,2},{7,3},{8,12},{9,13},{10,... | collective-permute-start | bytes 1327112 | tf_op jit(solution)/shard_map/ppermute | solution.py:602
  278.0 28.6 %collective-permute-start.31 = (bf16[2,2,2,24,3072]{4,3,0,1,2:T(8,128)(2,1)S(1)}, bf16[2,2,2,24,3072]{4,3,0,1,2:T(8,128)(2,1)S(1)}, u32[]{:S(2)}, u32[]{:S(2)}) collective-permute-start(bf16[2,2,2,24,3072]{4,3,0,1,2:T(8,128)(2,1)S(1)} %dynamic-slice_bitcast_fusion.1), channel_id=1, source_target_pairs={{0,4},{1,5},{2,6},{3,7},{4,0},{5,1},{6,2},{7,3},{8,12},{9,13},{10,... | collective-permute-start | bytes 3538952 | tf_op jit(solution)/shard_map/ppermute | solution.py:602
  283.2 25.5 %collective-permute-start.29 = (bf16[24,2304]{1,0:T(8,128)(2,1)S(1)}, bf16[24,2304]{1,0:T(8,128)(2,1)S(1)}, u32[]{:S(2)}, u32[]{:S(2)}) collective-permute-start(bf16[24,2304]{1,0:T(8,128)(2,1)S(1)} %dynamic-slice_bitcast_fusion.13), channel_id=1, source_target_pairs={{0,16},{1,17},{2,18},{3,19},{4,20},{5,21},{6,22},{7,23},{8,24},{9,... | collective-permute-start | bytes 331784 | tf_op jit(solution)/shard_map/ppermute | solution.py:602
  290.0 23.0 %collective-permute-start.37 = (bf16[2,2,96,768]{3,2,0,1:T(8,128)(2,1)S(1)}, bf16[2,2,96,768]{3,2,0,1:T(8,128)(2,1)S(1)}, u32[]{:S(2)}, u32[]{:S(2)}) collective-permute-start(bf16[2,2,96,768]{3,2,0,1:T(8,128)(2,1)S(1)} %dynamic-slice_bitcast_fusion.3), channel_id=1, source_target_pairs={{0,4},{1,5},{2,6},{3,7},{4,0},{5,1},{6,2},{7,3},{8,12},{9,13},{10,... | collective-permute-start | bytes 1769480 | tf_op jit(solution)/shard_map/ppermute | solution.py:602
  307.1 9.9 %collective-permute-start.32 = (bf16[2,2,24,3072]{3,2,0,1:T(8,128)(2,1)S(1)}, bf16[2,2,24,3072]{3,2,0,1:T(8,128)(2,1)S(1)}, u32[]{:S(2)}, u32[]{:S(2)}) collective-permute-start(bf16[2,2,24,3072]{3,2,0,1:T(8,128)(2,1)S(1)} %dynamic-slice_bitcast_fusion.4), channel_id=1, source_target_pairs={{0,2},{1,3},{2,0},{3,1},{4,6},{5,7},{6,4},{7,5},{8,10},{9,11},{10,... | collective-permute-start | bytes 1769480 | tf_op jit(solution)/shard_map/ppermute | solution.py:602
  313.2 9.5 %collective-permute-start.38 = (bf16[2,96,768]{2,1,0:T(8,128)(2,1)S(1)}, bf16[2,96,768]{2,1,0:T(8,128)(2,1)S(1)}, u32[]{:S(2)}, u32[]{:S(2)}) collective-permute-start(bf16[2,96,768]{2,1,0:T(8,128)(2,1)S(1)} %dynamic-slice_bitcast_fusion.6), channel_id=1, source_target_pairs={{0,8},{1,9},{2,10},{3,11},{4,12},{5,13},{6,14},{7,15},{8,0},{9,1},... | collective-permute-start | bytes 884744 | tf_op jit(solution)/shard_map/ppermute | solution.py:602
  317.2 9.0 %collective-permute-start.33 = (bf16[2,24,3072]{2,1,0:T(8,128)(2,1)S(1)}, bf16[2,24,3072]{2,1,0:T(8,128)(2,1)S(1)}, u32[]{:S(2)}, u32[]{:S(2)}) collective-permute-start(bf16[2,24,3072]{2,1,0:T(8,128)(2,1)S(1)} %dynamic-slice_bitcast_fusion.7), channel_id=1, source_target_pairs={{0,8},{1,9},{2,10},{3,11},{4,12},{5,13},{6,14},{7,15},{8,0},{9,1},... | collective-permute-start | bytes 884744 | tf_op jit(solution)/shard_map/ppermute | solution.py:602
  (102 other events, 1192.8 us)

commit v3 on v2

--- a/solution.py
+++ b/solution.py
@@ -163,7 +163,7 @@
             out_specs=[fixed(s.features, s.rows)] * len(members),
         ),
         out_shape=[shape((s.features, s.rows), BF16)] * len(members),
-        compiler_params=params(24),
+        compiler_params=params(60),
         cost_estimate=cost(2e9, 4e6),
     )(member, *args)
 
@@ -208,7 +208,7 @@
         ),
         out_shape=[shape((s.groups, s.tiles, LANES), jnp.int32), shape((s.tiles, LANES), F32)]
         + [shape((s.features, s.rows), BF16)] * s.groups,
-        compiler_params=params(24),
+        compiler_params=params(60),
         cost_estimate=cost(1e8, 4e6),
     )(member, *args)
 
@@ -306,7 +306,7 @@
             shape((rows, width), F32),
             shape((rows, width), BF16),
         ],
-        compiler_params=params(40),
+        compiler_params=params(60),
         cost_estimate=cost(1.5e10, 3e7),
     )(keep, seen, *picked, *weights, pos_lo, pos_hi, gain1, wqkv, gain2, wout)
 
@@ -332,7 +332,7 @@
         in_specs=[whole(seen)] + [along(s.features, ROWS)] * 4 + [whole(w) for w in weights],
         out_specs=[along(high, ROWS), across(ROWS, width), fixed(1, width)],
         out_shape=[shape((high, rows), BF16), shape((rows, width), BF16), shape((1, width), F32)],
-        compiler_params=params(16),
+        compiler_params=params(60),
         cost_estimate=cost(1e9, 4e6),
     )(seen, *cots, *weights)
 
@@ -368,7 +368,7 @@
         ],
         out_specs=[along(rows, columns), along(rows, columns), along(1, columns)],
         out_shape=[shape((rows, inner), BF16), shape((rows, inner), BF16), shape((1, inner), F32)],
-        compiler_params=params(40),
+        compiler_params=params(60),
         cost_estimate=cost(2e10, 2.5e7),
     )(b, gm, w1, b1, w2)
 
@@ -389,74 +389,185 @@
         ],
         out_specs=pl.BlockSpec((tall, broad), lambda i, j: (i, j)),
         out_shape=shape((m, n), BF16),
-        compiler_params=params(32),
+        compiler_params=params(60),
         cost_estimate=cost(2 * rows * m * n, 2 * (rows * (m + n) + m * n)),
     )(left, right)
 
 
-def middle_kernel(s, seen_ref, x1_ref, z_ref, gu_ref, gm_ref, gpred_ref, mixed_ref, w1_ref, w2_ref, b2_ref, gain2_ref, wout_ref, h0, h1, h2, h3, o0, o1, o2, o3, g1_ref, go_ref, ghead_ref, gln2_ref, gout_ref):
-    step = pl.program_id(0)
-    per = ROWS // LANES
-    first = step == 0
+def relative(ids_ref, x, y, z, c):
+    return ids_ref[0] ^ (2 * z + y), ids_ref[1] ^ (2 * x + c)
+
+
+def high_rows_kernel(far, block, ids_ref, left_ref, right_ref, o0_ref, o1_ref, acc_ref):
+    acc_ref[...] = tn(left_ref[...], right_ref[...])
+    for x in range(2):
+        for y in range(2):
+            for c, out_ref in enumerate((o0_ref, o1_ref)):
+                d, v = relative(ids_ref, x, y, 0, c)
+                start = pl.multiple_of(((d & 1) * 4 + v) * block, 8)
+                out_ref[x, y, 0] = acc_ref[pl.ds(start, block), :].astype(BF16)
+
+
+def high_rows(ids, far, left, right):
+    rows, width = right.shape
+    block = left.shape[1] // (8 * far)
+    out = pl.BlockSpec((2, 2, 1, block, width), lambda i, ids: (0, 0, i, 0, 0))
+    return pl.pallas_call(
+        functools.partial(high_rows_kernel, far, block),
+        grid_spec=pltpu.PrefetchScalarGridSpec(
+            num_scalar_prefetch=1,
+            grid=(far,),
+            in_specs=[
+                pl.BlockSpec((rows, 8 * block), lambda i, ids: (0, (ids[0] >> 1) ^ i)),
+                whole(right),
+            ],
+            out_specs=[out, out],
+            scratch_shapes=[pltpu.VMEM((8 * block, width), F32)],
+        ),
+        out_shape=[shape((2, 2, far, block, width), BF16)] * 2,
+        compiler_params=params(60),
+        cost_estimate=cost(2 * rows * left.shape[1] * width, 1.3e7),
+    )(ids, left, right)
+
+
+def spread(ids_ref, far, acc_ref, outs, block, extra=None):
+    for x in range(2):
+        for y in range(2):
+            for z in range(far):
+                for c, out_ref in enumerate(outs):
+                    d, v = relative(ids_ref, x, y, z, c)
+                    start = pl.multiple_of((d * 4 + v) * block, 8)
+                    out_ref[x, y, z, :block, :] = acc_ref[pl.ds(start, block), :].astype(BF16)
+                    if extra is not None:
+                        out_ref[x, y, z, block:, :] = extra
+
+
+def low_rows_kernel(far, block, ids_ref, left_ref, right_ref, o0_ref, o1_ref, turned_ref, acc_ref):
+    @pl.when(pl.program_id(0) == 0)
+    def _():
+        turned_ref[...] = left_ref[...].T
+
+    acc_ref[...] = nn(turned_ref[...], right_ref[...])
+    spread(ids_ref, far, acc_ref, (o0_ref, o1_ref), block)
+
+
+def low_rows(ids, far, left, right):
+    rows, width = left.shape
+    chunks = right.shape[1] // width
+    block = width // (8 * far)
+    out = pl.BlockSpec((2, 2, far, block, width), lambda i, ids: (0, 0, 0, i, 0))
+    return pl.pallas_call(
+        functools.partial(low_rows_kernel, far, block),
+        grid_spec=pltpu.PrefetchScalarGridSpec(
+            num_scalar_prefetch=1,
+            grid=(chunks,),
+            in_specs=[whole(left), pl.BlockSpec((rows, width), lambda i, ids: (0, i))],
+            out_specs=[out, out],
+            scratch_shapes=[pltpu.VMEM((width, rows), BF16), pltpu.VMEM((width, width), F32)],
+        ),
+        out_shape=[shape((2, 2, far, chunks * block, width), BF16)] * 2,
+        compiler_params=params(60),
+        cost_estimate=cost(2 * rows * width * right.shape[1], 1.3e7),
+    )(ids, left, right)
+
+
+def part_rows(width, offset):
+    return pl.BlockSpec((ROWS, width), lambda i, *_: (i + offset, 0))
+
+
+def middle_kernel(x1_ref, z_ref, gu_ref, gm_ref, w1_ref, w2_ref, b2_ref, gain2_ref, wout_ref, final_ref, ga_ref, g1_ref, go_ref, gln2_ref):
     middle = x1_ref[...]
-    final = (middle + (nn(z_ref[...], w2_ref[...]) + b2_ref[...])).astype(BF16)
-    seen = jnp.concatenate([seen_ref[pl.ds(step * per + j, 1), :] for j in range(per)], axis=1)
-    for head, out in zip((h0, h1, h2, h3), (o0, o1, o2, o3)):
-        out[...] = (nt(head[s.features :, :], final) * seen).astype(BF16)
-    accumulate(ghead_ref, first, nn(gpred_ref[...], final))
+    final_ref[...] = (middle + (nn(z_ref[...], w2_ref[...]) + b2_ref[...])).astype(BF16)
     upward = nt(gu_ref[...], w1_ref[...])
     normed, inverse = normalize(middle)
-    accumulate(gln2_ref, first, jnp.sum(upward * normed, axis=0, keepdims=True))
+    accumulate(gln2_ref, pl.program_id(0) == 0, jnp.sum(upward * normed, axis=0, keepdims=True))
     grad = gm_ref[...].astype(F32) + normalize_back(upward, normed, inverse, gain2_ref[...])
     g1_ref[...] = grad
     rounded = grad.astype(BF16)
+    ga_ref[...] = rounded
     go_ref[...] = nt(rounded, wout_ref[...]).astype(BF16)
-    accumulate(gout_ref, first, tn(mixed_ref[...], rounded))
-
-
-def middle(s, seen, x1, z, gu, gm, gpred, mixed, w1, w2, b2, gain2, wout, weights):
-    rows, width = s.rows, s.width
+
+
+def middle(part, parts, x1, z, gu, gm, w1, w2, b2, gain2, wout):
+    rows, width = x1.shape
     inner = w1.shape[1]
-    high = s.groups * s.features
-    return pl.pallas_call(
-        functools.partial(middle_kernel, s),
-        grid=(rows // ROWS,),
+    steps = rows // ROWS // parts
+    at = part * steps
+    size = steps * ROWS
+    return pl.pallas_call(
+        middle_kernel,
+        grid=(steps,),
         in_specs=[
-            whole(seen),
-            across(ROWS, width),
-            across(ROWS, inner),
-            across(ROWS, inner),
-            across(ROWS, width),
-            along(high, ROWS),
-            across(ROWS, width),
+            part_rows(width, at),
+            part_rows(inner, at),
+            part_rows(inner, at),
+            part_rows(width, at),
         ]
-        + [whole(a) for a in (w1, w2, b2, gain2, wout, *weights)],
-        out_specs=[along(s.features, ROWS)] * 4
-        + [
-            across(ROWS, width),
-            across(ROWS, width),
-            fixed(high, width),
-            fixed(1, width),
-            fixed(width, width),
+        + [whole(a) for a in (w1, w2, b2, gain2, wout)],
+        out_specs=[across(ROWS, width)] * 4 + [fixed(1, width)],
+        out_shape=[
+            shape((size, width), BF16),
+            shape((size, width), BF16),
+            shape((size, width), F32),
+            shape((size, width), BF16),
+            shape((1, width), F32),
         ],
-        out_shape=[shape((s.features, rows), BF16)] * 4
-        + [
-            shape((rows, width), F32),
-            shape((rows, width), BF16),
-            shape((high, width), F32),
-            shape((1, width), F32),
-            shape((width, width), F32),
-        ],
-        compiler_params=params(44),
-        cost_estimate=cost(1.5e10, 3e7),
-    )(seen, x1, z, gu, gm, gpred, mixed, w1, w2, b2, gain2, wout, *weights)
-
-
-def backward_kernel(s, heads, keep_ref, qkv_ref, probs_ref, go_ref, x0_ref, g1_ref, p0, p1, p2, p3, wqkv_ref, gain1_ref, w0, w1, w2, w3, gqkv_ref, o0, o1, o2, o3, gln1_ref, glo_ref, ghi_ref, gembed_ref):
-    step = pl.program_id(0)
+        compiler_params=params(60),
+        cost_estimate=cost(2e10 / parts, 3e7 / parts),
+    )(x1, z, gu, gm, w1, w2, b2, gain2, wout)
+
+
+def head_kernel(s, seen_ref, f0, f1, weights, out_refs):
+    final = jnp.concatenate([f0[...], f1[...]], axis=0)
+    seen = jnp.concatenate([seen_ref[t : t + 1, :] for t in range(s.tiles)], axis=1)
+    for head, out in zip(weights, out_refs):
+        out[...] = (nt(head[s.features :, :], final) * seen).astype(BF16)
+    return final
+
+
+def output_kernel(s, far, block, ids_ref, seen_ref, f0, f1, ga0, ga1, mixed_ref, gpred_ref, la, lb, gb1_ref, gb2_ref, h0, h1, h2, h3, p0, p1, p2, p3, o0_ref, o1_ref, n0_ref, n1_ref, acc_ref):
+    final = head_kernel(s, seen_ref, f0, f1, (h0, h1, h2, h3), (p0, p1, p2, p3))
+    ghead = nn(gpred_ref[...], final).astype(BF16)
+    for k in range(4):
+        (n0_ref, n1_ref)[k % 2][k // 2] = ghead[k * s.features : (k + 1) * s.features]
+    half = ga0.shape[0]
+    acc_ref[...] = tn(mixed_ref[:half, :], ga0[...]) + tn(mixed_ref[half:, :], ga1[...])
+    inner = gb1_ref.shape[1] // s.width
+    sides = [la[...] + lb[...], gb2_ref[...]]
+    sides += [gb1_ref[:, i * s.width : (i + 1) * s.width] for i in range(inner)]
+    sides.append(jnp.zeros((-len(sides) % 8, s.width), F32))
+    extra = jnp.concatenate(sides, axis=0).astype(BF16)
+    spread(ids_ref, far, acc_ref, (o0_ref, o1_ref), block, extra)
+
+
+def output_grads(s, ids, far, seen, finals, gas, mixed, gpred, gln2s, gb1, gb2, weights):
+    width, rows = s.width, s.rows
+    block = width // (8 * far)
+    tall = block + 8 * (-(-(2 + gb1.shape[1] // width) // 8))
+    args = [seen, *finals, *gas, mixed, gpred, *gln2s, gb1, gb2, *weights]
+    outs = (
+        [((s.features, rows), BF16)] * 4
+        + [((2, 2, far, tall, width), BF16)] * 2
+        + [((2, s.features, width), BF16)] * 2
+    )
+    return pl.pallas_call(
+        functools.partial(output_kernel, s, far, block),
+        grid_spec=pltpu.PrefetchScalarGridSpec(
+            num_scalar_prefetch=1,
+            grid=(1,),
+            in_specs=[whole(a) for a in args],
+            out_specs=[fixed(*dims) for dims, _ in outs],
+            scratch_shapes=[pltpu.VMEM((width, width), F32)],
+        ),
+        out_shape=[shape(*out) for out in outs],
+        compiler_params=params(60),
+        cost_estimate=cost(4e9, 1e7),
+    )(ids, *args)
+
+
+def backward_kernel(s, heads, qkv_ref, probs_ref, go_ref, x0_ref, g1_ref, wqkv_ref, gain1_ref, gqkv_ref, g0_ref, gln1_ref):
     per = ROWS // LANES
     width = s.width
-    first = step == 0
     masks = pair_masks()
     scale = 1.0 / math.sqrt(width // heads)
     for j in range(per):
@@ -477,54 +588,135 @@
             gqkv_ref[rows, 2 * width + at : 2 * width + at + LANES] = tn(probs.astype(BF16), out).astype(BF16)
     upward = nt(gqkv_ref[...], wqkv_ref[...])
     normed, inverse = normalize(x0_ref[...])
-    accumulate(gln1_ref, first, jnp.sum(upward * normed, axis=0, keepdims=True))
-    grad = (g1_ref[...] + normalize_back(upward, normed, inverse, gain1_ref[...])).astype(BF16)
-    for weight, out in zip((w0, w1, w2, w3), (o0, o1, o2, o3)):
-        out[...] = nt(weight[: s.features, :], grad).astype(BF16)
-    hot_hi = jnp.concatenate([chosen_rows(s, keep_ref, step * per + j, s.hi_patches, True) for j in range(per)], axis=1)
-    hot_lo = jnp.concatenate([chosen_rows(s, keep_ref, step * per + j, s.lo_patches, False) for j in range(per)], axis=1)
-    accumulate(ghi_ref, first, nn(hot_hi, grad))
-    accumulate(glo_ref, first, nn(hot_lo, grad))
-    picked = jnp.concatenate([p[...] for p in (p0, p1, p2, p3)], axis=0)
-    accumulate(gembed_ref, first, nn(picked, grad))
-
-
-def backward(s, heads, keep, qkv, probs, go, x0, g1, picked, wqkv, gain1, weights):
+    accumulate(gln1_ref, pl.program_id(0) == 0, jnp.sum(upward * normed, axis=0, keepdims=True))
+    g0_ref[...] = (g1_ref[...] + normalize_back(upward, normed, inverse, gain1_ref[...])).astype(BF16)
+
+
+def backward(s, heads, part, parts, qkv, probs, go, x0, g1, wqkv, gain1):
     rows, width = s.rows, s.width
     per, pairs = ROWS // LANES, width // LANES
-    high = s.groups * s.features
+    steps = rows // ROWS // parts
+    at = part * steps
+    size = steps * ROWS
     return pl.pallas_call(
         functools.partial(backward_kernel, s, heads),
-        grid=(rows // ROWS,),
+        grid=(steps,),
         in_specs=[
-            whole(keep),
-            across(ROWS, 3 * width),
-            pl.BlockSpec((per, pairs, 2 * LANES, LANES), lambda i: (i, 0, 0, 0)),
+            part_rows(3 * width, at),
+            pl.BlockSpec((per, pairs, 2 * LANES, LANES), lambda i: (i + at, 0, 0, 0)),
             across(ROWS, width),
+            part_rows(width, at),
             across(ROWS, width),
-            across(ROWS, width),
-        ]
-        + [along(s.features, ROWS)] * 4
-        + [whole(a) for a in (wqkv, gain1, *weights)],
-        out_specs=[across(ROWS, 3 * width)]
-        + [along(s.features, ROWS)] * 4
-        + [
-            fixed(1, width),
-            fixed(s.lo_patches, width),
-            fixed(s.hi_patches, width),
-            fixed(high, width),
+            whole(wqkv),
+            whole(gain1),
         ],
-        out_shape=[shape((rows, 3 * width), BF16)]
-        + [shape((s.features, rows), BF16)] * 4
-        + [
-            shape((1, width), F32),
-            shape((s.lo_patches, width), F32),
-            shape((s.hi_patches, width), F32),
-            shape((high, width), F32),
-        ],
-        compiler_params=params(44),
-        cost_estimate=cost(1.5e10, 3e7),
-    )(keep, qkv, probs, go, x0, g1, *picked, wqkv, gain1, *weights)
+        out_specs=[across(ROWS, 3 * width), across(ROWS, width), fixed(1, width)],
+        out_shape=[shape((size, 3 * width), BF16), shape((size, width), BF16), shape((1, width), F32)],
+        compiler_params=params(60),
+        cost_estimate=cost(2.5e10 / parts, 3e7 / parts),
+    )(qkv, probs, go, x0, g1, wqkv, gain1)
+
+
+def image_kernel(s, keep_ref, a_ref, b_ref, w0, w1, w2, w3, o0, o1, o2, o3):
+    half = a_ref.shape[0]
+    for weight, out in zip((w0, w1, w2, w3), (o0, o1, o2, o3)):
+        out[:, :half] = nt(weight[: s.features, :], a_ref[...]).astype(BF16)
+        out[:, half:] = nt(weight[: s.features, :], b_ref[...]).astype(BF16)
+
+
+def image_grads(s, keep, g0s, weights):
+    args = [keep, *g0s, *weights]
+    return pl.pallas_call(
+        functools.partial(image_kernel, s),
+        grid=(1,),
+        in_specs=[whole(a) for a in args],
+        out_specs=[fixed(s.features, s.rows)] * 4,
+        out_shape=[shape((s.features, s.rows), BF16)] * 4,
+        compiler_params=params(60),
+        cost_estimate=cost(1e9, 3e6),
+    )(*args)
+
+
+def position_grads(s, keep_ref, g0, picked):
+    hot_hi, hot_lo = [], []
+    for t in range(s.tiles):
+        row = keep_ref[t : t + 1, :]
+        patches = s.hi_patches if t < s.hi_each else s.lo_patches
+        hot = jnp.where(iota((patches, LANES), 0) == row, 1.0, 0.0).astype(BF16)
+        (hot_hi if t < s.hi_each else hot_lo).append(hot)
+    hi_rows = s.hi_each * LANES
+    hi = nn(jnp.concatenate(hot_hi, axis=1), g0[:hi_rows])
+    lo = nn(jnp.concatenate(hot_lo, axis=1), g0[hi_rows:])
+    return lo, hi, nn(jnp.concatenate(picked, axis=0), g0)
+
+
+def first_kernel(s, far, block, chunks, ids_ref, keep_ref, a_ref, r0_ref, r1_ref, g0a, g0b, la, lb, p0, p1, p2, p3, o0_ref, o1_ref, e0_ref, e1_ref, turned_ref, acc_ref, lo_ref, hi_ref):
+    step = pl.program_id(0)
+    half = r0_ref.shape[0]
+    width = s.width
+    outs = (o0_ref, o1_ref)
+
+    @pl.when(step == 0)
+    def _():
+        turned_ref[...] = a_ref[...].T
+
+    @pl.when(step < chunks)
+    def _():
+        acc_ref[...] = nn(turned_ref[:, :half], r0_ref[...]) + nn(turned_ref[:, half:], r1_ref[...])
+        spread(ids_ref, far, acc_ref, outs, block)
+
+    @pl.when(step == chunks)
+    def _():
+        g0 = jnp.concatenate([g0a[...], g0b[...]], axis=0)
+        lo, hi, embed = position_grads(s, keep_ref, g0, [p[...] for p in (p0, p1, p2, p3)])
+        lo_ref[...] = lo
+        hi_ref[...] = hi
+        embed = embed.astype(BF16)
+        for k in range(4):
+            (e0_ref, e1_ref)[k % 2][k // 2] = embed[k * s.features : (k + 1) * s.features]
+        hi_block = s.hi_patches // (8 * far)
+        lo_block = s.lo_patches // (8 * far)
+        gln1 = la[...] + lb[...]
+        pad = jnp.zeros((block - hi_block - lo_block - 1, width), F32)
+        for x in range(2):
+            for y in range(2):
+                for z in range(far):
+                    for c in range(2):
+                        d, v = relative(ids_ref, x, y, z, c)
+                        at = d * 4 + v
+                        mine = hi_ref[pl.ds(pl.multiple_of(at * hi_block, 8), hi_block), :]
+                        both = lo_ref[pl.ds(pl.multiple_of((at >> 1) * 8, 8), 8), :]
+                        less = jnp.where((at & 1) == 1, both[lo_block:], both[:lo_block])
+                        outs[c][x, y, z] = jnp.concatenate([mine, less, gln1, pad], axis=0).astype(BF16)
+
+
+def first_grads(s, ids, far, keep, a, gqkvs, g0s, gln1s, picked):
+    width, rows = s.width, s.rows
+    block = width // (8 * far)
+    chunks = gqkvs[0].shape[1] // width
+    half = gqkvs[0].shape[0]
+    out = pl.BlockSpec((2, 2, far, block, width), lambda i, ids: (0, 0, 0, i, 0))
+    right = pl.BlockSpec((half, width), lambda i, ids: (0, jnp.minimum(i, chunks - 1)))
+    rest = [*g0s, *gln1s, *picked]
+    return pl.pallas_call(
+        functools.partial(first_kernel, s, far, block, chunks),
+        grid_spec=pltpu.PrefetchScalarGridSpec(
+            num_scalar_prefetch=1,
+            grid=(chunks + 1,),
+            in_specs=[whole(keep), whole(a), right, right] + [whole(r) for r in rest],
+            out_specs=[out, out, fixed(2, s.features, width), fixed(2, s.features, width)],
+            scratch_shapes=[
+                pltpu.VMEM((width, rows), BF16),
+                pltpu.VMEM((width, width), F32),
+                pltpu.VMEM((s.lo_patches, width), F32),
+                pltpu.VMEM((s.hi_patches, width), F32),
+            ],
+        ),
+        out_shape=[shape((2, 2, far, (chunks + 1) * block, width), BF16)] * 2
+        + [shape((2, s.features, width), BF16)] * 2,
+        compiler_params=params(60),
+        cost_estimate=cost(7e9, 1.2e7),
+    )(ids, keep, a, *gqkvs, *rest)
 
 
 def place_kernel(s, member_ref, keep_ref, r0, r1, r2, r3, lo_ref, hi_ref):
@@ -558,7 +750,7 @@
             shape((lo, s.features, s.lo_patches), BF16),
             shape((hi, s.features, s.hi_patches), BF16),
         ],
-        compiler_params=params(24),
+        compiler_params=params(60),
         cost_estimate=cost(2e9, 4e6),
     )(member, keep, *blocks)
 
@@ -589,7 +781,7 @@
             out_specs=[fixed(lo, s.features), fixed(hi, s.features, s.hi_length)],
         ),
         out_shape=[shape((lo, s.features), BF16), shape((hi, s.features, s.hi_length), BF16)],
-        compiler_params=params(16),
+        compiler_params=params(60),
         cost_estimate=cost(1e8, 3e6),
     )(member, *blocks)
 
@@ -606,48 +798,111 @@
     return (left.astype(F32) + right.astype(F32)).astype(BF16)
 
 
-def stages(order):
-    dp, var = lax.axis_size("dp"), lax.axis_size("var")
-    data = [("d", 1 << i) for i in range(dp.bit_length() - 1)]
-    core = [("v", 1 << i) for i in range(var.bit_length() - 1)]
-    if order == 0:
-        return core + data
-    return core[:1] + data[:1] + core[1:] + data[1:]
-
-
-def reduce_scatter(full, order):
-    dp, var = lax.axis_size("dp"), lax.axis_size("var")
-    places = [("d", 1 << i) for i in reversed(range(dp.bit_length() - 1))]
-    places += [("v", 1 << i) for i in reversed(range(var.bit_length() - 1))]
-    rows = full.shape[0] // (dp * var)
-    value = full.astype(BF16).reshape((2,) * len(places) + (rows,) + full.shape[1:])
-    d, v = lax.axis_index("dp"), lax.axis_index("var")
-    for stage_of in stages(order):
-        axis = places.index(stage_of)
-        kind, bit = stage_of
-        mine = ((d if kind == "d" else v) // bit) % 2
-        keep = lax.dynamic_index_in_dim(value, mine, axis, keepdims=False)
-        send = lax.dynamic_index_in_dim(value, 1 - mine, axis, keepdims=False)
-        got = swap(send, bit if kind == "d" else 0, bit if kind == "v" else 0)
-        value = add_rounded(keep, got)
-        places.remove(stage_of)
-    return value.astype(F32)
-
-
-def reduce_relative(blocks):
-    var, dp = lax.axis_size("var"), lax.axis_size("dp")
-    value = blocks
+def added(*values):
+    values = [value.astype(F32) for value in values]
+    while len(values) > 1:
+        values = [values[i] + values[i + 1] for i in range(0, len(values), 2)]
+    return values[0]
+
+
+def tie(value, *tokens):
+    return lax.optimization_barrier((value, tokens))[0]
+
+
+PARTNERS = {"core": (0, 1), "x": (0, 2), "y": (1, 0), "z0": (2, 0), "z1": (4, 0)}
+
+
+class Chain:
+    def __init__(self, near, sent):
+        self.near, self.sent = near, sent
+        self.repeats = near.ndim == 3
+        self.names = ["x"] if self.repeats else ["x", "y", "z1", "z0"]
+        self.held = self.got = None
+
+    def outgoing(self, name):
+        if name == "core":
+            self.held = self.near
+            return self.sent
+        if name not in self.names:
+            self.held = add_rounded(self.held, self.got)
+            return self.held
+        axis = self.names.index(name)
+        self.names.remove(name)
+        kept, sent = (
+            [lax.index_in_dim(value, side, axis, keepdims=False) for value in (self.held, self.got)]
+            for side in range(2)
+        )
+        self.held = add_rounded(*kept)
+        return add_rounded(*sent)
+
+    def hold(self, *tokens):
+        self.held, self.got = tie((self.held, self.got), *tokens)
+
+    def final(self):
+        return added(self.held, self.got) if self.got is not None else added(*self.fanned)
+
+
+def send_rows(values, bits):
+    if len(values) == 1:
+        return [swap(values[0], *bits)]
+    width = values[0].shape[-1]
+    flat = [value.reshape(-1, width) for value in values]
+    got = swap(jnp.concatenate(flat, axis=0), *bits)
+    out, start = [], 0
+    for value, rows in zip(values, flat):
+        out.append(got[start : start + rows.shape[0]].reshape(value.shape))
+        start += rows.shape[0]
+    return out
+
+
+def trade(name, *chains):
+    got = send_rows([chain.outgoing(name) for chain in chains], PARTNERS[name])
+    for chain, value in zip(chains, got):
+        chain.got = value
+    return got[0]
+
+
+def trade_line(*chains):
+    values = [add_rounded(chain.held, chain.got) for chain in chains]
+    split = [
+        [value] * 4 if chain.repeats else list(value.reshape((4,) + value.shape[2:]))
+        for chain, value in zip(chains, values)
+    ]
+    for chain, value in zip(chains, split):
+        chain.fanned, chain.got = [value[0]], None
+    for z in range(1, 4):
+        for chain, got in zip(chains, send_rows([value[z] for value in split], (2 * z, 0))):
+            chain.fanned.append(got)
+    return chains[0].fanned[1:]
+
+
+def natural(near, sent):
+    both = jnp.stack([near, sent]).transpose(3, 2, 1, 0, 4, 5)
+    return both.reshape((-1,) + near.shape[3:])
+
+
+def scattered(full):
+    return lax.psum_scatter(full, AXES, scatter_dimension=0, tiled=True).astype(F32)
+
+
+def joined(blocks, chunks):
+    count, rows, width = blocks.shape
+    split = blocks.reshape(count, chunks, rows // chunks, width).transpose(0, 2, 1, 3)
+    return split.reshape(count * (rows // chunks), chunks * width)
+
+
+def plain_sum(near, sent):
+    if near.ndim == 6:
+        near, sent = (value.reshape((2, 2, 4) + value.shape[4:]) for value in (near, sent))
+        return natural(near, sent)
+    value = jnp.stack([near, sent], axis=1)
+    value = value.reshape((-1,) + value.shape[2:])
     bit = 1
-    while bit < var:
+    while value.shape[0] > 1:
         value = value.reshape((value.shape[0] // 2, 2) + value.shape[1:])
         value = add_rounded(value[:, 0], swap(value[:, 1], 0, bit))
         bit *= 2
-    value = value[0]
-    bit = 1
-    while bit < dp:
-        value = add_rounded(value, swap(value, bit, 0))
-        bit *= 2
-    return value.astype(F32)
+    return lax.psum(value[0], "dp").astype(F32)
 
 
 def exchange_relative(blocks):
@@ -692,7 +947,7 @@
     picked = [*pick(s, (0,), member, keep_lo, keep_hi, img_lo_t, img_hi_t), *picked]
     keep, seen, *cots = stage(
         s,
-        member,
+        tie(member, sent[0]),
         keep_lo,
         keep_hi,
         mask_lo,
@@ -705,68 +960,153 @@
     x0, a, qkv, probs, mixed, x1, b = forward(
         s, HEADS, own_keep, seen, picked, weights, pos_lo, pos_hi, gain1, w_qkv, gain2, w_out
     )
-    gpred, gm, grad_b2 = upstream(s, seen, cots, weights)
+    gpred, gm, grad_b2 = upstream(s, tie(seen, b), cots, weights)
     z, gu, grad_b1 = hidden(b, gm, w_fc1, b_fc1.reshape(1, -1), w_fc2)
-    grad_fc2 = reduce_scatter(weight_grad(z, gm, 768, width), 0)
-    grad_fc1 = reduce_scatter(weight_grad(b, gu, width, 1024), 1)
-    *preds, g1, go, grad_head, grad_ln2, grad_out = middle(
+    far = 4
+    cube = lax.axis_size("dp") == 2 * far
+    place_of = lax.axis_index("dp") * groups + lax.axis_index("var")
+    ids = jnp.stack([lax.axis_index("dp"), lax.axis_index("var")]).astype(jnp.int32)
+    if not cube:
+        ids = jnp.zeros_like(ids)
+
+    def chain_of(near, sent):
+        if near.ndim == 5:
+            near, sent = (
+                value.reshape((2, 2, 2, 2) + value.shape[3:]) for value in (near, sent)
+            )
+        return Chain(near, sent)
+
+    def step(name, *chains):
+        return trade(name, *chains) if cube else ()
+
+    def halves_of(chain):
+        out = []
+        for side in range(2):
+            piece = Chain(chain.near, chain.sent)
+            rows = chain.near.shape[4] // 2
+            piece.held, piece.got = (
+                lax.slice_in_dim(value, side * rows, (side + 1) * rows, axis=4)
+                for value in (chain.held, chain.got)
+            )
+            out.append(piece)
+        return out
+
+    bias2 = b_fc2.reshape(1, -1)
+
+    def middle_part(part, *tokens):
+        return middle(part, 2, x1, z, gu, gm, w_fc1, w_fc2, tie(bias2, *tokens), gain2, w_out)
+
+    two = chain_of(*high_rows(ids, far, z, gm))
+    token = step("core", two)
+    one = chain_of(*low_rows(tie(ids, two.near), far, b, gu))
+    halves = [middle_part(0, token, one.near)]
+    two_x = step("x", two)
+    halves.append(middle_part(1, step("core", one), halves[0][0]))
+    one_y = step("y", one)
+    finals, gas, g1s, gos, gln2s = zip(*halves)
+    *preds, near, sent, near_head, sent_head = output_grads(
         s,
+        tie(ids, two_x, *finals),
+        far,
         seen,
-        x1,
-        z,
-        gu,
-        gm,
+        finals,
+        gas,
+        mixed,
         gpred,
-        mixed,
-        w_fc1,
-        w_fc2,
-        b_fc2.reshape(1, -1),
-        gain2,
-        w_out,
+        gln2s,
+        grad_b1,
+        grad_b2,
         weights,
     )
-    pred_lo, pred_hi = predict(s, member, exchange_relative(preds))
-    gqkv, *blocks, grad_ln1, grad_pos_lo, grad_pos_hi, grad_embed = backward(
-        s, HEADS, own_keep, qkv, probs, go, x0, g1, picked, w_qkv, gain1, weights
+    out, head = chain_of(near, sent), chain_of(near_head, sent_head)
+
+    def backward_part(part, *tokens):
+        return backward(
+            s, HEADS, part, 2, qkv, probs, gos[part], x0, g1s[part], w_qkv, tie(gain1, *tokens)
+        )
+
+    tokens = [step("y", two), step("core", out), step("core", head)]
+    halves = [backward_part(0, near, one_y)]
+    tokens += [step("x", one)]
+    tokens += exchange_relative(preds)
+    got_preds = tokens[-groups:]
+    halves.append(backward_part(1, halves[0][0], *tokens))
+    tokens = [step("z0", two), step("x", out, head), step("z0", one)]
+    gqkvs, g0s, gln1s = zip(*halves)
+    near, sent, near_embed, sent_embed = first_grads(
+        s, tie(ids, *tokens), far, own_keep, a, gqkvs, g0s, gln1s, picked
     )
-    grad_qkv = reduce_scatter(weight_grad(a, gqkv, width, 768), 0)
+    first, embed = chain_of(near, sent), chain_of(near_embed, sent_embed)
+    tokens = [step("core", first), step("core", embed)]
+    blocks = image_grads(s, tie(own_keep, near), g0s, weights)
+    pred_lo, pred_hi = predict(s, tie(member, blocks[0]), got_preds)
+    if cube:
+        for chain in (out, head, two, one):
+            chain.hold(*tokens)
+        one_half, other_half = halves_of(first)
+        tokens = [trade("x", one_half), trade("y", other_half), trade("z0", embed)]
+        early = [trade("y", out, head), trade("z1", two), trade("z1", one)]
+        for chain in (out, head):
+            chain.hold(*tokens)
+        for chain in (one_half, other_half, embed):
+            chain.hold(*early)
+        tokens = [trade("y", one_half), trade("x", other_half), trade("z1", embed)]
+        early = [trade("z0", out, head)]
+        for chain in (out, head):
+            chain.hold(*tokens)
+        for chain in (one_half, other_half, embed):
+            chain.hold(*early)
+        blocks = [tie(block_of, *tokens) for block_of in blocks]
+        trade("x", embed)
+        trade("z1", out, head)
+        trade_line(one_half, other_half)
+        trade("y", embed)
+        grad_fc2, grad_fc1, rest, grad_head, grad_embed = (
+            chain.final() for chain in (two, one, out, head, embed)
+        )
+        first = jnp.concatenate([one_half.final(), other_half.final()], axis=0)
+    else:
+        grad_fc2, grad_fc1, rest, grad_head, grad_embed, first = (
+            plain_sum(chain.near, chain.sent) for chain in (two, one, out, head, embed, first)
+        )
     grad_img_lo, grad_img_hi = place(s, member, keep, exchange_relative(blocks))
-
-    pieces = [
-        value.reshape((devices, -1, width)) for value in (grad_out, grad_pos_lo, grad_pos_hi)
-    ]
-    sides = [value.reshape(devices, -1) for value in (grad_ln1, grad_ln2, grad_b1, grad_b2)]
-    length = sum(side.shape[1] for side in sides)
-    side_rows = -(-length // width)
-    sides = jnp.pad(jnp.concatenate(sides, axis=1), ((0, 0), (0, side_rows * width - length)))
-    pieces.append(sides.reshape(devices, side_rows, width))
-    counts = [piece.shape[1] for piece in pieces]
-    total = sum(counts)
-    rest = reduce_scatter(
-        jnp.concatenate([p.astype(BF16) for p in pieces], axis=1).reshape(-1, width), 1
+    grad_head = grad_head.T
+
+    block = width // devices
+    inner = w_fc1.shape[1] // width
+
+    hi_block = s.hi_patches // devices
+    lo_block = s.lo_patches // devices
+
+    def own_part(row):
+        return lax.dynamic_slice_in_dim(row, place_of * block, block)
+
+    if cube:
+        grad_fc1 = joined(grad_fc1[None], inner)
+        grad_qkv = joined(first[None, : 3 * block], 3)
+        grad_out, sides = rest[:block], rest[block:]
+        extra = first[3 * block :]
+        grad_pos_hi = extra[:hi_block]
+        grad_pos_lo = extra[hi_block : hi_block + lo_block]
+        first_side = extra[hi_block + lo_block]
+    else:
+        tall = width // 32
+        hi_tall, lo_tall = s.hi_patches // 32, s.lo_patches // 32
+        grad_fc2 = scattered(grad_fc2.reshape(-1, width))
+        grad_fc1 = scattered(joined(grad_fc1, inner))
+        grad_qkv = scattered(joined(first[:, : 3 * tall], 3))
+        grad_out, sides = scattered(rest[:, :tall].reshape(-1, width)), rest[0, tall:]
+        extra = first[:, 3 * tall :]
+        grad_pos_hi = scattered(extra[:, :hi_tall].reshape(-1, width))
+        grad_pos_lo = scattered(extra[:, hi_tall : hi_tall + lo_tall].reshape(-1, width))
+        sides = lax.psum(jnp.concatenate([sides, extra[0, hi_tall + lo_tall :]]), AXES).astype(F32)
+        first_side = sides[rest.shape[1] - tall]
+    grad_ln1 = own_part(first_side)
+    grad_ln2 = own_part(sides[0])
+    grad_b2 = own_part(sides[1])
+    grad_b1 = lax.dynamic_slice_in_dim(
+        sides[2 : 2 + inner].reshape(-1), place_of * inner * block, inner * block
     )
-    grad_out = rest[: counts[0]]
-    grad_pos_lo = rest[counts[0] : counts[0] + counts[1]]
-    grad_pos_hi = rest[counts[0] + counts[1] : counts[0] + counts[1] + counts[2]]
-    sides = rest[total - side_rows :].reshape(-1)
-    n1 = width // devices
-    nf = w_fc1.shape[1] // devices
-    grad_ln1 = sides[:n1]
-    grad_ln2 = sides[n1 : 2 * n1]
-    grad_b1 = sides[2 * n1 : 2 * n1 + nf]
-    grad_b2 = sides[2 * n1 + nf : 3 * n1 + nf]
-
-    both = reduce_relative(
-        jnp.concatenate(
-            [
-                grad_embed.astype(BF16).reshape(groups, features, width),
-                grad_head.astype(BF16).reshape(groups, features, width),
-            ],
-            axis=1,
-        )
-    )
-    grad_embed = both[:features]
-    grad_head = both[features:].T
     return (
         pred_lo.reshape(cot_lo.shape),
         pred_hi.transpose(0, 2, 1),

time: 339 us -> 295 us (0.87)
  waiting for transfers between devices: 90.7 us -> 40.3 us
  local copies, waits for them, and re-layouts: 57.2 us -> 20.7 us
  Pallas kernels: 130 us -> 165 us
  starting transfers between devices: 37.4 us -> 42.4 us
  other arithmetic: 17.7 us -> 21.3 us
    ppermute x40 -> x44, waiting for transfers between devices: 90.7 us -> 40.3 us  [swap(): return lax.ppermute(value, AXES, pairs)]
    unnamed x178 -> x104, local copies, waits for them, and re-layouts: 42.4 us -> 10.6 us
    pallas_call x5 -> x9, Pallas kernels: 83 us -> 104 us  [the longest x2 30.7 us: backward(): pl.pallas_call(functools.partial(backward_kernel, s, heads), grid=(steps,...]
    convert_element_type x19 -> x32, other arithmetic: 6.12 us -> 17.2 us  [add_rounded(): return (left.astype(F32) + right.astype(F32)).astype(BF16)]
    convert_element_type x10 -> x0, other arithmetic: 5.92 us -> none  [the longest x3 3.55 us: body(): p.astype(BF16)]
    ppermute x40 -> x44, starting transfers between devices: 37.4 us -> 42.4 us  [swap(): return lax.ppermute(value, AXES, pairs)]
    pallas_call x2, Pallas kernels: 1.99 us -> 6.19 us  [pick(): pl.pallas_call(functools.partial(pick_kernel, s, members), grid_spec=pltp...]
  transfers between devices with their start and end apart: 40 -> 44, of which waited for: 18 -> 10; matrix products, arithmetic and copies ran while one was open for 5% -> 11% of each run, Pallas kernels for 6% -> 40%
where the time goes in v3:
time: 295 us; the launch traced here: 292 us
  Pallas kernels  165 us (56%)
  starting transfers between devices  42.4 us (14%)
  waiting for transfers between devices  40.3 us (14%)
  other arithmetic  21.3 us (7%)
  local copies, waits for them, and re-layouts  20.7 us (7%)
    ppermute x44, starting transfers between devices, swap(): return lax.ppermute(value, AXES, pairs)  42.4 us
    ppermute x44, waiting for transfers between devices, swap(): return lax.ppermute(value, AXES, pairs)  40.3 us
    pallas_call x2, Pallas kernels, backward(): pl.pallas_call(functools.partial(backward_kernel, s, heads), grid=(steps,...  30.7 us
    pallas_call x2, Pallas kernels, middle(): pl.pallas_call(middle_kernel, grid=(steps,), in_specs=[part_rows(width, a...  27.3 us
    pallas_call x1, Pallas kernels, hidden(): pl.pallas_call(functools.partial(hidden_kernel, sub), grid=(inner // colu...  21.1 us
    pallas_call x1, Pallas kernels, forward(): pl.pallas_call(functools.partial(forward_kernel, s, heads), grid=(rows //...  20.7 us
    convert_element_type x32, other arithmetic, add_rounded(): return (left.astype(F32) + right.astype(F32)).astype(BF16)  17.2 us
    pallas_call x1, Pallas kernels, first_grads(): pl.pallas_call(functools.partial(first_kernel, s, far, block, chunks), gr...  11.6 us
  transfers between devices with their start and end apart: 44, of which 10 were waited for; matrix products, arithmetic and copies ran while one was open for 11% of the time, Pallas kernels for 40%

profile of v3, /device:TPU:0, one launch (start us, length us, event | category | flops | bytes accessed | tf_op | source)
XLA Modules:
  0.0 291.6 jit_solution(11504579645824333079)
XLA Ops:
  1.6 3.0 %collective-permute-start.4 = (bf16[160,768]{1,0:T(8,128)(2,1)S(1)}, bf16[160,768]{1,0:T(8,128)(2,1)S(1)}, u32[]{:S(2)}, u32[]{:S(2)}) collective-permute-start(bf16[160,768]{1,0:T(8,128)(2,1)S(1)} %pad_maximum_fusion.2.w0.h0), channel_id=1, source_target_pairs={{0,2},{1,3},{2,0},{3,1},{4,6},{5,7},{6,4},{7,5},{8,10},{9,11},{10,... | collective-permute-start | bytes 737288 | tf_op jit(solution)/shard_map/ppermute | solution.py:794
  6.1 3.3 %shard_map.315 = (bf16[80,1024]{1,0:T(8,128)(2,1)}, bf16[80,1024]{1,0:T(8,128)(2,1)}, bf16[80,1024]{1,0:T(8,128)(2,1)}) custom-call(s32[1]{0:T(128)} %bitcast.member_ref, s32[40,32]{1,0:T(8,128)} %copy.53.keep_lo_ref, s32[20,128]{1,0:T(8,128)} %keep_hi_ref.5, bf16[40,80,128]{2,1,0:T(8,128)(2,1)} %bitcast.224, bf16[20,80,512]{2,1,0:T(8,128)(2,1)} %bitcast.222), custom_call_target="tpu_custom_call" | custom-call | flops 2000000000 | bytes 4000000 | tf_op jit(solution)/shard_map/pallas_call | solution.py:157
  17.8 2.9 shard_map.317.p0
  23.6 20.7 %shard_map.318 = (f32[1024,768]{1,0:T(8,128)}, bf16[1024,768]{1,0:T(8,128)(2,1)}, bf16[1024,2304]{1,0:T(8,128)(2,1)}, f32[8,6,256,128]{3,2,1,0:T(8,128)}, bf16[1...) custom-call(s32[8,128]{1,0:T(8,128)} %slice_bitcast_fusion.17.keep_ref, ...), custom_call_target="tpu_custom_call" | custom-call | flops 15000000512 | bytes 30000000 | tf_op jit(solution)/shard_map/pallas_call | solution.py:284
  45.1 4.7 %shard_map.319 = (bf16[320,1024]{1,0:T(8,128)(2,1)}, bf16[1024,768]{1,0:T(8,128)(2,1)}, f32[1,768]{1,0:T(1,128)}) custom-call(f32[8,128]{1,0:T(8,128)} %get-tuple-element.127.seen_ref, bf16[80,1024]{1,0:T(8,128)(2,1)} %get-tuple-element.128.c0, bf16[80,1024]{1,0:T(8,128)(2,1)} %copy-done.47, bf16[80,1024]{1,0:T(8,128)(2,1)} %copy-done.48, ...), custom_call_target="tpu_custom_call" | custom-call | flops 1000000000 | bytes 4000000 | tf_op jit(solution)/shard_map/pallas_call | solution.py:329
  49.8 21.1 %shard_map.320 = (bf16[1024,3072]{1,0:T(8,128)(2,1)}, bf16[1024,3072]{1,0:T(8,128)(2,1)}, f32[1,3072]{1,0:T(1,128)}) custom-call(bf16[1024,768]{1,0:T(8,128)(2,1)} %get-tuple-element.126.b_ref.left_ref, bf16[1024,768]{1,0:T(8,128)(2,1)} %get-tuple-element.132.gm_ref.right_ref, bf16[768,3072]{1,0:T(8,128)(2,1)} %w1_ref.5, f32[1,3072]{1,0:T(1,128)} %bitcast.228, ...), custom_call_target="tpu_custom_call" | custom-call | flops 20000000000 | bytes 25000000 | tf_op jit(solution)/shard_map/pallas_call | solution.py:359
  70.9 10.6 %shard_map.322 = (bf16[2,2,4,96,768]{4,3,2,1,0:T(8,128)(2,1)}, bf16[2,2,4,96,768]{4,3,2,1,0:T(8,128)(2,1)}) custom-call(s32[2]{0:T(128)} %pad_add_fusion.ids_ref, bf16[1024,768]{1,0:T(8,128)(2,1)} %get-tuple-element.126.b_ref.left_ref, bf16[1024,3072]{1,0:T(8,128)(2,1)} %get-tuple-element.137.right_ref.gu_ref), custom_call_target="tpu_custom_call" | custom-call | flops 4831838208 | bytes 13000000 | tf_op jit(solution)/shard_map/pallas_call | solution.py:459
  82.1 10.4 %shard_map.321 = (bf16[2,2,4,96,768]{4,3,2,1,0:T(8,128)(2,1)}, bf16[2,2,4,96,768]{4,3,2,1,0:T(8,128)(2,1)}) custom-call(s32[2]{0:T(128)} %pad_add_fusion.ids_ref, bf16[1024,3072]{1,0:T(8,128)(2,1)} %get-tuple-element.133.left_ref.z_ref, bf16[1024,768]{1,0:T(8,128)(2,1)} %get-tuple-element.132.gm_ref.right_ref), custom_call_target="tpu_custom_call" | custom-call | flops 4831838208 | bytes 13000000 | tf_op jit(solution)/shard_map/pallas_call | solution.py:415
  102.8 13.6 %shard_map.323 = (bf16[512,768]{1,0:T(8,128)(2,1)}, bf16[512,768]{1,0:T(8,128)(2,1)}, f32[512,768]{1,0:T(8,128)}, bf16[512,768]{1,0:T(8,128)(2,1)}, f32[1,768]{1,0:T(1,128)}) custom-call(f32[1024,768]{1,0:T(8,128)} %get-tuple-element.136.x1_ref, bf16[1024,3072]{1,0:T(8,128)(2,1)} %get-tuple-element.133.left_ref.z_ref, ...), custom_call_target="tpu_custom_call" | custom-call | flops 10000000000 | bytes 15000000 | tf_op jit(solution)/shard_map/pallas_call | solution.py:497
  118.3 13.7 %shard_map.324 = (bf16[512,768]{1,0:T(8,128)(2,1)}, bf16[512,768]{1,0:T(8,128)(2,1)}, f32[512,768]{1,0:T(8,128)}, bf16[512,768]{1,0:T(8,128)(2,1)}, f32[1,768]{1,0:T(1,128)}) custom-call(f32[1024,768]{1,0:T(8,128)} %get-tuple-element.136.x1_ref, bf16[1024,3072]{1,0:T(8,128)(2,1)} %get-tuple-element.133.left_ref.z_ref, ...), custom_call_target="tpu_custom_call" | custom-call | flops 10000000000 | bytes 15000000 | tf_op jit(solution)/shard_map/pallas_call | solution.py:497
  134.6 8.6 %shard_map.325 = (bf16[80,1024]{1,0:T(8,128)(2,1)}, bf16[80,1024]{1,0:T(8,128)(2,1)}, bf16[80,1024]{1,0:T(8,128)(2,1)}, bf16[80,1024]{1,0:T(8,128)(2,1)}, bf16[2...) custom-call(s32[2]{0:T(128)} %pad_add_fusion.ids_ref, ...), custom_call_target="tpu_custom_call" | custom-call | flops 4000000000 | bytes 10000000 | tf_op jit(solution)/shard_map/pallas_call | solution.py:553
  143.2 15.5 %shard_map.326 = (bf16[512,2304]{1,0:T(8,128)(2,1)}, bf16[512,768]{1,0:T(8,128)(2,1)}, f32[1,768]{1,0:T(1,128)}) custom-call(bf16[1024,2304]{1,0:T(8,128)(2,1)} %get-tuple-element.159.qkv_ref, f32[8,6,256,128]{3,2,1,0:T(8,128)} %get-tuple-element.160.probs_ref, bf16[512,768]{1,0:T(8,128)(2,1)} %get-tuple-element.161.go_ref, ...), custom_call_target="tpu_custom_call" | custom-call | flops 12499999744 | bytes 15000000 | tf_op jit(solution)/shard_map/pallas_call | solution.py:601
  166.0 10.0 %collective-permute-done.11 = bf16[2,2,96,768]{3,2,0,1:T(8,128)(2,1)S(1)} collective-permute-done((bf16[2,2,96,768]{3,2,0,1:T(8,128)(2,1)S(1)}, bf16[2,2,96,768]{3,2,0,1:T(8,128)(2,1)S(1)}, u32[]{:S(2)}, u32[]{:S(2)}) %collective-permute-start.11) | collective-permute-done | bytes 589856 | tf_op jit(solution)/shard_map/ppermute | solution.py:794
  180.8 15.3 %shard_map.327 = (bf16[512,2304]{1,0:T(8,128)(2,1)}, bf16[512,768]{1,0:T(8,128)(2,1)}, f32[1,768]{1,0:T(1,128)}) custom-call(bf16[1024,2304]{1,0:T(8,128)(2,1)} %get-tuple-element.159.qkv_ref, f32[8,6,256,128]{3,2,1,0:T(8,128)} %get-tuple-element.160.probs_ref, bf16[512,768]{1,0:T(8,128)(2,1)} %get-tuple-element.166.go_ref, ...), custom_call_target="tpu_custom_call" | custom-call | flops 12499999744 | bytes 15000000 | tf_op jit(solution)/shard_map/pallas_call | solution.py:601
  196.1 11.6 %shard_map.328 = (bf16[2,2,4,96,768]{4,3,2,1,0:T(8,128)(2,1)}, bf16[2,2,4,96,768]{4,3,2,1,0:T(8,128)(2,1)}, bf16[2,80,768]{2,1,0:T(8,128)(2,1)}, bf16[2,80,768]{2,1,0:T(8,128)(2,1)}) custom-call(s32[2]{0:T(128)} %pad_add_fusion.ids_ref, s32[8,128]{1,0:T(8,128)} %slice_bitcast_fusion.17.keep_ref, bf16[1024,768]{1,0:T(8,128)(2,1)} %get-tuple-element.158.a_ref, ...), custom_call_target="tpu_custom_call" | custom-call | flops 7000000000 | bytes 12000000 | tf_op jit(solution)/shard_map/pallas_call | solution.py:701
  211.3 4.3 %shard_map.329 = (bf16[80,1024]{1,0:T(8,128)(2,1)}, bf16[80,1024]{1,0:T(8,128)(2,1)}, bf16[80,1024]{1,0:T(8,128)(2,1)}, bf16[80,1024]{1,0:T(8,128)(2,1)}) custom-call(s32[8,128]{1,0:T(8,128)} %slice_bitcast_fusion.17.keep_ref, bf16[512,768]{1,0:T(8,128)(2,1)} %get-tuple-element.174.g0a.a_ref, bf16[512,768]{1,0:T(8,128)(2,1)} %get-tuple-element.175.g0b.b_ref, ...), custom_call_target="tpu_custom_call" | custom-call | flops 1000000000 | bytes 3000000 | tf_op jit(solution)/shard_map/pallas_call | solution.py:629
  221.8 2.7 collective-permute-start.28
  230.8 5.8 %collective-permute-done.26 = bf16[208,768]{1,0:T(8,128)(2,1)S(1)} collective-permute-done((bf16[208,768]{1,0:T(8,128)(2,1)S(1)}, bf16[208,768]{1,0:T(8,128)(2,1)S(1)}, u32[]{:S(2)}, u32[]{:S(2)}) %collective-permute-start.26) | collective-permute-done | bytes 319520 | tf_op jit(solution)/shard_map/ppermute | solution.py:794
  239.4 2.8 collective-permute-done.24
  243.0 6.3 %collective-permute-done.30 = bf16[2,2,2,48,768]{4,3,2,1,0:T(8,128)(2,1)S(1)} collective-permute-done((bf16[2,2,2,48,768]{4,3,2,1,0:T(8,128)(2,1)S(1)}, bf16[2,2,2,48,768]{4,3,2,1,0:T(8,128)(2,1)S(1)}, u32[]{:S(2)}, u32[]{:S(2)}) %collective-permute-start.30) | collective-permute-done | bytes 589856 | tf_op jit(solution)/shard_map/ppermute | solution.py:794
  257.1 2.5 collective-permute-done.31
  265.2 9.1 %collective-permute-done.41 = bf16[96,768]{1,0:T(8,128)(2,1)S(1)} collective-permute-done((bf16[96,768]{1,0:T(8,128)(2,1)S(1)}, bf16[96,768]{1,0:T(8,128)(2,1)S(1)}, u32[]{:S(2)}, u32[]{:S(2)}) %collective-permute-start.41) | collective-permute-done | bytes 147488 | tf_op jit(solution)/shard_map/ppermute | solution.py:794
  274.5 4.6 %collective-permute-start.43 = (bf16[112,768]{1,0:T(8,128)(2,1)S(1)}, bf16[112,768]{1,0:T(8,128)(2,1)S(1)}, u32[]{:S(2)}, u32[]{:S(2)}) collective-permute-start(bf16[112,768]{1,0:T(8,128)(2,1)S(1)} %pad_maximum_fusion.5), channel_id=1, source_target_pairs={{0,16},{1,17},{2,18},{3,19},{4,20},{5,21},{6,22},{7,23},{8,24},{9,... | collective-permute-start | bytes 516104 | tf_op jit(solution)/shard_map/ppermute | solution.py:794
  283.7 4.3 %shard_map.331 = (bf16[40,80,128]{2,1,0:T(8,128)(2,1)}, bf16[20,80,512]{2,1,0:T(8,128)(2,1)}) custom-call(s32[1]{0:T(128)} %bitcast.member_ref, s32[4,8,128]{2,1,0:T(8,128)} %get-tuple-element.122.keep_ref, bf16[80,1024]{1,0:T(8,128)(2,1)} %get-tuple-element.201.r0, bf16[80,1024]{1,0:T(8,128)(2,1)} %copy-done.38, bf16[80,1024]{1,0:T(8,128)(2,1)} %copy-done.39, ...), custom_call_target="tpu_custom_call" | custom-call | flops 2000000000 | bytes 4000000 | tf_op jit(solution)/shard_map/pallas_call | solution.py:741
  (265 shorter events, 82.5 us)
Async XLA Ops:
  1.6 14.1 %collective-permute-start.4 = (bf16[160,768]{1,0:T(8,128)(2,1)S(1)}, bf16[160,768]{1,0:T(8,128)(2,1)S(1)}, u32[]{:S(2)}, u32[]{:S(2)}) collective-permute-start(bf16[160,768]{1,0:T(8,128)(2,1)S(1)} %pad_maximum_fusion.2.w0.h0), channel_id=1, source_target_pairs={{0,2},{1,3},{2,0},{3,1},{4,6},{5,7},{6,4},{7,5},{8,10},{9,11},{10,... | collective-permute-start | bytes 737288 | tf_op jit(solution)/shard_map/ppermute | solution.py:794
  4.6 18.1 %collective-permute-start.3 = (bf16[160,768]{1,0:T(8,128)(2,1)S(1)}, bf16[160,768]{1,0:T(8,128)(2,1)S(1)}, u32[]{:S(2)}, u32[]{:S(2)}) collective-permute-start(bf16[160,768]{1,0:T(8,128)(2,1)S(1)} %pad_maximum_fusion.2.w0.h0), channel_id=1, source_target_pairs={{0,1},{1,0},{2,3},{3,2},{4,5},{5,4},{6,7},{7,6},{8,9},{9,8},{10,11... | collective-permute-start | bytes 737288 | tf_op jit(solution)/shard_map/ppermute | solution.py:794
  20.7 23.6 %collective-permute-start.6 = (bf16[80,1024]{1,0:T(8,128)(2,1)S(1)}, bf16[80,1024]{1,0:T(8,128)(2,1)S(1)}, u32[]{:S(2)}, u32[]{:S(2)}) collective-permute-start(bf16[80,1024]{1,0:T(8,128)(2,1)S(1)} %copy-done.45), channel_id=1, source_target_pairs={{0,1},{1,0},{2,3},{3,2},{4,5},{5,4},{6,7},{7,6},{8,9},{9,8},{10,11... | collective-permute-start | bytes 491528 | tf_op jit(solution)/shard_map/ppermute | solution.py:794
  21.0 23.3 %collective-permute-start.7 = (bf16[80,1024]{1,0:T(8,128)(2,1)S(1)}, bf16[80,1024]{1,0:T(8,128)(2,1)S(1)}, u32[]{:S(2)}, u32[]{:S(2)}) collective-permute-start(bf16[80,1024]{1,0:T(8,128)(2,1)S(1)} %copy-done.44), channel_id=1, source_target_pairs={{0,2},{1,3},{2,0},{3,1},{4,6},{5,7},{6,4},{7,5},{8,10},{9,11},{10,... | collective-permute-start | bytes 491528 | tf_op jit(solution)/shard_map/ppermute | solution.py:794
  21.2 23.1 %collective-permute-start.8 = (bf16[80,1024]{1,0:T(8,128)(2,1)S(1)}, bf16[80,1024]{1,0:T(8,128)(2,1)S(1)}, u32[]{:S(2)}, u32[]{:S(2)}) collective-permute-start(bf16[80,1024]{1,0:T(8,128)(2,1)S(1)} %copy-done.43), channel_id=1, source_target_pairs={{0,3},{1,2},{2,1},{3,0},{4,7},{5,6},{6,5},{7,4},{8,11},{9,10},{10,... | collective-permute-start | bytes 491528 | tf_op jit(solution)/shard_map/ppermute | solution.py:794
  99.0 33.0 %collective-permute-start.17 = (bf16[2,2,2,96,768]{4,3,2,1,0:T(8,128)(2,1)}, bf16[2,2,2,96,768]{4,3,2,1,0:T(8,128)(2,1)S(1)}, u32[]{:S(2)}, u32[]{:S(2)}) collective-permute-start(bf16[2,2,2,96,768]{4,3,2,1,0:T(8,128)(2,1)} %fusion.2), channel_id=1, source_target_pairs={{0,4},{1,5},{2,6},{3,7},{4,0},{5,1},{6,2},{7,3},{8,12},{9,13},{10,... | collective-permute-start | bytes 3538952 | tf_op jit(solution)/shard_map/ppermute | solution.py:794
  102.2 32.4 %collective-permute-start.10 = (bf16[2,2,2,96,768]{4,3,1,2,0:T(8,128)(2,1)}, bf16[2,2,2,96,768]{4,3,1,2,0:T(8,128)(2,1)}, u32[]{:S(2)}, u32[]{:S(2)}) collective-permute-start(bf16[2,2,2,96,768]{4,3,1,2,0:T(8,128)(2,1)} %get-tuple-element.229), channel_id=1, source_target_pairs={{0,2},{1,3},{2,0},{3,1},{4,6},{5,7},{6,4},{7,5},{8,10},{9,11},{10,... | collective-permute-start | bytes 3538952 | tf_op jit(solution)/shard_map/ppermute | solution.py:794
  133.1 31.8 %collective-permute-start.18 = (bf16[2,2,96,768]{3,2,1,0:T(8,128)(2,1)}, bf16[2,2,96,768]{3,2,1,0:T(8,128)(2,1)S(1)}, u32[]{:S(2)}, u32[]{:S(2)}) collective-permute-start(bf16[2,2,96,768]{3,2,1,0:T(8,128)(2,1)} %fusion.13), channel_id=1, source_target_pairs={{0,2},{1,3},{2,0},{3,1},{4,6},{5,7},{6,4},{7,5},{8,10},{9,11},{10,... | collective-permute-start | bytes 1769480 | tf_op jit(solution)/shard_map/ppermute | solution.py:794
  161.1 14.9 %collective-permute-start.11 = (bf16[2,2,96,768]{3,2,0,1:T(8,128)(2,1)S(1)}, bf16[2,2,96,768]{3,2,0,1:T(8,128)(2,1)S(1)}, u32[]{:S(2)}, u32[]{:S(2)}) collective-permute-start(bf16[2,2,96,768]{3,2,0,1:T(8,128)(2,1)S(1)} %get-tuple-element.227), channel_id=1, source_target_pairs={{0,4},{1,5},{2,6},{3,7},{4,0},{5,1},{6,2},{7,3},{8,12},{9,13},{10,... | collective-permute-start | bytes 1769480 | tf_op jit(solution)/shard_map/ppermute | solution.py:794
  161.7 16.7 %collective-permute-start.20 = (bf16[80,1024]{1,0:T(8,128)(2,1)S(1)}, bf16[80,1024]{1,0:T(8,128)(2,1)S(1)}, u32[]{:S(2)}, u32[]{:S(2)}) collective-permute-start(bf16[80,1024]{1,0:T(8,128)(2,1)S(1)} %copy-done.42), channel_id=1, source_target_pairs={{0,1},{1,0},{2,3},{3,2},{4,5},{5,4},{6,7},{7,6},{8,9},{9,8},{10,11... | collective-permute-start | bytes 491528 | tf_op jit(solution)/shard_map/ppermute | solution.py:794
  162.3 16.7 %collective-permute-start.14 = (bf16[2,2,2,2,32,768]{5,4,2,3,1,0:T(8,128)(2,1)S(1)}, bf16[2,2,2,2,32,768]{5,4,2,3,1,0:T(8,128)(2,1)S(1)}, u32[]{:S(2)}, u32[]{:S(2)}) collective-permute-start(bf16[2,2,2,2,32,768]{5,4,2,3,1,0:T(8,128)(2,1)S(1)} %copy.60), channel_id=1, source_target_pairs={{0,1},{1,0},{2,3},{3,2},{4,5},{5,4},{6,7},{7,6},{8,9},{9,8},{10,11... | collective-permute-start | bytes 2359304 | tf_op jit(solution)/shard_map/ppermute | solution.py:794
  163.7 15.3 %collective-permute-start.21 = (bf16[80,1024]{1,0:T(8,128)(2,1)S(1)}, bf16[80,1024]{1,0:T(8,128)(2,1)S(1)}, u32[]{:S(2)}, u32[]{:S(2)}) collective-permute-start(bf16[80,1024]{1,0:T(8,128)(2,1)S(1)} %copy-done.41), channel_id=1, source_target_pairs={{0,2},{1,3},{2,0},{3,1},{4,6},{5,7},{6,4},{7,5},{8,10},{9,11},{10,... | collective-permute-start | bytes 491528 | tf_op jit(solution)/shard_map/ppermute | solution.py:794
  164.9 14.1 %collective-permute-start.22 = (bf16[80,1024]{1,0:T(8,128)(2,1)S(1)}, bf16[80,1024]{1,0:T(8,128)(2,1)S(1)}, u32[]{:S(2)}, u32[]{:S(2)}) collective-permute-start(bf16[80,1024]{1,0:T(8,128)(2,1)S(1)} %copy-done.40), channel_id=1, source_target_pairs={{0,3},{1,2},{2,1},{3,0},{4,7},{5,6},{6,5},{7,4},{8,11},{9,10},{10,... | collective-permute-start | bytes 491528 | tf_op jit(solution)/shard_map/ppermute | solution.py:794
  176.0 20.0 %collective-permute-start.19 = (bf16[2,96,768]{2,1,0:T(8,128)(2,1)S(1)}, bf16[2,96,768]{2,1,0:T(8,128)(2,1)S(1)}, u32[]{:S(2)}, u32[]{:S(2)}) collective-permute-start(bf16[2,96,768]{2,1,0:T(8,128)(2,1)S(1)} %fusion.18), channel_id=1, source_target_pairs={{0,8},{1,9},{2,10},{3,11},{4,12},{5,13},{6,14},{7,15},{8,0},{9,1},... | collective-permute-start | bytes 884744 | tf_op jit(solution)/shard_map/ppermute | solution.py:794
  178.4 17.6 %collective-permute-start.12 = (bf16[2,96,768]{2,1,0:T(8,128)(2,1)S(1)}, bf16[2,96,768]{2,1,0:T(8,128)(2,1)S(1)}, u32[]{:S(2)}, u32[]{:S(2)}) collective-permute-start(bf16[2,96,768]{2,1,0:T(8,128)(2,1)S(1)} %get-tuple-element.237), channel_id=1, source_target_pairs={{0,8},{1,9},{2,10},{3,11},{4,12},{5,13},{6,14},{7,15},{8,0},{9,1},... | collective-permute-start | bytes 884744 | tf_op jit(solution)/shard_map/ppermute | solution.py:794
  180.2 15.9 %collective-permute-start.16 = (bf16[336,768]{1,0:T(8,128)(2,1)S(1)}, bf16[336,768]{1,0:T(8,128)(2,1)S(1)}, u32[]{:S(2)}, u32[]{:S(2)}) collective-permute-start(bf16[336,768]{1,0:T(8,128)(2,1)S(1)} %pad_maximum_fusion), channel_id=1, source_target_pairs={{0,2},{1,3},{2,0},{3,1},{4,6},{5,7},{6,4},{7,5},{8,10},{9,11},{10,... | collective-permute-start | bytes 1548296 | tf_op jit(solution)/shard_map/ppermute | solution.py:794
  219.1 17.6 %collective-permute-start.32 = (bf16[2,80,768]{2,1,0:T(8,128)(2,1)S(1)}, bf16[2,80,768]{2,1,0:T(8,128)(2,1)S(1)}, u32[]{:S(2)}, u32[]{:S(2)}) collective-permute-start(bf16[2,80,768]{2,1,0:T(8,128)(2,1)S(1)} %add_convert_fusion.18), channel_id=1, source_target_pairs={{0,8},{1,9},{2,10},{3,11},{4,12},{5,13},{6,14},{7,15},{8,0},{9,1},... | collective-permute-start | bytes 737288 | tf_op jit(solution)/shard_map/ppermute | solution.py:794
  227.5 14.8 %collective-permute-start.24 = (bf16[2,2,2,48,768]{4,3,2,1,0:T(8,128)(2,1)S(1)}, bf16[2,2,2,48,768]{4,3,2,1,0:T(8,128)(2,1)S(1)}, u32[]{:S(2)}, u32[]{:S(2)}) collective-permute-start(bf16[2,2,2,48,768]{4,3,2,1,0:T(8,128)(2,1)S(1)} %get-tuple-element.224), channel_id=1, source_target_pairs={{0,2},{1,3},{2,0},{3,1},{4,6},{5,7},{6,4},{7,5},{8,10},{9,11},{10,... | collective-permute-start | bytes 1769480 | tf_op jit(solution)/shard_map/ppermute | solution.py:794
  230.3 19.0 %collective-permute-start.30 = (bf16[2,2,2,48,768]{4,3,2,1,0:T(8,128)(2,1)S(1)}, bf16[2,2,2,48,768]{4,3,2,1,0:T(8,128)(2,1)S(1)}, u32[]{:S(2)}, u32[]{:S(2)}) collective-permute-start(bf16[2,2,2,48,768]{4,3,2,1,0:T(8,128)(2,1)S(1)} %fusion.12), channel_id=1, source_target_pairs={{0,4},{1,5},{2,6},{3,7},{4,0},{5,1},{6,2},{7,3},{8,12},{9,13},{10,... | collective-permute-start | bytes 1769480 | tf_op jit(solution)/shard_map/ppermute | solution.py:794
  237.9 17.6 %collective-permute-start.33 = (bf16[2,80,768]{2,1,0:T(8,128)(2,1)S(1)}, bf16[2,80,768]{2,1,0:T(8,128)(2,1)S(1)}, u32[]{:S(2)}, u32[]{:S(2)}) collective-permute-start(bf16[2,80,768]{2,1,0:T(8,128)(2,1)S(1)} %add_convert_fusion.17), channel_id=1, source_target_pairs={{0,16},{1,17},{2,18},{3,19},{4,20},{5,21},{6,22},{7,23},{8,24},{9,... | collective-permute-start | bytes 737288 | tf_op jit(solution)/shard_map/ppermute | solution.py:794
  242.4 14.6 %collective-permute-start.29 = (bf16[2,2,48,768]{3,2,1,0:T(8,128)(2,1)S(1)}, bf16[2,2,48,768]{3,2,1,0:T(8,128)(2,1)S(1)}, u32[]{:S(2)}, u32[]{:S(2)}) collective-permute-start(bf16[2,2,48,768]{3,2,1,0:T(8,128)(2,1)S(1)} %get-tuple-element.233), channel_id=1, source_target_pairs={{0,4},{1,5},{2,6},{3,7},{4,0},{5,1},{6,2},{7,3},{8,12},{9,13},{10,... | collective-permute-start | bytes 884744 | tf_op jit(solution)/shard_map/ppermute | solution.py:794
  259.5 22.8 %collective-permute-start.34 = (bf16[80,1024]{1,0:T(8,128)(2,1)S(1)}, bf16[80,1024]{1,0:T(8,128)(2,1)S(1)}, u32[]{:S(2)}, u32[]{:S(2)}) collective-permute-start(bf16[80,1024]{1,0:T(8,128)(2,1)S(1)} %copy-done.37), channel_id=1, source_target_pairs={{0,1},{1,0},{2,3},{3,2},{4,5},{5,4},{6,7},{7,6},{8,9},{9,8},{10,11... | collective-permute-start | bytes 491528 | tf_op jit(solution)/shard_map/ppermute | solution.py:794
  259.5 22.8 %collective-permute-start.35 = (bf16[80,1024]{1,0:T(8,128)(2,1)S(1)}, bf16[80,1024]{1,0:T(8,128)(2,1)S(1)}, u32[]{:S(2)}, u32[]{:S(2)}) collective-permute-start(bf16[80,1024]{1,0:T(8,128)(2,1)S(1)} %copy-done.36), channel_id=1, source_target_pairs={{0,2},{1,3},{2,0},{3,1},{4,6},{5,7},{6,4},{7,5},{8,10},{9,11},{10,... | collective-permute-start | bytes 491528 | tf_op jit(solution)/shard_map/ppermute | solution.py:794
  264.2 14.8 %collective-permute-start.40 = (bf16[96,768]{1,0:T(8,128)(2,1)S(1)}, bf16[96,768]{1,0:T(8,128)(2,1)S(1)}, u32[]{:S(2)}, u32[]{:S(2)}) collective-permute-start(bf16[96,768]{1,0:T(8,128)(2,1)S(1)} %pad_maximum_fusion.6), channel_id=1, source_target_pairs={{0,8},{1,9},{2,10},{3,11},{4,12},{5,13},{6,14},{7,15},{8,0},{9,1},... | collective-permute-start | bytes 442376 | tf_op jit(solution)/shard_map/ppermute | solution.py:794
  (73 other events, 417.2 us)
